TPU v7x, 32 devices: a whole 2x2x4 slice. The times are simulated.
32 devices in a mesh: groups: 2 (over x), seq: 8 (over z, y), dp: 2 (over core).
Axes of the slice: x: 2, y: 2, z: 4, core: 2. Of those that a mesh axis runs over, the one named last changes fastest.
Arguments:
- tokens: bfloat16 [4, 4096, 1024], P(('groups', 'dp'), 'seq'), parts along dimension 0, may hold values from -12 to 12
- qk_weight: bfloat16 [1024, 1024], replicated, may hold values from -0.1875 to 0.1875
- value_weight: bfloat16 [1024, 1024], replicated, may hold values from -0.1875 to 0.1875
- out_weight: bfloat16 [1024, 1024], replicated, may hold values from -0.1875 to 0.1875
- neighbour_list: int32 [4, 32, 4], P(('groups', 'dp'), 'seq'), parts along dimension 0, may hold values from 0 to 31, as said below
- neighbour_count: int32 [4, 32], P(('groups', 'dp'), 'seq'), parts along dimension 0, may hold values from 1 to 4, as said below
Outputs:
- update: bfloat16 [4, 4096, 1024], P(('groups', 'dp'), 'seq'), parts along dimension 0
There are 2 independent parts, one for each index of `groups`. A program takes and returns all parts, laid end to end along the dimension named above; an argument that names none is the same for every part. Nothing has to cross between parts.
Inputs may be any that keep to these rules, and one draw needn't show every extreme that they name: `neighbour_list`: slot 0 of block b's list is b itself; the other slots name distinct blocks within 4 blocks of b on either side; slots at or beyond the count also name such blocks but are not attended. `neighbour_count`: every query block whose index is a multiple of 7 has count 4.
All inputs are finite; a program needn't handle non-finite values.
Results may differ from a plain program's by a relative error of at most 0.0066.
Values may be sent and summed in bfloat16 or wider, within the bound.
No kernel may reach another device: no remote copies, remote signals or barrier semaphores. Data moves between devices by JAX's collectives and lax.ppermute only.
A program may use at most 192 MiB of HBM per device.

v0:
```python
import functools

import jax
import jax.numpy as jnp
from jax import lax
from jax.experimental import pallas as pl
from jax.experimental.pallas import tpu as pltpu
from jax.sharding import PartitionSpec as P

H = 16
DH = 64
HL = 8
DL = 128
F32 = jnp.float32
BF16 = jnp.bfloat16
NT = (((1,), (1,)), ((), ()))
VMEM = pl.BlockSpec(memory_space=pltpu.VMEM)
SMEM = pl.BlockSpec(memory_space=pltpu.SMEM)
MIB = 1 << 20


def dot_nt(a, b):
    return lax.dot_general(a, b, NT, preferred_element_type=F32)


def dot_nn(a, b):
    return jnp.dot(a, b, preferred_element_type=F32)


def tile(i, size):
    return pl.ds(pl.multiple_of(i * size, size), size)


def project(x, wk_ref, wvt_ref, k_ref, vt_ref):
    k_ref[...] = dot_nn(x, wk_ref[...]).astype(BF16)
    vt_ref[...] = dot_nt(wvt_ref[...], x).astype(BF16)


def own_kernel(x_ref, wk_ref, wvt_ref, k_ref, f_ref, vt_ref, s_ref):
    project(x_ref[...], wk_ref, wvt_ref, k_ref, vt_ref)
    for h in range(HL):
        part = slice(h * DL, (h + 1) * DL)
        k = k_ref[:, part].astype(F32)
        f = (k / (1.0 + jnp.exp(-k))).astype(BF16)
        f_ref[:, part] = f
        s_ref[part, :] = dot_nn(vt_ref[part, :], f).astype(BF16)


def within_kernel(f_ref, vt_ref, n_ref):
    rows = f_ref.shape[0]
    half = rows // 2
    upper = lax.broadcasted_iota(jnp.int32, (half, half), 0) <= lax.broadcasted_iota(
        jnp.int32, (half, half), 1
    )

    def head(h, carry):
        cols = tile(h, DL)
        f0 = f_ref[:half, cols]
        f1 = f_ref[half:, cols]
        v0 = vt_ref[cols, :half]
        v1 = vt_ref[cols, half:]
        a00 = jnp.where(upper, dot_nt(f0, f0), 0.0).astype(BF16)
        a01 = dot_nt(f0, f1).astype(BF16)
        a11 = jnp.where(upper, dot_nt(f1, f1), 0.0).astype(BF16)
        n_ref[cols, :half] = dot_nn(v0, a00)
        n_ref[cols, half:] = dot_nn(v0, a01) + dot_nn(v1, a11)
        return carry

    lax.fori_loop(0, HL, head, 0, unroll=2)


def linear_kernel(stages, pos_ref, f_ref, n_ref, *refs):
    heard = refs[:stages]
    o_ref = refs[stages]
    bits = [((pos_ref[0] >> k) & 1).astype(F32) for k in range(stages)]

    def head(h, carry):
        cols = tile(h, DL)
        before = sum(ref[cols, :].astype(F32) * bit for ref, bit in zip(heard, bits)).astype(BF16)
        n = n_ref[cols, :] + dot_nt(before, f_ref[:, cols])
        mean = jnp.sum(n * n, axis=0, keepdims=True) * (1.0 / DL)
        o_ref[cols, :] = n * lax.rsqrt(mean + 1e-06)
        return carry

    lax.fori_loop(0, HL, head, 0, unroll=2)


def listed(list_ref, count_ref, qb, block):
    found = False
    for j in range(list_ref.shape[1]):
        found = jnp.logical_or(
            found, jnp.logical_and(j < count_ref[qb], list_ref[qb, j] == block)
        )
    return found


def attend(first, size, qb, kbs, q_ref, k_ref, vt_ref, m_ref, l_ref, acc_ref):
    qrows = tile(qb, size)
    krows = [tile(kb, size) for kb in kbs]
    lane = lax.broadcasted_iota(jnp.int32, (size, 2 * DH), 1)
    pairs = H // 2
    cols = [slice(p * 2 * DH, (p + 1) * 2 * DH) for p in range(pairs)]
    if first:
        shape = (size * len(kbs), 2 * size)
        key = lax.broadcasted_iota(jnp.int32, shape, 0)
        query = lax.broadcasted_iota(jnp.int32, shape, 1) % size
        other = key != query
    else:
        tops = m_ref[qb]
        totals = l_ref[qb]
    scores = []
    for p in range(pairs):
        q = q_ref[qrows, cols[p]] * jnp.asarray(DH ** (-0.5), BF16)
        zero = jnp.zeros_like(q)
        pair = jnp.concatenate([jnp.where(lane < DH, q, zero), jnp.where(lane < DH, zero, q)], axis=0)
        k = jnp.concatenate([k_ref[r, cols[p]] for r in krows], axis=0)
        s = dot_nt(k, pair)
        scores.append(jnp.where(other, s, -1e30) if first else s)
    raised = []
    new_tops = []
    new_totals = []
    for p in range(pairs):
        top = jnp.max(scores[p], axis=0, keepdims=True)
        if not first:
            top = jnp.maximum(top, tops[p : p + 1])
        e = jnp.exp(scores[p] - top)
        new_tops.append(top)
        new_totals.append(jnp.sum(e, axis=0, keepdims=True))
        raised.append(e.astype(BF16))
    for p in range(pairs):
        v = jnp.concatenate([vt_ref[cols[p], r] for r in krows], axis=1)
        o = dot_nn(v, raised[p])
        o = jnp.concatenate([o[:DH, :size], o[DH:, size:]], axis=0)
        if not first:
            fade = jnp.exp(tops[p : p + 1] - new_tops[p])
            new_totals[p] = new_totals[p] + totals[p : p + 1] * fade
            o = o + acc_ref[qb, cols[p], :] * by_head(fade, size)
        acc_ref[qb, cols[p], :] = o
    m_ref[qb] = jnp.concatenate(new_tops, axis=0)
    l_ref[qb] = jnp.concatenate(new_totals, axis=0)


def by_head(row, size):
    return jnp.concatenate(
        [jnp.broadcast_to(row[:, :size], (DH, size)), jnp.broadcast_to(row[:, size:], (DH, size))], axis=0
    )


def attend_listed(own, size, blocks, list_ref, count_ref, found_ref, *rest):
    def query(qb, carry):
        found_ref[0] = qb
        n = jnp.int32(1 if own else 0)
        for kb, block in enumerate(blocks):
            wanted = listed(list_ref, count_ref, qb, block)
            if own:
                wanted = jnp.logical_and(wanted, qb != kb)

            @pl.when(wanted)
            def _(n=n, kb=kb):
                found_ref[n] = kb

            n = n + wanted.astype(jnp.int32)
        start = 0
        if own:

            @pl.when(n == 1)
            def _():
                attend(True, size, qb, [qb], *rest)

            @pl.when(n > 1)
            def _():
                attend(True, size, qb, [qb, found_ref[1]], *rest)

            start = 2
        if len(blocks) - start > 1:

            def two(i, carry):
                attend(False, size, qb, [found_ref[start + 2 * i], found_ref[start + 2 * i + 1]], *rest)
                return carry

            lax.fori_loop(0, jnp.maximum(n - start, 0) // 2, two, 0)

        @pl.when(jnp.logical_and(n > start, n % 2 == 1))
        def _():
            attend(False, size, qb, [found_ref[n - 1]], *rest)

        return carry

    lax.fori_loop(0, list_ref.shape[0], query, 0)


def own_attention_kernel(size, list_ref, count_ref, pos_ref, k_ref, vt_ref, m_ref, l_ref, acc_ref, found_ref):
    queries = list_ref.shape[0]
    blocks = [pos_ref[0] * queries + kb for kb in range(queries)]
    attend_listed(
        True, size, blocks, list_ref, count_ref, found_ref, k_ref, k_ref, vt_ref, m_ref, l_ref, acc_ref
    )


def attend_halo(size, pieces, list_ref, count_ref, pos_ref, piece_refs, wk_ref, wvt_ref, q_ref, state, scratch):
    found_ref, x_ref, k_ref, vt_ref = scratch
    queries = list_ref.shape[0]
    pos = pos_ref[0]
    step = 1 - 2 * (pos % 2)
    row = 0
    blocks = []
    for (near, first), ref in zip(pieces, piece_refs):
        rows = ref.shape[0]
        x_ref[row : row + rows, :] = ref[...]
        row += rows
        run = pos + step if near else pos - step
        blocks += [run * queries + first + i for i in range(rows // size)]
    project(x_ref[...], wk_ref, wvt_ref, k_ref, vt_ref)
    attend_listed(
        False, size, blocks, list_ref, count_ref, found_ref, q_ref, k_ref, vt_ref, *state
    )


def halo_kernel(size, pieces, list_ref, count_ref, pos_ref, *refs):
    n = len(pieces)
    wk_ref, wvt_ref, q_ref = refs[n : n + 3]
    attend_halo(
        size, pieces, list_ref, count_ref, pos_ref, refs[:n], wk_ref, wvt_ref, q_ref, refs[n + 6 : n + 9], refs[n + 9 :]
    )


def final_kernel(size, pieces, list_ref, count_ref, pos_ref, *refs):
    n = len(pieces)
    wk_ref, wvt_ref, q_ref, lin_ref, wo_ref = refs[n : n + 5]
    out_ref, m_ref, l_ref, acc_ref, comb_ref = refs[n + 8 : n + 13]
    attend_halo(
        size,
        pieces,
        list_ref,
        count_ref,
        pos_ref,
        refs[:n],
        wk_ref,
        wvt_ref,
        q_ref,
        (m_ref, l_ref, acc_ref),
        refs[n + 13 :],
    )

    def finish(qb, carry):
        rows = tile(qb, size)
        share = 1.0 / l_ref[qb]
        for p in range(H // 2):
            cols = slice(p * 2 * DH, (p + 1) * 2 * DH)
            both = acc_ref[qb, cols, :] * by_head(share[p : p + 1], size) + lin_ref[cols, rows]
            comb_ref[rows, cols] = both.T.astype(BF16)
        return carry

    lax.fori_loop(0, list_ref.shape[0], finish, 0)
    out_ref[...] = dot_nn(comb_ref[...], wo_ref[...]).astype(BF16)


def call(kernel, name, ins, outs, smem=0, scratch=(), aliases=None, limit=20 * MIB):
    return pl.pallas_call(
        kernel,
        name=name,
        in_specs=[SMEM] * smem + [VMEM] * (len(ins) - smem),
        out_specs=[VMEM] * len(outs),
        out_shape=[jax.ShapeDtypeStruct(s, d) for s, d in outs],
        scratch_shapes=list(scratch),
        input_output_aliases=aliases or {},
        cost_estimate=pl.CostEstimate(flops=1000, bytes_accessed=1000, transcendentals=0),
        compiler_params=pltpu.CompilerParams(vmem_limit_bytes=limit),
    )(*ins)


def after(value, *done):
    return lax.optimization_barrier((value,) + done)[0]


def on_device(tokens, qk_weight, value_weight, out_weight, neighbour_list, neighbour_count):
    rows = tokens.shape[1]
    width = tokens.shape[2]
    blocks = neighbour_list.shape[1]
    size = rows // blocks
    half = blocks // 2
    count = lax.axis_size("seq")
    position = lax.axis_index("seq").astype(jnp.int32).reshape(1)
    own = tokens[0]
    tables = (neighbour_list[0], neighbour_count[0], position)

    def swap(value, bit):
        return lax.ppermute(value, "seq", [(i, i ^ bit) for i in range(count)])

    def onward(value):
        pairs = [(i, i + 2) for i in range(0, count - 2, 2)] + [(i, i - 2) for i in range(3, count, 2)]
        return lax.ppermute(value, "seq", pairs)

    def across(value):
        odd = range(1, count - 1, 2)
        return lax.ppermute(value, "seq", [(i, i + 1) for i in odd] + [(i + 1, i) for i in odd])

    def flat(total):
        return (
            pltpu.SMEM((total // size + 2,), jnp.int32),
            pltpu.VMEM((total, width), BF16),
            pltpu.VMEM((total, width), BF16),
            pltpu.VMEM((width, total), BF16),
        )

    def join_halo(softmax, pieces, arrays):
        ins = tables + tuple(arrays) + (qk_weight, value_t, keyed) + tuple(softmax)
        first = len(ins) - 3
        return call(
            functools.partial(halo_kernel, size, pieces),
            "halo",
            ins,
            shapes,
            smem=3,
            scratch=flat(sum(a.shape[0] for a in arrays)),
            aliases={first + i: i for i in range(3)},
        )

    cuts = [0, half * size, (half + 1) * size, rows]
    near_a = swap(own[: cuts[1]], 1)
    value_t = value_weight.T
    keyed, features, values_t, state = call(
        own_kernel,
        "own",
        (own, qk_weight, value_t),
        [((rows, width), BF16), ((rows, width), BF16), ((width, rows), BF16), ((width, DL), BF16)],
    )
    heard = [swap(state, 1)]
    rest = after(own, state)
    near_b = swap(rest[cuts[1] : cuts[2]], 1)
    near_c = swap(rest[cuts[2] :], 1)
    far_c = across(rest[cuts[2] :])
    shapes = [((blocks, H // 2, 2 * size), F32)] * 2 + [((blocks, width, size), F32)]
    softmax = call(
        functools.partial(own_attention_kernel, size),
        "own_attention",
        tables + (keyed, values_t),
        shapes,
        smem=3,
        scratch=(pltpu.SMEM((blocks + 1,), jnp.int32),),
    )
    far_a = onward(after(near_a, softmax[0]))
    total = state + after(heard[0], softmax[0])
    heard.append(swap(total, 2))
    (within,) = call(
        within_kernel,
        "within",
        (after(features, near_a, total), values_t),
        [((width, rows), F32)],
    )
    softmax = join_halo(softmax, [(True, 0)], [after(near_a, within)])
    far_b = onward(after(near_b, softmax[0]))
    stride = 4
    while stride < count:
        total = total + after(heard[-1], softmax[0])
        heard.append(swap(total, stride))
        stride *= 2
    softmax = join_halo(
        softmax, [(True, half), (False, 0)], [after(near_b, total), far_a]
    )
    (linear,) = call(
        functools.partial(linear_kernel, len(heard)),
        "linear",
        (position, after(features, softmax[0]), within) + tuple(heard),
        [((width, rows), F32)],
        smem=1,
    )
    softmax = join_halo(softmax, [(False, half)], [after(far_b, linear)])
    pieces = [(True, half + 1), (False, half + 1)]
    arrays = (near_c, far_c)
    ins = tables + arrays + (qk_weight, value_t, keyed, linear, out_weight) + tuple(softmax)
    first = len(ins) - 3
    update, *_ = call(
        functools.partial(final_kernel, size, pieces),
        "final",
        ins,
        [((rows, width), BF16)] + shapes,
        smem=3,
        scratch=(pltpu.VMEM((rows, width), BF16),) + flat(sum(a.shape[0] for a in arrays)),
        aliases={first + i: i + 1 for i in range(3)},
    )
    return update[None]


def solution(mesh):
    placed = (
        P(("groups", "dp"), "seq", None),
        P(),
        P(),
        P(),
        P(("groups", "dp"), "seq", None),
        P(("groups", "dp"), "seq"),
    )
    return jax.shard_map(
        on_device,
        mesh=mesh,
        in_specs=placed,
        out_specs=P(("groups", "dp"), "seq", None),
        check_vma=False,
    )
```

profile of v0, /device:TPU:16, one launch (start us, length us, event | category | flops | bytes accessed | tf_op | source)
XLA Modules:
  0.0 63.5 jit_solution(13829071560213964784)
XLA Ops:
  0.0 1.9 %slice_bitcast_fusion = bf16[256,1024]{1,0:T(8,128)(2,1)} fusion(bf16[1,512,1024]{2,1,0:T(8,128)(2,1)} %param.6), kind=kLoop, calls=%fused_computation | loop fusion | bytes 1048576 | tf_op jit(solution)/shard_map/slice | solution.py:320
  1.9 1.5 %collective-permute-start.5 = (bf16[256,1024]{1,0:T(8,128)(2,1)}, bf16[256,1024]{1,0:T(8,128)(2,1)}, u32[]{:S(2)}, u32[]{:S(2)}) collective-permute-start(bf16[256,1024]{1,0:T(8,128)(2,1)} %slice_bitcast_fusion), channel_id=1, source_target_pairs={{0,2},{2,0},{4,6},{6,4},{8,10},{10,8},{12,14},{14,12},{1,3},{3,1},... | collective-permute-start | bytes 1572872 | tf_op jit(solution)/shard_map/ppermute | solution.py:288
  3.4 2.9 %copy.19 = bf16[1024,1024]{0,1:T(8,128)(2,1)S(1)} copy(bf16[1024,1024]{1,0:T(8,128)(2,1)} %param.8) | data formatting | bytes 4194304 | tf_op args[2]
  6.3 0.0 copy-start
  6.3 1.6 %copy-done = bf16[1024,1024]{1,0:T(8,128)(2,1)S(1)} copy-done((bf16[1024,1024]{1,0:T(8,128)(2,1)S(1)}, bf16[1024,1024]{1,0:T(8,128)(2,1)}, u32[]{:S(2)}) %copy-start) | copy-done | bytes 2097176
  7.9 1.2 %copy-done.2 = bf16[1,512,1024]{2,1,0:T(8,128)(2,1)S(1)} copy-done((bf16[1,512,1024]{2,1,0:T(8,128)(2,1)S(1)}, bf16[1,512,1024]{2,1,0:T(8,128)(2,1)}, u32[]{:S(2)}) %copy-start.2) | copy-done | bytes 1048600
  9.1 3.4 %own.1 = (bf16[512,1024]{1,0:T(8,128)(2,1)S(1)}, bf16[512,1024]{1,0:T(8,128)(2,1)S(1)}, bf16[1024,512]{1,0:T(8,128)(2,1)S(1)}, bf16[1024,128]{1,0:T(8,128)(2,1)}) custom-call(bf16[512,1024]{1,0:T(8,128)(2,1)S(1)} %bitcast.13, bf16[1024,1024]{1,0:T(8,128)(2,1)S(1)} %copy-done, bf16[1024,1024]{1,0:T(8,128)(2,1)S(1)} %bitcast.8), custom_call_target="tpu_custom_call" | custom-call | flops 1000 | bytes 1000 | tf_op jit(solution)/shard_map/own/pallas_call | solution.py:259
  12.5 1.0 %copy-done.4 = bf16[1024,512]{1,0:T(8,128)(2,1)} copy-done((bf16[1024,512]{1,0:T(8,128)(2,1)}, bf16[1024,512]{1,0:T(8,128)(2,1)S(1)}, u32[]{:S(2)}) %copy-start.4) | copy-done | bytes 1048600
  13.5 1.0 %copy-done.6 = bf16[512,1024]{1,0:T(8,128)(2,1)} copy-done((bf16[512,1024]{1,0:T(8,128)(2,1)}, bf16[512,1024]{1,0:T(8,128)(2,1)S(1)}, u32[]{:S(2)}) %copy-start.6) | copy-done | bytes 1048600
  14.5 0.5 collective-permute-start.3
  15.0 1.3 %copy-done.5 = bf16[1024,512]{1,0:T(8,128)(2,1)S(1)} copy-done((bf16[1024,512]{1,0:T(8,128)(2,1)S(1)}, bf16[1024,512]{1,0:T(8,128)(2,1)}, u32[]{:S(2)}) %copy-start.5) | copy-done | bytes 1048600
  16.3 5.0 %own_attention.1 = (f32[4,8,256]{2,1,0:T(8,128)S(1)}, f32[4,8,256]{2,1,0:T(8,128)S(1)}, f32[4,1024,128]{2,1,0:T(8,128)S(1)}) custom-call(s32[4,4]{1,0:T(4,128)S(1)} %bitcast.15, s32[4]{0:T(128)S(1)} %bitcast.20, s32[1]{0:T(128)} %bitcast.2.pos_ref, bf16[512,1024]{1,0:T(8,128)(2,1)S(1)} %get-tuple-element.34.k_ref.refs_3_.refs_4_, bf16[1024,512]{1,0:T(8,128)(2,1)S(1)} %copy-done.5), custom_call_target="tpu_custom_call" | custom-call | flops 1000 | bytes 1000 | tf_op jit(solution)/shard_map/own_attention/pallas_call | solution.py:259
  21.3 1.2 %collective-permute-done.3.refs_0_ = bf16[1024,128]{1,0:T(8,128)(2,1)S(1)} collective-permute-done((bf16[1024,128]{1,0:T(8,128)(2,1)}, bf16[1024,128]{1,0:T(8,128)(2,1)S(1)}, u32[]{:S(2)}, u32[]{:S(2)}) %collective-permute-start.3) | collective-permute-done | bytes 262176 | tf_op jit(solution)/shard_map/ppermute | solution.py:288
  22.5 1.0 %add.6 = bf16[1024,128]{1,0:T(8,128)(2,1)S(1)} add(bf16[1024,128]{1,0:T(8,128)(2,1)} %get-tuple-element.32, bf16[1024,128]{1,0:T(8,128)(2,1)S(1)} %collective-permute-done.3.refs_0_) | non-fusion elementwise | flops 131072 | bytes 786432 | tf_op jit(solution)/shard_map/add | solution.py:343
  23.5 1.6 %collective-permute-start.4 = (bf16[1024,128]{1,0:T(8,128)(2,1)S(1)}, bf16[1024,128]{1,0:T(8,128)(2,1)S(1)}, u32[]{:S(2)}, u32[]{:S(2)}) collective-permute-start(bf16[1024,128]{1,0:T(8,128)(2,1)S(1)} %add.6), channel_id=1, source_target_pairs={{0,4},{2,6},{4,0},{6,2},{8,12},{10,14},{12,8},{14,10},{1,5},{3,7},... | collective-permute-start | bytes 786440 | tf_op jit(solution)/shard_map/ppermute | solution.py:288
  25.1 0.0 collective-permute-done.5.refs_0_
  25.1 2.3 %collective-permute-start.6 = (bf16[256,1024]{1,0:T(8,128)(2,1)}, bf16[256,1024]{1,0:T(8,128)(2,1)S(1)}, u32[]{:S(2)}, u32[]{:S(2)}) collective-permute-start(bf16[256,1024]{1,0:T(8,128)(2,1)} %collective-permute-done.5.refs_0_), channel_id=1, source_target_pairs={{0,4},{4,8},{8,12},{6,2},{10,6},{14,10},{1,5},{5,9},{9,13},{7,3},{... | collective-permute-start | bytes 1572872 | tf_op jit(solution)/shard_map/ppermute | solution.py:292
  27.6 0.1 collective-permute-start.2
  27.7 2.7 %within.1.n_ref = f32[1024,512]{1,0:T(8,128)S(1)} custom-call(bf16[512,1024]{1,0:T(8,128)(2,1)S(1)} %copy-done.7, bf16[1024,512]{1,0:T(8,128)(2,1)S(1)} %copy-done.5), custom_call_target="tpu_custom_call" | custom-call | flops 1000 | bytes 1000 | tf_op jit(solution)/shard_map/within/pallas_call | solution.py:259
  30.4 3.2 %halo.3 = (f32[4,8,256]{2,1,0:T(8,128)S(1)}, f32[4,8,256]{2,1,0:T(8,128)S(1)}, f32[4,1024,128]{2,1,0:T(8,128)S(1)}) custom-call(s32[4,4]{1,0:T(4,128)S(1)} %bitcast.16, s32[4]{0:T(128)S(1)} %bitcast.21, s32[1]{0:T(128)} %bitcast.2.pos_ref, ...), custom_call_target="tpu_custom_call", output_to_operand_aliasing={{0}: (7, {}), {1}: (8, {}), {2}: (9, {})} | custom-call | flops 1000 | bytes 1000 | tf_op jit(solution)/shard_map/halo/pallas_call | solution.py:259
  33.6 0.1 add.7
  33.7 2.9 %collective-permute-start.7 = (bf16[1024,128]{1,0:T(8,128)(2,1)S(1)}, bf16[1024,128]{1,0:T(8,128)(2,1)S(1)}, u32[]{:S(2)}, u32[]{:S(2)}) collective-permute-start(bf16[1024,128]{1,0:T(8,128)(2,1)S(1)} %add.7), channel_id=1, source_target_pairs={{0,8},{2,10},{4,12},{6,14},{8,0},{10,2},{12,4},{14,6},{1,9},{3,11}... | collective-permute-start | bytes 786440 | tf_op jit(solution)/shard_map/ppermute | solution.py:288
  36.6 2.7 %collective-permute-start.8 = (bf16[128,1024]{1,0:T(8,128)(2,1)S(1)}, bf16[128,1024]{1,0:T(8,128)(2,1)S(1)}, u32[]{:S(2)}, u32[]{:S(2)}) collective-permute-start(bf16[128,1024]{1,0:T(8,128)(2,1)S(1)} %collective-permute-done.2.refs_0_), channel_id=1, source_target_pairs={{0,4},{4,8},{8,12},{6,2},{10,6},{14,10},{1,5},{5,9},{9,13},{7,3},{... | collective-permute-start | bytes 786440 | tf_op jit(solution)/shard_map/ppermute | solution.py:292
  39.3 0.1 collective-permute-start
  39.4 4.7 %collective-permute-start.1 = (bf16[128,1024]{1,0:T(8,128)(2,1)S(1)}, bf16[128,1024]{1,0:T(8,128)(2,1)S(1)}, u32[]{:S(2)}, u32[]{:S(2)}) collective-permute-start(bf16[128,1024]{1,0:T(8,128)(2,1)S(1)} %get-tuple-element.60), channel_id=1, source_target_pairs={{2,4},{6,8},{10,12},{4,2},{8,6},{12,10},{3,5},{7,9},{11,13},{5,3},... | collective-permute-start | bytes 786440 | tf_op jit(solution)/shard_map/ppermute | solution.py:296
  44.1 2.3 %collective-permute-done.6.refs_1_ = bf16[256,1024]{1,0:T(8,128)(2,1)S(1)} collective-permute-done((bf16[256,1024]{1,0:T(8,128)(2,1)}, bf16[256,1024]{1,0:T(8,128)(2,1)S(1)}, u32[]{:S(2)}, u32[]{:S(2)}) %collective-permute-start.6) | collective-permute-done | bytes 524320 | tf_op jit(solution)/shard_map/ppermute | solution.py:292
  46.4 2.8 %halo.4 = (f32[4,8,256]{2,1,0:T(8,128)S(1)}, f32[4,8,256]{2,1,0:T(8,128)S(1)}, f32[4,1024,128]{2,1,0:T(8,128)S(1)}) custom-call(s32[4,4]{1,0:T(4,128)S(1)} %bitcast.17, s32[4]{0:T(128)S(1)} %bitcast.22, s32[1]{0:T(128)} %bitcast.2.pos_ref, ...), custom_call_target="tpu_custom_call", output_to_operand_aliasing={{0}: (8, {}), {1}: (9, {}), {2}: (10, {})} | custom-call | flops 1000 | bytes 1000 | tf_op jit(solution)/shard_map/halo/pallas_call | solution.py:259
  49.3 0.8 %collective-permute-done.7.refs_2_ = bf16[1024,128]{1,0:T(8,128)(2,1)S(1)} collective-permute-done((bf16[1024,128]{1,0:T(8,128)(2,1)S(1)}, bf16[1024,128]{1,0:T(8,128)(2,1)S(1)}, u32[]{:S(2)}, u32[]{:S(2)}) %collective-permute-start.7) | collective-permute-done | bytes 262176 | tf_op jit(solution)/shard_map/ppermute | solution.py:288
  50.1 1.2 %linear.1.refs_5_ = f32[1024,512]{1,0:T(8,128)S(1)} custom-call(s32[1]{0:T(128)} %bitcast.2.pos_ref, bf16[512,1024]{1,0:T(8,128)(2,1)S(1)} %copy-done.7, f32[1024,512]{1,0:T(8,128)S(1)} %within.1.n_ref, bf16[1024,128]{1,0:T(8,128)(2,1)S(1)} %collective-permute-done.3.refs_0_, bf16[1024,128]{1,0:T(8,128)(2,1)S(1)} %collective-permute-done.4.refs_1_, ...), custom_call_target="tpu_custom_call" | custom-call | flops 1000 | bytes 1000 | tf_op jit(solution)/shard_map/linear/pallas_call | solution.py:259
  51.3 5.0 %collective-permute-done.8.refs_0_ = bf16[128,1024]{1,0:T(8,128)(2,1)S(1)} collective-permute-done((bf16[128,1024]{1,0:T(8,128)(2,1)S(1)}, bf16[128,1024]{1,0:T(8,128)(2,1)S(1)}, u32[]{:S(2)}, u32[]{:S(2)}) %collective-permute-start.8) | collective-permute-done | bytes 262176 | tf_op jit(solution)/shard_map/ppermute | solution.py:292
  56.3 1.7 %halo.5 = (f32[4,8,256]{2,1,0:T(8,128)S(1)}, f32[4,8,256]{2,1,0:T(8,128)S(1)}, f32[4,1024,128]{2,1,0:T(8,128)S(1)}) custom-call(s32[4,4]{1,0:T(4,128)S(1)} %bitcast.18, s32[4]{0:T(128)S(1)} %bitcast.23, s32[1]{0:T(128)} %bitcast.2.pos_ref, ...), custom_call_target="tpu_custom_call", output_to_operand_aliasing={{0}: (7, {}), {1}: (8, {}), {2}: (9, {})} | custom-call | flops 1000 | bytes 1000 | tf_op jit(solution)/shard_map/halo/pallas_call | solution.py:259
  58.0 5.6 %final.1 = (bf16[512,1024]{1,0:T(8,128)(2,1)}, f32[4,8,256]{2,1,0:T(8,128)S(1)}, f32[4,8,256]{2,1,0:T(8,128)S(1)}, f32[4,1024,128]{2,1,0:T(8,128)S(1)}) custom-call(s32[4,4]{1,0:T(4,128)S(1)} %bitcast.19, s32[4]{0:T(128)S(1)} %bitcast.24, s32[1]{0:T(128)} %bitcast.2.pos_ref, ...), custom_call_target="tpu_custom_call", output_to_operand_aliasing={{1}: (10, {}), {2}: (11, {}), {3}: (12, {})} | custom-call | flops 1000 | bytes 1000 | tf_op jit(solution)/shard_map/final/pallas_call | solution.py:259
  (21 shorter events, 0.1 us)
Async XLA Ops:
  1.9 23.2 %collective-permute-start.5 = (bf16[256,1024]{1,0:T(8,128)(2,1)}, bf16[256,1024]{1,0:T(8,128)(2,1)}, u32[]{:S(2)}, u32[]{:S(2)}) collective-permute-start(bf16[256,1024]{1,0:T(8,128)(2,1)} %slice_bitcast_fusion), channel_id=1, source_target_pairs={{0,2},{2,0},{4,6},{6,4},{8,10},{10,8},{12,14},{14,12},{1,3},{3,1},... | collective-permute-start | bytes 1572872 | tf_op jit(solution)/shard_map/ppermute | solution.py:288
  6.3 1.6 %copy-start = (bf16[1024,1024]{1,0:T(8,128)(2,1)S(1)}, bf16[1024,1024]{1,0:T(8,128)(2,1)}, u32[]{:S(2)}) copy-start(bf16[1024,1024]{1,0:T(8,128)(2,1)} %refs_2_.3) | copy-start | bytes 6291460
  7.9 1.2 %copy-start.2 = (bf16[1,512,1024]{2,1,0:T(8,128)(2,1)S(1)}, bf16[1,512,1024]{2,1,0:T(8,128)(2,1)}, u32[]{:S(2)}) copy-start(bf16[1,512,1024]{2,1,0:T(8,128)(2,1)} %param.6) | copy-start | bytes 3145732
  9.1 5.9 %copy-start.9 = (s32[1,4,4]{2,1,0:T(4,128)S(1)}, s32[1,4,4]{2,1,0:T(4,128)}, u32[]{:S(2)}) copy-start(s32[1,4,4]{2,1,0:T(4,128)} %param.10) | copy-start | bytes 196
  9.1 5.9 %copy-start.10 = (s32[1,4]{1,0:T(1,128)S(1)}, s32[1,4]{1,0:T(1,128)}, u32[]{:S(2)}) copy-start(s32[1,4]{1,0:T(1,128)} %param.11) | copy-start | bytes 52
  12.5 1.0 %copy-start.4 = (bf16[1024,512]{1,0:T(8,128)(2,1)}, bf16[1024,512]{1,0:T(8,128)(2,1)S(1)}, u32[]{:S(2)}) copy-start(bf16[1024,512]{1,0:T(8,128)(2,1)S(1)} %get-tuple-element.36.vt_ref) | copy-start | bytes 3145732
  13.5 1.0 %copy-start.6 = (bf16[512,1024]{1,0:T(8,128)(2,1)}, bf16[512,1024]{1,0:T(8,128)(2,1)S(1)}, u32[]{:S(2)}) copy-start(bf16[512,1024]{1,0:T(8,128)(2,1)S(1)} %get-tuple-element.50.f_ref) | copy-start | bytes 3145732
  14.5 8.0 %collective-permute-start.3 = (bf16[1024,128]{1,0:T(8,128)(2,1)}, bf16[1024,128]{1,0:T(8,128)(2,1)S(1)}, u32[]{:S(2)}, u32[]{:S(2)}) collective-permute-start(bf16[1024,128]{1,0:T(8,128)(2,1)} %get-tuple-element.32), channel_id=1, source_target_pairs={{0,2},{2,0},{4,6},{6,4},{8,10},{10,8},{12,14},{14,12},{1,3},{3,1},... | collective-permute-start | bytes 786440 | tf_op jit(solution)/shard_map/ppermute | solution.py:288
  15.0 12.5 %copy-start.3 = (bf16[1,512,1024]{2,1,0:T(8,128)(2,1)S(1)}, bf16[1,512,1024]{2,1,0:T(8,128)(2,1)}, u32[]{:S(2)}) copy-start(bf16[1,512,1024]{2,1,0:T(8,128)(2,1)} %param.6) | copy-start | bytes 3145732
  15.0 1.3 %copy-start.5 = (bf16[1024,512]{1,0:T(8,128)(2,1)S(1)}, bf16[1024,512]{1,0:T(8,128)(2,1)}, u32[]{:S(2)}) copy-start(bf16[1024,512]{1,0:T(8,128)(2,1)} %copy-done.4) | copy-start | bytes 3145732
  16.3 11.4 %copy-start.7 = (bf16[512,1024]{1,0:T(8,128)(2,1)S(1)}, bf16[512,1024]{1,0:T(8,128)(2,1)}, u32[]{:S(2)}) copy-start(bf16[512,1024]{1,0:T(8,128)(2,1)} %copy-done.6) | copy-start | bytes 3145732
  23.5 10.1 %collective-permute-start.4 = (bf16[1024,128]{1,0:T(8,128)(2,1)S(1)}, bf16[1024,128]{1,0:T(8,128)(2,1)S(1)}, u32[]{:S(2)}, u32[]{:S(2)}) collective-permute-start(bf16[1024,128]{1,0:T(8,128)(2,1)S(1)} %add.6), channel_id=1, source_target_pairs={{0,4},{2,6},{4,0},{6,2},{8,12},{10,14},{12,8},{14,10},{1,5},{3,7},... | collective-permute-start | bytes 786440 | tf_op jit(solution)/shard_map/ppermute | solution.py:288
  25.1 21.3 %collective-permute-start.6 = (bf16[256,1024]{1,0:T(8,128)(2,1)}, bf16[256,1024]{1,0:T(8,128)(2,1)S(1)}, u32[]{:S(2)}, u32[]{:S(2)}) collective-permute-start(bf16[256,1024]{1,0:T(8,128)(2,1)} %collective-permute-done.5.refs_0_), channel_id=1, source_target_pairs={{0,4},{4,8},{8,12},{6,2},{10,6},{14,10},{1,5},{5,9},{9,13},{7,3},{... | collective-permute-start | bytes 1572872 | tf_op jit(solution)/shard_map/ppermute | solution.py:292
  27.6 9.0 %collective-permute-start.2 = (bf16[128,1024]{1,0:T(8,128)(2,1)S(1)}, bf16[128,1024]{1,0:T(8,128)(2,1)S(1)}, u32[]{:S(2)}, u32[]{:S(2)}) collective-permute-start(bf16[128,1024]{1,0:T(8,128)(2,1)S(1)} %get-tuple-element.59), channel_id=1, source_target_pairs={{0,2},{2,0},{4,6},{6,4},{8,10},{10,8},{12,14},{14,12},{1,3},{3,1},... | collective-permute-start | bytes 786440 | tf_op jit(solution)/shard_map/ppermute | solution.py:288
  27.7 2.7 %copy-start.1 = (bf16[1024,1024]{1,0:T(8,128)(2,1)S(1)}, bf16[1024,1024]{1,0:T(8,128)(2,1)}, u32[]{:S(2)}) copy-start(bf16[1024,1024]{1,0:T(8,128)(2,1)} %refs_2_.3) | copy-start | bytes 6291460
  33.7 16.4 %collective-permute-start.7 = (bf16[1024,128]{1,0:T(8,128)(2,1)S(1)}, bf16[1024,128]{1,0:T(8,128)(2,1)S(1)}, u32[]{:S(2)}, u32[]{:S(2)}) collective-permute-start(bf16[1024,128]{1,0:T(8,128)(2,1)S(1)} %add.7), channel_id=1, source_target_pairs={{0,8},{2,10},{4,12},{6,14},{8,0},{10,2},{12,4},{14,6},{1,9},{3,11}... | collective-permute-start | bytes 786440 | tf_op jit(solution)/shard_map/ppermute | solution.py:288
  36.6 19.7 %collective-permute-start.8 = (bf16[128,1024]{1,0:T(8,128)(2,1)S(1)}, bf16[128,1024]{1,0:T(8,128)(2,1)S(1)}, u32[]{:S(2)}, u32[]{:S(2)}) collective-permute-start(bf16[128,1024]{1,0:T(8,128)(2,1)S(1)} %collective-permute-done.2.refs_0_), channel_id=1, source_target_pairs={{0,4},{4,8},{8,12},{6,2},{10,6},{14,10},{1,5},{5,9},{9,13},{7,3},{... | collective-permute-start | bytes 786440 | tf_op jit(solution)/shard_map/ppermute | solution.py:292
  39.3 18.6 %collective-permute-start = (bf16[128,1024]{1,0:T(8,128)(2,1)S(1)}, bf16[128,1024]{1,0:T(8,128)(2,1)S(1)}, u32[]{:S(2)}, u32[]{:S(2)}) collective-permute-start(bf16[128,1024]{1,0:T(8,128)(2,1)S(1)} %get-tuple-element.60), channel_id=1, source_target_pairs={{0,2},{2,0},{4,6},{6,4},{8,10},{10,8},{12,14},{14,12},{1,3},{3,1},... | collective-permute-start | bytes 786440 | tf_op jit(solution)/shard_map/ppermute | solution.py:288
  39.4 18.5 %collective-permute-start.1 = (bf16[128,1024]{1,0:T(8,128)(2,1)S(1)}, bf16[128,1024]{1,0:T(8,128)(2,1)S(1)}, u32[]{:S(2)}, u32[]{:S(2)}) collective-permute-start(bf16[128,1024]{1,0:T(8,128)(2,1)S(1)} %get-tuple-element.60), channel_id=1, source_target_pairs={{2,4},{6,8},{10,12},{4,2},{8,6},{12,10},{3,5},{7,9},{11,13},{5,3},... | collective-permute-start | bytes 786440 | tf_op jit(solution)/shard_map/ppermute | solution.py:296
  56.3 1.7 %copy-start.8 = (bf16[1024,1024]{1,0:T(8,128)(2,1)S(1)}, bf16[1024,1024]{1,0:T(8,128)(2,1)}, u32[]{:S(2)}) copy-start(bf16[1024,1024]{1,0:T(8,128)(2,1)} %refs_6_.1) | copy-start | bytes 6291460
where the time goes:
time: 64.1 us; the launch traced here: 63.5 us
  Pallas kernels  25.6 us (40%)
  starting transfers between devices  16.6 us (26%)
  local copies, waits for them, and re-layouts  10.9 us (17%)
  waiting for transfers between devices  9.22 us (14%)
  other arithmetic  1.09 us (2%)
    pallas_call x8, Pallas kernels, call(): pl.pallas_call(kernel, name=name, in_specs=[SMEM] * smem + [VMEM] * (len(...  25.6 us
    unnamed x23, local copies, waits for them, and re-layouts  8.98 us
    ppermute x2, waiting for transfers between devices, onward(): return lax.ppermute(value, 'seq', pairs)  7.27 us
    ppermute x6, starting transfers between devices, swap(): return lax.ppermute(value, 'seq', [(i, i ^ bit) for i in range(count)])  6.78 us
    ppermute x2, starting transfers between devices, onward(): return lax.ppermute(value, 'seq', pairs)  5.09 us
    ppermute x1, starting transfers between devices, across(): lax.ppermute(value, 'seq', [(i, i + 1) for i in odd] + [(i + 1, i) for i...  4.71 us
    ppermute x6, waiting for transfers between devices, swap(): return lax.ppermute(value, 'seq', [(i, i ^ bit) for i in range(count)])  1.95 us
    slice x1, local copies, waits for them, and re-layouts, on_device(): near_a = swap(own[:cuts[1]], 1)  1.89 us
  transfers between devices with their start and end apart: 9, of which 4 were waited for; matrix products, arithmetic and copies ran while one was open for 6% of the time, Pallas kernels for 32%

commit v1 on v0

--- a/solution.py
+++ b/solution.py
@@ -14,7 +14,6 @@
 F32 = jnp.float32
 BF16 = jnp.bfloat16
 NT = (((1,), (1,)), ((), ()))
-VMEM = pl.BlockSpec(memory_space=pltpu.VMEM)
 SMEM = pl.BlockSpec(memory_space=pltpu.SMEM)
 MIB = 1 << 20
 
@@ -36,14 +35,38 @@
     vt_ref[...] = dot_nt(wvt_ref[...], x).astype(BF16)
 
 
-def own_kernel(x_ref, wk_ref, wvt_ref, k_ref, f_ref, vt_ref, s_ref):
-    project(x_ref[...], wk_ref, wvt_ref, k_ref, vt_ref)
-    for h in range(HL):
-        part = slice(h * DL, (h + 1) * DL)
-        k = k_ref[:, part].astype(F32)
-        f = (k / (1.0 + jnp.exp(-k))).astype(BF16)
-        f_ref[:, part] = f
-        s_ref[part, :] = dot_nn(vt_ref[part, :], f).astype(BF16)
+def cut_kernel(x_ref, a_ref, sem):
+    copy = pltpu.make_async_copy(x_ref.at[: a_ref.shape[0]], a_ref, sem)
+    copy.start()
+    copy.wait()
+
+
+def own_kernel(x_hbm, wk_hbm, wv_hbm, k_ref, f_ref, vt_ref, s_ref, wvt_ref, x_ref, wk_ref, wv_ref, sems):
+    width = x_ref.shape[1]
+    step = 256
+    tiles = [slice(i, i + step) for i in range(0, width, step)]
+    n = len(tiles)
+    copies = [pltpu.make_async_copy(x_hbm, x_ref, sems.at[0])]
+    for i, (src, dst) in enumerate(((wk_hbm, wk_ref), (wv_hbm, wv_ref))):
+        for j, part in enumerate(tiles):
+            copies.append(pltpu.make_async_copy(src.at[:, part], dst.at[:, part], sems.at[1 + i * n + j]))
+    for copy in copies:
+        copy.start()
+    copies[0].wait()
+    for j, part in enumerate(tiles):
+        copies[1 + j].wait()
+        k = dot_nn(x_ref[...], wk_ref[:, part]).astype(BF16)
+        k_ref[:, part] = k
+        k = k.astype(F32)
+        f_ref[:, part] = (k / (1.0 + jnp.exp(-k))).astype(BF16)
+    for j, part in enumerate(tiles):
+        copies[1 + n + j].wait()
+        turned = wv_ref[:, part].T
+        wvt_ref[part, :] = turned
+        vt_ref[part, :] = dot_nt(turned, x_ref[...]).astype(BF16)
+        for h in range(part.start, part.stop, DL):
+            head = slice(h, h + DL)
+            s_ref[head, :] = dot_nn(vt_ref[head, :], f_ref[:, head]).astype(BF16)
 
 
 def within_kernel(f_ref, vt_ref, n_ref):
@@ -255,16 +278,32 @@
     out_ref[...] = dot_nn(comb_ref[...], wo_ref[...]).astype(BF16)
 
 
-def call(kernel, name, ins, outs, smem=0, scratch=(), aliases=None, limit=20 * MIB):
+COSTLY = ("halo_b",)
+
+
+def call(
+    kernel,
+    name,
+    ins,
+    outs,
+    smem=0,
+    scratch=(),
+    aliases=None,
+    limit=20 * MIB,
+    space=pltpu.VMEM,
+    out_space=pltpu.VMEM,
+):
     return pl.pallas_call(
         kernel,
         name=name,
-        in_specs=[SMEM] * smem + [VMEM] * (len(ins) - smem),
-        out_specs=[VMEM] * len(outs),
+        in_specs=[SMEM] * smem + [pl.BlockSpec(memory_space=space)] * (len(ins) - smem),
+        out_specs=[pl.BlockSpec(memory_space=out_space)] * len(outs),
         out_shape=[jax.ShapeDtypeStruct(s, d) for s, d in outs],
         scratch_shapes=list(scratch),
         input_output_aliases=aliases or {},
-        cost_estimate=pl.CostEstimate(flops=1000, bytes_accessed=1000, transcendentals=0),
+        cost_estimate=pl.CostEstimate(
+            flops=10**11 if name in COSTLY else 1, bytes_accessed=1000, transcendentals=0
+        ),
         compiler_params=pltpu.CompilerParams(vmem_limit_bytes=limit),
     )(*ins)
 
@@ -303,12 +342,12 @@
             pltpu.VMEM((width, total), BF16),
         )
 
-    def join_halo(softmax, pieces, arrays):
+    def join_halo(name, softmax, pieces, arrays):
         ins = tables + tuple(arrays) + (qk_weight, value_t, keyed) + tuple(softmax)
         first = len(ins) - 3
         return call(
             functools.partial(halo_kernel, size, pieces),
-            "halo",
+            name,
             ins,
             shapes,
             smem=3,
@@ -317,13 +356,36 @@
         )
 
     cuts = [0, half * size, (half + 1) * size, rows]
-    near_a = swap(own[: cuts[1]], 1)
-    value_t = value_weight.T
-    keyed, features, values_t, state = call(
+    (first_rows,) = call(
+        cut_kernel,
+        "cut",
+        (own,),
+        [((cuts[1], width), BF16)],
+        scratch=(pltpu.SemaphoreType.DMA(()),),
+        limit=60 * MIB,
+        space=pltpu.HBM,
+        out_space=pltpu.HBM,
+    )
+    near_a = swap(first_rows, 1)
+    keyed, features, values_t, state, value_t = call(
         own_kernel,
         "own",
-        (own, qk_weight, value_t),
-        [((rows, width), BF16), ((rows, width), BF16), ((width, rows), BF16), ((width, DL), BF16)],
+        (own, qk_weight, value_weight),
+        [
+            ((rows, width), BF16),
+            ((rows, width), BF16),
+            ((width, rows), BF16),
+            ((width, DL), BF16),
+            ((width, width), BF16),
+        ],
+        scratch=(
+            pltpu.VMEM((rows, width), BF16),
+            pltpu.VMEM((width, width), BF16),
+            pltpu.VMEM((width, width), BF16),
+            pltpu.SemaphoreType.DMA((1 + 2 * (width // 256),)),
+        ),
+        limit=50 * MIB,
+        space=pltpu.HBM,
     )
     heard = [swap(state, 1)]
     rest = after(own, state)
@@ -334,12 +396,13 @@
     softmax = call(
         functools.partial(own_attention_kernel, size),
         "own_attention",
-        tables + (keyed, values_t),
+        tables + (after(keyed, near_a), values_t),
         shapes,
         smem=3,
         scratch=(pltpu.SMEM((blocks + 1,), jnp.int32),),
-    )
-    far_a = onward(after(near_a, softmax[0]))
+
+    )
+    far_a = onward(near_a)
     total = state + after(heard[0], softmax[0])
     heard.append(swap(total, 2))
     (within,) = call(
@@ -348,7 +411,7 @@
         (after(features, near_a, total), values_t),
         [((width, rows), F32)],
     )
-    softmax = join_halo(softmax, [(True, 0)], [after(near_a, within)])
+    softmax = join_halo("halo_a", softmax, [(True, 0)], [after(near_a, within)])
     far_b = onward(after(near_b, softmax[0]))
     stride = 4
     while stride < count:
@@ -356,7 +419,7 @@
         heard.append(swap(total, stride))
         stride *= 2
     softmax = join_halo(
-        softmax, [(True, half), (False, 0)], [after(near_b, total), far_a]
+        "halo_b", softmax, [(True, half), (False, 0)], [after(near_b, total), far_a]
     )
     (linear,) = call(
         functools.partial(linear_kernel, len(heard)),
@@ -365,7 +428,7 @@
         [((width, rows), F32)],
         smem=1,
     )
-    softmax = join_halo(softmax, [(False, half)], [after(far_b, linear)])
+    softmax = join_halo("halo_c", softmax, [(False, half)], [after(far_b, linear)])
     pieces = [(True, half + 1), (False, half + 1)]
     arrays = (near_c, far_c)
     ins = tables + arrays + (qk_weight, value_t, keyed, linear, out_weight) + tuple(softmax)

time: 64.1 us -> 83.9 us (1.31)
  the two profiles are of different devices: /device:TPU:16 before, /device:TPU:6 now
where the time goes in v1:
time: 83.9 us; the launch traced here: 84 us
  Pallas kernels  49.3 us (59%)
  starting transfers between devices  16.7 us (20%)
  waiting for transfers between devices  15.9 us (19%)
  other arithmetic  1.11 us (1%)
  local copies, waits for them, and re-layouts  0.85 us (1%)
    pallas_call x9, Pallas kernels, call(): pl.pallas_call(kernel, name=name, in_specs=[SMEM] * smem + [pl.BlockSpec(...  49.3 us
    ppermute x6, waiting for transfers between devices, swap(): return lax.ppermute(value, 'seq', [(i, i ^ bit) for i in range(count)])  15.9 us
    ppermute x6, starting transfers between devices, swap(): return lax.ppermute(value, 'seq', [(i, i ^ bit) for i in range(count)])  9.38 us
    ppermute x1, starting transfers between devices, across(): lax.ppermute(value, 'seq', [(i, i + 1) for i in odd] + [(i + 1, i) for i...  4.57 us
    ppermute x2, starting transfers between devices, onward(): return lax.ppermute(value, 'seq', pairs)  2.75 us
  transfers between devices with their start and end apart: 9, of which 2 were waited for; matrix products, arithmetic and copies ran while one was open for 2% of the time, Pallas kernels for 33%

profile of v1, /device:TPU:6, one launch (start us, length us, event | category | flops | bytes accessed | tf_op | source)
XLA Modules:
  0.0 84.0 jit_solution(11476371752301378044)
XLA Ops:
  0.0 17.0 %cut.1 = bf16[256,1024]{1,0:T(8,128)(2,1)} custom-call(bf16[512,1024]{1,0:T(8,128)(2,1)} %bitcast.15), custom_call_target="tpu_custom_call" | custom-call | flops 1 | bytes 1000 | tf_op jit(solution)/shard_map/cut/pallas_call | solution.py:296
  17.0 0.0 copy-start.5
  17.0 0.0 copy-start.3
  17.0 0.0 copy-start.4
  17.0 0.6 collective-permute-start.4
  17.6 8.1 %own.1 = (bf16[512,1024]{1,0:T(8,128)(2,1)S(1)}, bf16[512,1024]{1,0:T(8,128)(2,1)S(1)}, bf16[1024,512]{1,0:T(8,128)(2,1)S(1)}, bf16[1024,128]{1,0:T(8,128)(2,1)}, bf16[1024,1024]{1,0:T(8,128)(2,1)}) custom-call(bf16[512,1024]{1,0:T(8,128)(2,1)} %bitcast.16, bf16[1024,1024]{1,0:T(8,128)(2,1)} %refs_2_.3, bf16[1024,1024]{1,0:T(8,128)(2,1)} %wv_hbm.1), custom_call_target="tpu_custom_call" | custom-call | flops 1 | bytes 1000 | tf_op jit(solution)/shard_map/own/pallas_call | solution.py:296
  25.7 1.6 %collective-permute-start.3 = (bf16[1024,128]{1,0:T(8,128)(2,1)}, bf16[1024,128]{1,0:T(8,128)(2,1)S(1)}, u32[]{:S(2)}, u32[]{:S(2)}) collective-permute-start(bf16[1024,128]{1,0:T(8,128)(2,1)} %get-tuple-element.33), channel_id=1, source_target_pairs={{0,2},{2,0},{4,6},{6,4},{8,10},{10,8},{12,14},{14,12},{1,3},{3,1},... | collective-permute-start | bytes 786440 | tf_op jit(solution)/shard_map/ppermute | solution.py:327
  27.3 4.9 %collective-permute-done.4.refs_0_ = bf16[256,1024]{1,0:T(8,128)(2,1)} collective-permute-done((bf16[256,1024]{1,0:T(8,128)(2,1)}, bf16[256,1024]{1,0:T(8,128)(2,1)}, u32[]{:S(2)}, u32[]{:S(2)}) %collective-permute-start.4) | collective-permute-done | bytes 524320 | tf_op jit(solution)/shard_map/ppermute | solution.py:327
  32.2 1.3 %collective-permute-start.6 = (bf16[256,1024]{1,0:T(8,128)(2,1)}, bf16[256,1024]{1,0:T(8,128)(2,1)}, u32[]{:S(2)}, u32[]{:S(2)}) collective-permute-start(bf16[256,1024]{1,0:T(8,128)(2,1)} %collective-permute-done.4.refs_0_), channel_id=1, source_target_pairs={{0,4},{4,8},{8,12},{6,2},{10,6},{14,10},{1,5},{5,9},{9,13},{7,3},{... | collective-permute-start | bytes 1572872 | tf_op jit(solution)/shard_map/ppermute | solution.py:331
  33.5 0.8 fusion
  34.3 3.5 %collective-permute-start.2 = (bf16[128,1024]{1,0:T(8,128)(2,1)}, bf16[128,1024]{1,0:T(8,128)(2,1)}, u32[]{:S(2)}, u32[]{:S(2)}) collective-permute-start(bf16[128,1024]{1,0:T(8,128)(2,1)} %get-tuple-element.61), channel_id=1, source_target_pairs={{0,2},{2,0},{4,6},{6,4},{8,10},{10,8},{12,14},{14,12},{1,3},{3,1},... | collective-permute-start | bytes 786440 | tf_op jit(solution)/shard_map/ppermute | solution.py:327
  37.8 4.6 %own_attention.1 = (f32[4,8,256]{2,1,0:T(8,128)S(1)}, f32[4,8,256]{2,1,0:T(8,128)S(1)}, f32[4,1024,128]{2,1,0:T(8,128)S(1)}) custom-call(s32[4,4]{1,0:T(4,128)S(1)} %bitcast.5, s32[4]{0:T(128)S(1)} %bitcast.10, s32[1]{0:T(128)} %bitcast.2.pos_ref, bf16[512,1024]{1,0:T(8,128)(2,1)S(1)} %get-tuple-element.38.k_ref.refs_3_.refs_4_, ...), custom_call_target="tpu_custom_call" | custom-call | flops 1 | bytes 1000 | tf_op jit(solution)/shard_map/own_attention/pallas_call | solution.py:296
  42.5 0.0 collective-permute-done.3.refs_0_
  42.5 1.0 %add.6 = bf16[1024,128]{1,0:T(8,128)(2,1)S(1)} add(bf16[1024,128]{1,0:T(8,128)(2,1)} %get-tuple-element.33, bf16[1024,128]{1,0:T(8,128)(2,1)S(1)} %collective-permute-done.3.refs_0_) | non-fusion elementwise | flops 131072 | bytes 786432 | tf_op jit(solution)/shard_map/add | solution.py:406
  43.5 0.9 %collective-permute-start.5 = (bf16[1024,128]{1,0:T(8,128)(2,1)S(1)}, bf16[1024,128]{1,0:T(8,128)(2,1)S(1)}, u32[]{:S(2)}, u32[]{:S(2)}) collective-permute-start(bf16[1024,128]{1,0:T(8,128)(2,1)S(1)} %add.6), channel_id=1, source_target_pairs={{0,4},{2,6},{4,0},{6,2},{8,12},{10,14},{12,8},{14,10},{1,5},{3,7},... | collective-permute-start | bytes 786440 | tf_op jit(solution)/shard_map/ppermute | solution.py:327
  44.4 0.0 collective-permute-start
  44.4 4.6 %collective-permute-start.1 = (bf16[128,1024]{1,0:T(8,128)(2,1)S(1)}, bf16[128,1024]{1,0:T(8,128)(2,1)S(1)}, u32[]{:S(2)}, u32[]{:S(2)}) collective-permute-start(bf16[128,1024]{1,0:T(8,128)(2,1)S(1)} %copy-done.6), channel_id=1, source_target_pairs={{2,4},{6,8},{10,12},{4,2},{8,6},{12,10},{3,5},{7,9},{11,13},{5,3},... | collective-permute-start | bytes 786440 | tf_op jit(solution)/shard_map/ppermute | solution.py:335
  49.0 0.0 copy-start
  49.0 2.7 %within.1.n_ref = f32[1024,512]{1,0:T(8,128)S(1)} custom-call(bf16[512,1024]{1,0:T(8,128)(2,1)S(1)} %get-tuple-element.52.f_ref, bf16[1024,512]{1,0:T(8,128)(2,1)S(1)} %get-tuple-element.39.vt_ref), custom_call_target="tpu_custom_call" | custom-call | flops 1 | bytes 1000 | tf_op jit(solution)/shard_map/within/pallas_call | solution.py:296
  51.8 3.2 %halo_a.1 = (f32[4,8,256]{2,1,0:T(8,128)S(1)}, f32[4,8,256]{2,1,0:T(8,128)S(1)}, f32[4,1024,128]{2,1,0:T(8,128)S(1)}) custom-call(s32[4,4]{1,0:T(4,128)S(1)} %bitcast.6, s32[4]{0:T(128)S(1)} %bitcast.11, s32[1]{0:T(128)} %bitcast.2.pos_ref, ...), custom_call_target="tpu_custom_call", output_to_operand_aliasing={{0}: (7, {}), {1}: (8, {}), {2}: (9, {})} | custom-call | flops 1 | bytes 1000 | tf_op jit(solution)/shard_map/halo_a/pallas_call | solution.py:296
  54.9 0.0 collective-permute-done.2.refs_0_
  55.0 1.5 %collective-permute-start.8 = (bf16[128,1024]{1,0:T(8,128)(2,1)}, bf16[128,1024]{1,0:T(8,128)(2,1)S(1)}, u32[]{:S(2)}, u32[]{:S(2)}) collective-permute-start(bf16[128,1024]{1,0:T(8,128)(2,1)} %collective-permute-done.2.refs_0_), channel_id=1, source_target_pairs={{0,4},{4,8},{8,12},{6,2},{10,6},{14,10},{1,5},{5,9},{9,13},{7,3},{... | collective-permute-start | bytes 786440 | tf_op jit(solution)/shard_map/ppermute | solution.py:331
  56.4 0.1 add.7
  56.5 2.8 %collective-permute-start.7 = (bf16[1024,128]{1,0:T(8,128)(2,1)S(1)}, bf16[1024,128]{1,0:T(8,128)(2,1)S(1)}, u32[]{:S(2)}, u32[]{:S(2)}) collective-permute-start(bf16[1024,128]{1,0:T(8,128)(2,1)S(1)} %add.7), channel_id=1, source_target_pairs={{0,8},{2,10},{4,12},{6,14},{8,0},{10,2},{12,4},{14,6},{1,9},{3,11}... | collective-permute-start | bytes 786440 | tf_op jit(solution)/shard_map/ppermute | solution.py:327
  59.4 0.0 collective-permute-done.6.refs_1_
  59.4 5.1 %halo_b.1 = (f32[4,8,256]{2,1,0:T(8,128)S(1)}, f32[4,8,256]{2,1,0:T(8,128)S(1)}, f32[4,1024,128]{2,1,0:T(8,128)S(1)}) custom-call(s32[4,4]{1,0:T(4,128)S(1)} %bitcast.7, s32[4]{0:T(128)S(1)} %bitcast.12, s32[1]{0:T(128)} %bitcast.2.pos_ref, ...), custom_call_target="tpu_custom_call", output_to_operand_aliasing={{0}: (8, {}), {1}: (9, {}), {2}: (10, {})} | custom-call | flops 99999997952 | bytes 1000 | tf_op jit(solution)/shard_map/halo_b/pallas_call | solution.py:296
  64.5 10.9 %collective-permute-done.7.refs_2_ = bf16[1024,128]{1,0:T(8,128)(2,1)S(1)} collective-permute-done((bf16[1024,128]{1,0:T(8,128)(2,1)S(1)}, bf16[1024,128]{1,0:T(8,128)(2,1)S(1)}, u32[]{:S(2)}, u32[]{:S(2)}) %collective-permute-start.7) | collective-permute-done | bytes 262176 | tf_op jit(solution)/shard_map/ppermute | solution.py:327
  75.5 1.2 %linear.1.refs_5_ = f32[1024,512]{1,0:T(8,128)S(1)} custom-call(s32[1]{0:T(128)} %bitcast.2.pos_ref, bf16[512,1024]{1,0:T(8,128)(2,1)S(1)} %get-tuple-element.52.f_ref, f32[1024,512]{1,0:T(8,128)S(1)} %within.1.n_ref, bf16[1024,128]{1,0:T(8,128)(2,1)S(1)} %collective-permute-done.3.refs_0_, bf16[1024,128]{1,0:T(8,128)(2,1)S(1)} %collective-permute-done.5.refs_1_, ...), custom_call_target="tpu_custom_call" | custom-call | flops 1 | bytes 1000 | tf_op jit(solution)/shard_map/linear/pallas_call | solution.py:296
  76.7 0.0 copy-start.2
  76.7 2.3 %halo_c.1 = (f32[4,8,256]{2,1,0:T(8,128)S(1)}, f32[4,8,256]{2,1,0:T(8,128)S(1)}, f32[4,1024,128]{2,1,0:T(8,128)S(1)}) custom-call(s32[4,4]{1,0:T(4,128)S(1)} %bitcast.8, s32[4]{0:T(128)S(1)} %bitcast.13, s32[1]{0:T(128)} %bitcast.2.pos_ref, ...), custom_call_target="tpu_custom_call", output_to_operand_aliasing={{0}: (7, {}), {1}: (8, {}), {2}: (9, {})} | custom-call | flops 1 | bytes 1000 | tf_op jit(solution)/shard_map/halo_c/pallas_call | solution.py:296
  79.1 0.0 collective-permute-done.refs_0_
  79.1 4.9 %final.1 = (bf16[512,1024]{1,0:T(8,128)(2,1)}, f32[4,8,256]{2,1,0:T(8,128)S(1)}, f32[4,8,256]{2,1,0:T(8,128)S(1)}, f32[4,1024,128]{2,1,0:T(8,128)S(1)}) custom-call(s32[4,4]{1,0:T(4,128)S(1)} %bitcast.9, s32[4]{0:T(128)S(1)} %bitcast.14, s32[1]{0:T(128)} %bitcast.2.pos_ref, ...), custom_call_target="tpu_custom_call", output_to_operand_aliasing={{1}: (10, {}), {2}: (11, {}), {3}: (12, {})} | custom-call | flops 1 | bytes 1000 | tf_op jit(solution)/shard_map/final/pallas_call | solution.py:296
  (12 shorter events, 0.0 us)
Async XLA Ops:
  17.0 16.5 %copy-start.5 = (bf16[1,512,1024]{2,1,0:T(8,128)(2,1)S(1)}, bf16[1,512,1024]{2,1,0:T(8,128)(2,1)}, u32[]{:S(2)}) copy-start(bf16[1,512,1024]{2,1,0:T(8,128)(2,1)} %param.6) | copy-start | bytes 3145732
  17.0 20.8 %copy-start.3 = (s32[1,4,4]{2,1,0:T(4,128)S(1)}, s32[1,4,4]{2,1,0:T(4,128)}, u32[]{:S(2)}) copy-start(s32[1,4,4]{2,1,0:T(4,128)} %param.10) | copy-start | bytes 196
  17.0 20.8 %copy-start.4 = (s32[1,4]{1,0:T(1,128)S(1)}, s32[1,4]{1,0:T(1,128)}, u32[]{:S(2)}) copy-start(s32[1,4]{1,0:T(1,128)} %param.11) | copy-start | bytes 52
  17.0 15.2 %collective-permute-start.4 = (bf16[256,1024]{1,0:T(8,128)(2,1)}, bf16[256,1024]{1,0:T(8,128)(2,1)}, u32[]{:S(2)}, u32[]{:S(2)}) collective-permute-start(bf16[256,1024]{1,0:T(8,128)(2,1)} %cut.1), channel_id=1, source_target_pairs={{0,2},{2,0},{4,6},{6,4},{8,10},{10,8},{12,14},{14,12},{1,3},{3,1},... | collective-permute-start | bytes 1572872 | tf_op jit(solution)/shard_map/ppermute | solution.py:327
  25.7 16.8 %collective-permute-start.3 = (bf16[1024,128]{1,0:T(8,128)(2,1)}, bf16[1024,128]{1,0:T(8,128)(2,1)S(1)}, u32[]{:S(2)}, u32[]{:S(2)}) collective-permute-start(bf16[1024,128]{1,0:T(8,128)(2,1)} %get-tuple-element.33), channel_id=1, source_target_pairs={{0,2},{2,0},{4,6},{6,4},{8,10},{10,8},{12,14},{14,12},{1,3},{3,1},... | collective-permute-start | bytes 786440 | tf_op jit(solution)/shard_map/ppermute | solution.py:327
  32.2 27.2 %collective-permute-start.6 = (bf16[256,1024]{1,0:T(8,128)(2,1)}, bf16[256,1024]{1,0:T(8,128)(2,1)}, u32[]{:S(2)}, u32[]{:S(2)}) collective-permute-start(bf16[256,1024]{1,0:T(8,128)(2,1)} %collective-permute-done.4.refs_0_), channel_id=1, source_target_pairs={{0,4},{4,8},{8,12},{6,2},{10,6},{14,10},{1,5},{5,9},{9,13},{7,3},{... | collective-permute-start | bytes 1572872 | tf_op jit(solution)/shard_map/ppermute | solution.py:331
  34.3 20.6 %collective-permute-start.2 = (bf16[128,1024]{1,0:T(8,128)(2,1)}, bf16[128,1024]{1,0:T(8,128)(2,1)}, u32[]{:S(2)}, u32[]{:S(2)}) collective-permute-start(bf16[128,1024]{1,0:T(8,128)(2,1)} %get-tuple-element.61), channel_id=1, source_target_pairs={{0,2},{2,0},{4,6},{6,4},{8,10},{10,8},{12,14},{14,12},{1,3},{3,1},... | collective-permute-start | bytes 786440 | tf_op jit(solution)/shard_map/ppermute | solution.py:327
  37.8 6.6 %copy-start.6 = (bf16[128,1024]{1,0:T(8,128)(2,1)S(1)}, bf16[128,1024]{1,0:T(8,128)(2,1)}, u32[]{:S(2)}) copy-start(bf16[128,1024]{1,0:T(8,128)(2,1)} %get-tuple-element.62) | copy-start | bytes 786436
  43.5 12.9 %collective-permute-start.5 = (bf16[1024,128]{1,0:T(8,128)(2,1)S(1)}, bf16[1024,128]{1,0:T(8,128)(2,1)S(1)}, u32[]{:S(2)}, u32[]{:S(2)}) collective-permute-start(bf16[1024,128]{1,0:T(8,128)(2,1)S(1)} %add.6), channel_id=1, source_target_pairs={{0,4},{2,6},{4,0},{6,2},{8,12},{10,14},{12,8},{14,10},{1,5},{3,7},... | collective-permute-start | bytes 786440 | tf_op jit(solution)/shard_map/ppermute | solution.py:327
  44.4 34.7 %collective-permute-start = (bf16[128,1024]{1,0:T(8,128)(2,1)S(1)}, bf16[128,1024]{1,0:T(8,128)(2,1)S(1)}, u32[]{:S(2)}, u32[]{:S(2)}) collective-permute-start(bf16[128,1024]{1,0:T(8,128)(2,1)S(1)} %copy-done.6), channel_id=1, source_target_pairs={{0,2},{2,0},{4,6},{6,4},{8,10},{10,8},{12,14},{14,12},{1,3},{3,1},... | collective-permute-start | bytes 786440 | tf_op jit(solution)/shard_map/ppermute | solution.py:327
  44.4 34.7 %collective-permute-start.1 = (bf16[128,1024]{1,0:T(8,128)(2,1)S(1)}, bf16[128,1024]{1,0:T(8,128)(2,1)S(1)}, u32[]{:S(2)}, u32[]{:S(2)}) collective-permute-start(bf16[128,1024]{1,0:T(8,128)(2,1)S(1)} %copy-done.6), channel_id=1, source_target_pairs={{2,4},{6,8},{10,12},{4,2},{8,6},{12,10},{3,5},{7,9},{11,13},{5,3},... | collective-permute-start | bytes 786440 | tf_op jit(solution)/shard_map/ppermute | solution.py:335
  49.0 2.8 %copy-start = (bf16[1024,1024]{1,0:T(8,128)(2,1)S(1)}, bf16[1024,1024]{1,0:T(8,128)(2,1)}, u32[]{:S(2)}) copy-start(bf16[1024,1024]{1,0:T(8,128)(2,1)} %refs_2_.3) | copy-start | bytes 6291460
  49.0 2.8 %copy-start.1 = (bf16[1024,1024]{1,0:T(8,128)(2,1)S(1)}, bf16[1024,1024]{1,0:T(8,128)(2,1)}, u32[]{:S(2)}) copy-start(bf16[1024,1024]{1,0:T(8,128)(2,1)} %get-tuple-element.35.refs_2_.refs_3_) | copy-start | bytes 6291460
  55.0 21.8 %collective-permute-start.8 = (bf16[128,1024]{1,0:T(8,128)(2,1)}, bf16[128,1024]{1,0:T(8,128)(2,1)S(1)}, u32[]{:S(2)}, u32[]{:S(2)}) collective-permute-start(bf16[128,1024]{1,0:T(8,128)(2,1)} %collective-permute-done.2.refs_0_), channel_id=1, source_target_pairs={{0,4},{4,8},{8,12},{6,2},{10,6},{14,10},{1,5},{5,9},{9,13},{7,3},{... | collective-permute-start | bytes 786440 | tf_op jit(solution)/shard_map/ppermute | solution.py:331
  56.5 18.9 %collective-permute-start.7 = (bf16[1024,128]{1,0:T(8,128)(2,1)S(1)}, bf16[1024,128]{1,0:T(8,128)(2,1)S(1)}, u32[]{:S(2)}, u32[]{:S(2)}) collective-permute-start(bf16[1024,128]{1,0:T(8,128)(2,1)S(1)} %add.7), channel_id=1, source_target_pairs={{0,8},{2,10},{4,12},{6,14},{8,0},{10,2},{12,4},{14,6},{1,9},{3,11}... | collective-permute-start | bytes 786440 | tf_op jit(solution)/shard_map/ppermute | solution.py:327
  76.7 2.4 %copy-start.2 = (bf16[1024,1024]{1,0:T(8,128)(2,1)S(1)}, bf16[1024,1024]{1,0:T(8,128)(2,1)}, u32[]{:S(2)}) copy-start(bf16[1024,1024]{1,0:T(8,128)(2,1)} %refs_6_.1) | copy-start | bytes 6291460

commit v2 on v1

--- a/solution.py
+++ b/solution.py
@@ -35,41 +35,58 @@
     vt_ref[...] = dot_nt(wvt_ref[...], x).astype(BF16)
 
 
-def cut_kernel(x_ref, a_ref, sem):
-    copy = pltpu.make_async_copy(x_ref.at[: a_ref.shape[0]], a_ref, sem)
+def cut_kernel(x_hbm, a_ref, sem):
+    copy = pltpu.make_async_copy(x_hbm.at[: a_ref.shape[0]], a_ref, sem)
     copy.start()
     copy.wait()
 
 
-def own_kernel(x_hbm, wk_hbm, wv_hbm, k_ref, f_ref, vt_ref, s_ref, wvt_ref, x_ref, wk_ref, wv_ref, sems):
+def own_kernel(
+    x_hbm, wk_hbm, wv_hbm, k_hbm, f_hbm, vt_hbm, wvt_hbm, b_hbm, s_ref, x_ref, wk_ref, wv_ref, k_ref, f_ref, vt_ref,
+    wvt_ref, in_sems, out_sems
+):
     width = x_ref.shape[1]
     step = 256
     tiles = [slice(i, i + step) for i in range(0, width, step)]
     n = len(tiles)
-    copies = [pltpu.make_async_copy(x_hbm, x_ref, sems.at[0])]
+    ins = [pltpu.make_async_copy(x_hbm, x_ref, in_sems.at[0])]
     for i, (src, dst) in enumerate(((wk_hbm, wk_ref), (wv_hbm, wv_ref))):
         for j, part in enumerate(tiles):
-            copies.append(pltpu.make_async_copy(src.at[:, part], dst.at[:, part], sems.at[1 + i * n + j]))
-    for copy in copies:
+            ins.append(pltpu.make_async_copy(src.at[:, part], dst.at[:, part], in_sems.at[1 + i * n + j]))
+    for copy in ins:
         copy.start()
-    copies[0].wait()
+    outs = []
+
+    def put(src, dst):
+        copy = pltpu.make_async_copy(src, dst, out_sems.at[len(outs)])
+        copy.start()
+        outs.append(copy)
+
+    ins[0].wait()
+    put(x_ref.at[x_ref.shape[0] - b_hbm.shape[0] :], b_hbm)
     for j, part in enumerate(tiles):
-        copies[1 + j].wait()
+        ins[1 + j].wait()
         k = dot_nn(x_ref[...], wk_ref[:, part]).astype(BF16)
         k_ref[:, part] = k
+        put(k_ref.at[:, part], k_hbm.at[:, part])
         k = k.astype(F32)
         f_ref[:, part] = (k / (1.0 + jnp.exp(-k))).astype(BF16)
+        put(f_ref.at[:, part], f_hbm.at[:, part])
     for j, part in enumerate(tiles):
-        copies[1 + n + j].wait()
+        ins[1 + n + j].wait()
         turned = wv_ref[:, part].T
         wvt_ref[part, :] = turned
+        put(wvt_ref.at[part], wvt_hbm.at[part])
         vt_ref[part, :] = dot_nt(turned, x_ref[...]).astype(BF16)
+        put(vt_ref.at[part], vt_hbm.at[part])
         for h in range(part.start, part.stop, DL):
             head = slice(h, h + DL)
             s_ref[head, :] = dot_nn(vt_ref[head, :], f_ref[:, head]).astype(BF16)
-
-
-def within_kernel(f_ref, vt_ref, n_ref):
+    for copy in outs:
+        copy.wait()
+
+
+def add_within(f_ref, vt_ref, n_ref):
     rows = f_ref.shape[0]
     half = rows // 2
     upper = lax.broadcasted_iota(jnp.int32, (half, half), 0) <= lax.broadcasted_iota(
@@ -212,12 +229,15 @@
     lax.fori_loop(0, list_ref.shape[0], query, 0)
 
 
-def own_attention_kernel(size, list_ref, count_ref, pos_ref, k_ref, vt_ref, m_ref, l_ref, acc_ref, found_ref):
+def local_kernel(
+    size, list_ref, count_ref, pos_ref, k_ref, vt_ref, f_ref, m_ref, l_ref, acc_ref, n_ref, found_ref
+):
     queries = list_ref.shape[0]
     blocks = [pos_ref[0] * queries + kb for kb in range(queries)]
     attend_listed(
         True, size, blocks, list_ref, count_ref, found_ref, k_ref, k_ref, vt_ref, m_ref, l_ref, acc_ref
     )
+    add_within(f_ref, vt_ref, n_ref)
 
 
 def attend_halo(size, pieces, list_ref, count_ref, pos_ref, piece_refs, wk_ref, wvt_ref, q_ref, state, scratch):
@@ -278,7 +298,7 @@
     out_ref[...] = dot_nn(comb_ref[...], wo_ref[...]).astype(BF16)
 
 
-COSTLY = ("halo_b",)
+COSTLY = ()
 
 
 def call(
@@ -297,7 +317,10 @@
         kernel,
         name=name,
         in_specs=[SMEM] * smem + [pl.BlockSpec(memory_space=space)] * (len(ins) - smem),
-        out_specs=[pl.BlockSpec(memory_space=out_space)] * len(outs),
+        out_specs=[
+            pl.BlockSpec(memory_space=m)
+            for m in (out_space if isinstance(out_space, list) else [out_space] * len(outs))
+        ],
         out_shape=[jax.ShapeDtypeStruct(s, d) for s, d in outs],
         scratch_shapes=list(scratch),
         input_output_aliases=aliases or {},
@@ -355,71 +378,68 @@
             aliases={first + i: i for i in range(3)},
         )
 
-    cuts = [0, half * size, (half + 1) * size, rows]
+    cut = half * size
+    own = pltpu.with_memory_space_constraint(own, pltpu.HBM)
     (first_rows,) = call(
         cut_kernel,
         "cut",
         (own,),
-        [((cuts[1], width), BF16)],
+        [((cut, width), BF16)],
         scratch=(pltpu.SemaphoreType.DMA(()),),
-        limit=60 * MIB,
         space=pltpu.HBM,
-        out_space=pltpu.HBM,
     )
     near_a = swap(first_rows, 1)
-    keyed, features, values_t, state, value_t = call(
+    steps = width // 256
+    keyed, features, values_t, value_t, last_rows, state = call(
         own_kernel,
         "own",
-        (own, qk_weight, value_weight),
+        (own,) + tuple(pltpu.with_memory_space_constraint(w, pltpu.HBM) for w in (qk_weight, value_weight)),
         [
             ((rows, width), BF16),
             ((rows, width), BF16),
             ((width, rows), BF16),
+            ((width, width), BF16),
+            ((rows - cut, width), BF16),
             ((width, DL), BF16),
-            ((width, width), BF16),
         ],
         scratch=(
             pltpu.VMEM((rows, width), BF16),
             pltpu.VMEM((width, width), BF16),
             pltpu.VMEM((width, width), BF16),
-            pltpu.SemaphoreType.DMA((1 + 2 * (width // 256),)),
+            pltpu.VMEM((rows, width), BF16),
+            pltpu.VMEM((rows, width), BF16),
+            pltpu.VMEM((width, rows), BF16),
+            pltpu.VMEM((width, width), BF16),
+            pltpu.SemaphoreType.DMA((1 + 2 * steps,)),
+            pltpu.SemaphoreType.DMA((1 + 4 * steps,)),
         ),
-        limit=50 * MIB,
+        limit=56 * MIB,
         space=pltpu.HBM,
+        out_space=[pltpu.HBM] * 5 + [pltpu.VMEM],
     )
     heard = [swap(state, 1)]
-    rest = after(own, state)
-    near_b = swap(rest[cuts[1] : cuts[2]], 1)
-    near_c = swap(rest[cuts[2] :], 1)
-    far_c = across(rest[cuts[2] :])
+    near_b = swap(last_rows, 1)
+    far_b = across(last_rows)
     shapes = [((blocks, H // 2, 2 * size), F32)] * 2 + [((blocks, width, size), F32)]
-    softmax = call(
-        functools.partial(own_attention_kernel, size),
-        "own_attention",
-        tables + (after(keyed, near_a), values_t),
-        shapes,
+    *softmax, within = call(
+        functools.partial(local_kernel, size),
+        "local",
+        tables + tuple(pltpu.with_memory_space_constraint(a, pltpu.HBM) for a in (keyed, values_t, features)),
+        shapes + [((width, rows), F32)],
         smem=3,
         scratch=(pltpu.SMEM((blocks + 1,), jnp.int32),),
-
-    )
-    far_a = onward(near_a)
-    total = state + after(heard[0], softmax[0])
+    )
+    far_a = onward(after(near_a, within))
+    total = state + after(heard[0], within)
     heard.append(swap(total, 2))
-    (within,) = call(
-        within_kernel,
-        "within",
-        (after(features, near_a, total), values_t),
-        [((width, rows), F32)],
-    )
-    softmax = join_halo("halo_a", softmax, [(True, 0)], [after(near_a, within)])
-    far_b = onward(after(near_b, softmax[0]))
+    softmax = join_halo("halo_a", softmax, [(True, 0)], [after(near_a, within, total)])
     stride = 4
     while stride < count:
         total = total + after(heard[-1], softmax[0])
         heard.append(swap(total, stride))
         stride *= 2
     softmax = join_halo(
-        "halo_b", softmax, [(True, half), (False, 0)], [after(near_b, total), far_a]
+        "halo_b", softmax, [(False, 0), (True, half)], [after(far_a, total), near_b]
     )
     (linear,) = call(
         functools.partial(linear_kernel, len(heard)),
@@ -428,9 +448,8 @@
         [((width, rows), F32)],
         smem=1,
     )
-    softmax = join_halo("halo_c", softmax, [(False, half)], [after(far_b, linear)])
-    pieces = [(True, half + 1), (False, half + 1)]
-    arrays = (near_c, far_c)
+    pieces = [(False, half)]
+    arrays = (after(far_b, linear),)
     ins = tables + arrays + (qk_weight, value_t, keyed, linear, out_weight) + tuple(softmax)
     first = len(ins) - 3
     update, *_ = call(

time: 83.9 us -> 62.5 us (0.74)
  the two profiles are of different devices: /device:TPU:6 before, /device:TPU:0 now
where the time goes in v2:
time: 62.5 us; the launch traced here: 62.1 us
  Pallas kernels  35.2 us (56%)
  waiting for transfers between devices  13.2 us (21%)
  starting transfers between devices  10.8 us (17%)
  local copies, waits for them, and re-layouts  1.63 us (3%)
  other arithmetic  1.09 us (2%)
    pallas_call x7, Pallas kernels, call(): pl.pallas_call(kernel, name=name, in_specs=[SMEM] * smem + [pl.BlockSpec(...  35.2 us
    ppermute x5, waiting for transfers between devices, swap(): return lax.ppermute(value, 'seq', [(i, i ^ bit) for i in range(count)])  13.1 us
    ppermute x5, starting transfers between devices, swap(): return lax.ppermute(value, 'seq', [(i, i ^ bit) for i in range(count)])  8.62 us
    unnamed x18, local copies, waits for them, and re-layouts  1.63 us
    ppermute x1, starting transfers between devices, onward(): return lax.ppermute(value, 'seq', pairs)  1.32 us
  transfers between devices with their start and end apart: 7, of which 2 were waited for; matrix products, arithmetic and copies ran while one was open for 2% of the time, Pallas kernels for 46%

profile of v2, /device:TPU:0, one launch (start us, length us, event | category | flops | bytes accessed | tf_op | source)
XLA Modules:
  0.0 62.1 jit_solution(10356105191796547540)
XLA Ops:
  0.0 1.8 %cut.1 = bf16[256,1024]{1,0:T(8,128)(2,1)} custom-call(bf16[512,1024]{1,0:T(8,128)(2,1)} %bitcast.13), custom_call_target="tpu_custom_call" | custom-call | flops 1 | bytes 1000 | tf_op jit(solution)/shard_map/cut/pallas_call | solution.py:316
  1.9 0.0 copy-start.6
  1.9 0.0 copy-start.7
  1.9 3.0 %collective-permute-start.1 = (bf16[256,1024]{1,0:T(8,128)(2,1)}, bf16[256,1024]{1,0:T(8,128)(2,1)}, u32[]{:S(2)}, u32[]{:S(2)}) collective-permute-start(bf16[256,1024]{1,0:T(8,128)(2,1)} %cut.1), channel_id=1, source_target_pairs={{0,2},{2,0},{4,6},{6,4},{8,10},{10,8},{12,14},{14,12},{1,3},{3,1},... | collective-permute-start | bytes 1572872 | tf_op jit(solution)/shard_map/ppermute | solution.py:350
  4.9 8.3 %own.1 = (bf16[512,1024]{1,0:T(8,128)(2,1)}, bf16[512,1024]{1,0:T(8,128)(2,1)}, bf16[1024,512]{1,0:T(8,128)(2,1)}, bf16[1024,1024]{1,0:T(8,128)(2,1)}, bf16[256,...) custom-call(bf16[512,1024]{1,0:T(8,128)(2,1)} %bitcast.14, bf16[1024,1024]{1,0:T(8,128)(2,1)} %refs_1_.3, ...), custom_call_target="tpu_custom_call" | custom-call | flops 1 | bytes 1000 | tf_op jit(solution)/shard_map/own/pallas_call | solution.py:316
  13.2 0.0 copy-start
  13.2 0.0 copy-start.3
  13.2 0.1 collective-permute-start.3
  13.3 2.0 %collective-permute-start.5 = (bf16[256,1024]{1,0:T(8,128)(2,1)}, bf16[256,1024]{1,0:T(8,128)(2,1)}, u32[]{:S(2)}, u32[]{:S(2)}) collective-permute-start(bf16[256,1024]{1,0:T(8,128)(2,1)} %get-tuple-element.29), channel_id=1, source_target_pairs={{0,2},{2,0},{4,6},{6,4},{8,10},{10,8},{12,14},{14,12},{1,3},{3,1},... | collective-permute-start | bytes 1572872 | tf_op jit(solution)/shard_map/ppermute | solution.py:350
  15.3 10.4 %local.1 = (f32[4,8,256]{2,1,0:T(8,128)S(1)}, f32[4,8,256]{2,1,0:T(8,128)S(1)}, f32[4,1024,128]{2,1,0:T(8,128)S(1)}, f32[1024,512]{1,0:T(8,128)S(1)}) custom-call(s32[4,4]{1,0:T(4,128)S(1)} %bitcast.5, s32[4]{0:T(128)S(1)} %bitcast.9, s32[1]{0:T(128)} %bitcast.2.pos_ref, bf16[512,1024]{1,0:T(8,128)(2,1)} %get-tuple-element.31.k_ref.refs_3_.refs_4_, ...), custom_call_target="tpu_custom_call" | custom-call | flops 1 | bytes 1000 | tf_op jit(solution)/shard_map/local/pallas_call | solution.py:316
  25.7 0.0 collective-permute-done.1.refs_0_
  25.7 1.3 %collective-permute-start.2 = (bf16[256,1024]{1,0:T(8,128)(2,1)}, bf16[256,1024]{1,0:T(8,128)(2,1)S(1)}, u32[]{:S(2)}, u32[]{:S(2)}) collective-permute-start(bf16[256,1024]{1,0:T(8,128)(2,1)} %collective-permute-done.1.refs_0_), channel_id=1, source_target_pairs={{0,4},{4,8},{8,12},{6,2},{10,6},{14,10},{1,5},{5,9},{9,13},{7,3},{... | collective-permute-start | bytes 1572872 | tf_op jit(solution)/shard_map/ppermute | solution.py:354
  27.0 0.0 collective-permute-done.3.refs_0_
  27.0 1.0 %add.6 = bf16[1024,128]{1,0:T(8,128)(2,1)S(1)} add(bf16[1024,128]{1,0:T(8,128)(2,1)} %get-tuple-element.35, bf16[1024,128]{1,0:T(8,128)(2,1)S(1)} %collective-permute-done.3.refs_0_) | non-fusion elementwise | flops 131072 | bytes 786432 | tf_op jit(solution)/shard_map/add | solution.py:433
  28.1 1.2 %collective-permute-start.4 = (bf16[1024,128]{1,0:T(8,128)(2,1)S(1)}, bf16[1024,128]{1,0:T(8,128)(2,1)S(1)}, u32[]{:S(2)}, u32[]{:S(2)}) collective-permute-start(bf16[1024,128]{1,0:T(8,128)(2,1)S(1)} %add.6), channel_id=1, source_target_pairs={{0,4},{2,6},{4,0},{6,2},{8,12},{10,14},{12,8},{14,10},{1,5},{3,7},... | collective-permute-start | bytes 786440 | tf_op jit(solution)/shard_map/ppermute | solution.py:350
  29.2 0.9 %collective-permute-start = (bf16[256,1024]{1,0:T(8,128)(2,1)S(1)}, bf16[256,1024]{1,0:T(8,128)(2,1)S(1)}, u32[]{:S(2)}, u32[]{:S(2)}) collective-permute-start(bf16[256,1024]{1,0:T(8,128)(2,1)S(1)} %copy-done.8), channel_id=1, source_target_pairs={{2,4},{6,8},{10,12},{4,2},{8,6},{12,10},{3,5},{7,9},{11,13},{5,3},... | collective-permute-start | bytes 1572872 | tf_op jit(solution)/shard_map/ppermute | solution.py:358
  30.1 0.0 copy-done
  30.1 0.0 copy-done.3
  30.1 0.0 copy-start.1
  30.1 1.6 %copy-done.1 = bf16[1024,1024]{1,0:T(8,128)(2,1)S(1)} copy-done((bf16[1024,1024]{1,0:T(8,128)(2,1)S(1)}, bf16[1024,1024]{1,0:T(8,128)(2,1)}, u32[]{:S(2)}) %copy-start.1) | copy-done | bytes 2097176
  31.7 4.8 %halo_a.1 = (f32[4,8,256]{2,1,0:T(8,128)S(1)}, f32[4,8,256]{2,1,0:T(8,128)S(1)}, f32[4,1024,128]{2,1,0:T(8,128)S(1)}) custom-call(s32[4,4]{1,0:T(4,128)S(1)} %bitcast.6, s32[4]{0:T(128)S(1)} %bitcast.10, s32[1]{0:T(128)} %bitcast.2.pos_ref, ...), custom_call_target="tpu_custom_call", output_to_operand_aliasing={{0}: (7, {}), {1}: (8, {}), {2}: (9, {})} | custom-call | flops 1 | bytes 1000 | tf_op jit(solution)/shard_map/halo_a/pallas_call | solution.py:316
  36.6 6.5 %collective-permute-done.4.refs_1_ = bf16[1024,128]{1,0:T(8,128)(2,1)S(1)} collective-permute-done((bf16[1024,128]{1,0:T(8,128)(2,1)S(1)}, bf16[1024,128]{1,0:T(8,128)(2,1)S(1)}, u32[]{:S(2)}, u32[]{:S(2)}) %collective-permute-start.4) | collective-permute-done | bytes 262176 | tf_op jit(solution)/shard_map/ppermute | solution.py:350
  43.0 0.1 add.7
  43.1 2.3 %collective-permute-start.6 = (bf16[1024,128]{1,0:T(8,128)(2,1)S(1)}, bf16[1024,128]{1,0:T(8,128)(2,1)S(1)}, u32[]{:S(2)}, u32[]{:S(2)}) collective-permute-start(bf16[1024,128]{1,0:T(8,128)(2,1)S(1)} %add.7), channel_id=1, source_target_pairs={{0,8},{2,10},{4,12},{6,14},{8,0},{10,2},{12,4},{14,6},{1,9},{3,11}... | collective-permute-start | bytes 786440 | tf_op jit(solution)/shard_map/ppermute | solution.py:350
  45.4 0.0 collective-permute-done.2.refs_0_
  45.4 0.0 collective-permute-done.5.refs_1_
  45.4 3.7 %halo_b.1 = (f32[4,8,256]{2,1,0:T(8,128)S(1)}, f32[4,8,256]{2,1,0:T(8,128)S(1)}, f32[4,1024,128]{2,1,0:T(8,128)S(1)}) custom-call(s32[4,4]{1,0:T(4,128)S(1)} %bitcast.7, s32[4]{0:T(128)S(1)} %bitcast.11, s32[1]{0:T(128)} %bitcast.2.pos_ref, ...), custom_call_target="tpu_custom_call", output_to_operand_aliasing={{0}: (8, {}), {1}: (9, {}), {2}: (10, {})} | custom-call | flops 1 | bytes 1000 | tf_op jit(solution)/shard_map/halo_b/pallas_call | solution.py:316
  49.2 0.0 copy-start.5
  49.2 6.7 %collective-permute-done.6.refs_2_ = bf16[1024,128]{1,0:T(8,128)(2,1)S(1)} collective-permute-done((bf16[1024,128]{1,0:T(8,128)(2,1)S(1)}, bf16[1024,128]{1,0:T(8,128)(2,1)S(1)}, u32[]{:S(2)}, u32[]{:S(2)}) %collective-permute-start.6) | collective-permute-done | bytes 262176 | tf_op jit(solution)/shard_map/ppermute | solution.py:350
  55.9 1.2 %linear.1.refs_4_ = f32[1024,512]{1,0:T(8,128)S(1)} custom-call(s32[1]{0:T(128)} %bitcast.2.pos_ref, bf16[512,1024]{1,0:T(8,128)(2,1)S(1)} %copy-done.4, f32[1024,512]{1,0:T(8,128)S(1)} %get-tuple-element.33.n_ref, bf16[1024,128]{1,0:T(8,128)(2,1)S(1)} %collective-permute-done.3.refs_0_, bf16[1024,128]{1,0:T(8,128)(2,1)S(1)} %collective-permute-done.4.refs_1_, ...), custom_call_target="tpu_custom_call" | custom-call | flops 1 | bytes 1000 | tf_op jit(solution)/shard_map/linear/pallas_call | solution.py:316
  57.1 0.0 collective-permute-done.refs_0_
  57.2 4.9 %final.1 = (bf16[512,1024]{1,0:T(8,128)(2,1)}, f32[4,8,256]{2,1,0:T(8,128)S(1)}, f32[4,8,256]{2,1,0:T(8,128)S(1)}, f32[4,1024,128]{2,1,0:T(8,128)S(1)}) custom-call(s32[4,4]{1,0:T(4,128)S(1)} %bitcast.8, s32[4]{0:T(128)S(1)} %bitcast.12, s32[1]{0:T(128)} %bitcast.2.pos_ref, ...), custom_call_target="tpu_custom_call", output_to_operand_aliasing={{1}: (9, {}), {2}: (10, {}), {3}: (11, {})} | custom-call | flops 1 | bytes 1000 | tf_op jit(solution)/shard_map/final/pallas_call | solution.py:316
  (9 shorter events, 0.0 us)
Async XLA Ops:
  1.9 13.5 %copy-start.6 = (s32[1,4,4]{2,1,0:T(4,128)S(1)}, s32[1,4,4]{2,1,0:T(4,128)}, u32[]{:S(2)}) copy-start(s32[1,4,4]{2,1,0:T(4,128)} %param.10) | copy-start | bytes 196
  1.9 13.4 %copy-start.7 = (s32[1,4]{1,0:T(1,128)S(1)}, s32[1,4]{1,0:T(1,128)}, u32[]{:S(2)}) copy-start(s32[1,4]{1,0:T(1,128)} %param.11) | copy-start | bytes 52
  1.9 23.8 %collective-permute-start.1 = (bf16[256,1024]{1,0:T(8,128)(2,1)}, bf16[256,1024]{1,0:T(8,128)(2,1)}, u32[]{:S(2)}, u32[]{:S(2)}) collective-permute-start(bf16[256,1024]{1,0:T(8,128)(2,1)} %cut.1), channel_id=1, source_target_pairs={{0,2},{2,0},{4,6},{6,4},{8,10},{10,8},{12,14},{14,12},{1,3},{3,1},... | collective-permute-start | bytes 1572872 | tf_op jit(solution)/shard_map/ppermute | solution.py:350
  13.2 16.9 %copy-start = (bf16[1024,1024]{1,0:T(8,128)(2,1)S(1)}, bf16[1024,1024]{1,0:T(8,128)(2,1)}, u32[]{:S(2)}) copy-start(bf16[1024,1024]{1,0:T(8,128)(2,1)} %refs_1_.3) | copy-start | bytes 6291460
  13.2 16.9 %copy-start.3 = (bf16[512,1024]{1,0:T(8,128)(2,1)S(1)}, bf16[512,1024]{1,0:T(8,128)(2,1)}, u32[]{:S(2)}) copy-start(bf16[512,1024]{1,0:T(8,128)(2,1)} %get-tuple-element.31.k_ref.refs_3_.refs_4_) | copy-start | bytes 3145732
  13.2 13.8 %collective-permute-start.3 = (bf16[1024,128]{1,0:T(8,128)(2,1)}, bf16[1024,128]{1,0:T(8,128)(2,1)S(1)}, u32[]{:S(2)}, u32[]{:S(2)}) collective-permute-start(bf16[1024,128]{1,0:T(8,128)(2,1)} %get-tuple-element.35), channel_id=1, source_target_pairs={{0,2},{2,0},{4,6},{6,4},{8,10},{10,8},{12,14},{14,12},{1,3},{3,1},... | collective-permute-start | bytes 786440 | tf_op jit(solution)/shard_map/ppermute | solution.py:350
  13.3 32.1 %collective-permute-start.5 = (bf16[256,1024]{1,0:T(8,128)(2,1)}, bf16[256,1024]{1,0:T(8,128)(2,1)}, u32[]{:S(2)}, u32[]{:S(2)}) collective-permute-start(bf16[256,1024]{1,0:T(8,128)(2,1)} %get-tuple-element.29), channel_id=1, source_target_pairs={{0,2},{2,0},{4,6},{6,4},{8,10},{10,8},{12,14},{14,12},{1,3},{3,1},... | collective-permute-start | bytes 1572872 | tf_op jit(solution)/shard_map/ppermute | solution.py:350
  15.3 13.9 %copy-start.8 = (bf16[256,1024]{1,0:T(8,128)(2,1)S(1)}, bf16[256,1024]{1,0:T(8,128)(2,1)}, u32[]{:S(2)}) copy-start(bf16[256,1024]{1,0:T(8,128)(2,1)} %get-tuple-element.29) | copy-start | bytes 1572868
  25.7 19.7 %collective-permute-start.2 = (bf16[256,1024]{1,0:T(8,128)(2,1)}, bf16[256,1024]{1,0:T(8,128)(2,1)S(1)}, u32[]{:S(2)}, u32[]{:S(2)}) collective-permute-start(bf16[256,1024]{1,0:T(8,128)(2,1)} %collective-permute-done.1.refs_0_), channel_id=1, source_target_pairs={{0,4},{4,8},{8,12},{6,2},{10,6},{14,10},{1,5},{5,9},{9,13},{7,3},{... | collective-permute-start | bytes 1572872 | tf_op jit(solution)/shard_map/ppermute | solution.py:354
  28.1 15.0 %collective-permute-start.4 = (bf16[1024,128]{1,0:T(8,128)(2,1)S(1)}, bf16[1024,128]{1,0:T(8,128)(2,1)S(1)}, u32[]{:S(2)}, u32[]{:S(2)}) collective-permute-start(bf16[1024,128]{1,0:T(8,128)(2,1)S(1)} %add.6), channel_id=1, source_target_pairs={{0,4},{2,6},{4,0},{6,2},{8,12},{10,14},{12,8},{14,10},{1,5},{3,7},... | collective-permute-start | bytes 786440 | tf_op jit(solution)/shard_map/ppermute | solution.py:350
  29.2 27.9 %collective-permute-start = (bf16[256,1024]{1,0:T(8,128)(2,1)S(1)}, bf16[256,1024]{1,0:T(8,128)(2,1)S(1)}, u32[]{:S(2)}, u32[]{:S(2)}) collective-permute-start(bf16[256,1024]{1,0:T(8,128)(2,1)S(1)} %copy-done.8), channel_id=1, source_target_pairs={{2,4},{6,8},{10,12},{4,2},{8,6},{12,10},{3,5},{7,9},{11,13},{5,3},... | collective-permute-start | bytes 1572872 | tf_op jit(solution)/shard_map/ppermute | solution.py:358
  30.1 1.6 %copy-start.1 = (bf16[1024,1024]{1,0:T(8,128)(2,1)S(1)}, bf16[1024,1024]{1,0:T(8,128)(2,1)}, u32[]{:S(2)}) copy-start(bf16[1024,1024]{1,0:T(8,128)(2,1)} %get-tuple-element.38.refs_2_.refs_3_) | copy-start | bytes 6291460
  43.1 12.8 %collective-permute-start.6 = (bf16[1024,128]{1,0:T(8,128)(2,1)S(1)}, bf16[1024,128]{1,0:T(8,128)(2,1)S(1)}, u32[]{:S(2)}, u32[]{:S(2)}) collective-permute-start(bf16[1024,128]{1,0:T(8,128)(2,1)S(1)} %add.7), channel_id=1, source_target_pairs={{0,8},{2,10},{4,12},{6,14},{8,0},{10,2},{12,4},{14,6},{1,9},{3,11}... | collective-permute-start | bytes 786440 | tf_op jit(solution)/shard_map/ppermute | solution.py:350
  45.4 10.4 %copy-start.4 = (bf16[512,1024]{1,0:T(8,128)(2,1)S(1)}, bf16[512,1024]{1,0:T(8,128)(2,1)}, u32[]{:S(2)}) copy-start(bf16[512,1024]{1,0:T(8,128)(2,1)} %get-tuple-element.48.f_ref) | copy-start | bytes 3145732
  49.2 8.0 %copy-start.2 = (bf16[1024,1024]{1,0:T(8,128)(2,1)S(1)}, bf16[1024,1024]{1,0:T(8,128)(2,1)}, u32[]{:S(2)}) copy-start(bf16[1024,1024]{1,0:T(8,128)(2,1)} %get-tuple-element.38.refs_2_.refs_3_) | copy-start | bytes 6291460
  49.2 8.0 %copy-start.5 = (bf16[1024,1024]{1,0:T(8,128)(2,1)S(1)}, bf16[1024,1024]{1,0:T(8,128)(2,1)}, u32[]{:S(2)}) copy-start(bf16[1024,1024]{1,0:T(8,128)(2,1)} %refs_5_.1) | copy-start | bytes 6291460

commit v3 on v2

--- a/solution.py
+++ b/solution.py
@@ -30,9 +30,17 @@
     return pl.ds(pl.multiple_of(i * size, size), size)
 
 
-def project(x, wk_ref, wvt_ref, k_ref, vt_ref):
+def silu(k):
+    k = k.astype(F32)
+    return (k / (1.0 + jnp.exp(-k))).astype(BF16)
+
+
+def project(x, wk_ref, wv_ref, k_ref, vt_ref):
     k_ref[...] = dot_nn(x, wk_ref[...]).astype(BF16)
-    vt_ref[...] = dot_nt(wvt_ref[...], x).astype(BF16)
+    step = 256
+    for i in range(0, wv_ref.shape[1], step):
+        part = slice(i, i + step)
+        vt_ref[part, :] = dot_nn(x, wv_ref[:, part]).astype(BF16).T
 
 
 def cut_kernel(x_hbm, a_ref, sem):
@@ -42,18 +50,17 @@
 
 
 def own_kernel(
-    x_hbm, wk_hbm, wv_hbm, k_hbm, f_hbm, vt_hbm, wvt_hbm, b_hbm, s_ref, x_ref, wk_ref, wv_ref, k_ref, f_ref, vt_ref,
-    wvt_ref, in_sems, out_sems
+    x_hbm, wk_hbm, wv_hbm, k_hbm, vt_hbm, b_hbm, s_ref, x_ref, wk_ref, wv_ref, k_ref, vt_ref, in_sems, out_sems
 ):
     width = x_ref.shape[1]
     step = 256
     tiles = [slice(i, i + step) for i in range(0, width, step)]
     n = len(tiles)
     ins = [pltpu.make_async_copy(x_hbm, x_ref, in_sems.at[0])]
-    for i, (src, dst) in enumerate(((wk_hbm, wk_ref), (wv_hbm, wv_ref))):
-        for j, part in enumerate(tiles):
-            ins.append(pltpu.make_async_copy(src.at[:, part], dst.at[:, part], in_sems.at[1 + i * n + j]))
-    for copy in ins:
+    for j, part in enumerate(tiles):
+        for i, (src, dst) in enumerate(((wk_hbm, wk_ref), (wv_hbm, wv_ref))):
+            ins.append(pltpu.make_async_copy(src.at[:, part], dst.at[:, part], in_sems.at[1 + 2 * j + i]))
+    for copy in ins[:3]:
         copy.start()
     outs = []
 
@@ -65,29 +72,25 @@
     ins[0].wait()
     put(x_ref.at[x_ref.shape[0] - b_hbm.shape[0] :], b_hbm)
     for j, part in enumerate(tiles):
-        ins[1 + j].wait()
+        for copy in ins[3 + 2 * j : 5 + 2 * j]:
+            copy.start()
+        ins[1 + 2 * j].wait()
         k = dot_nn(x_ref[...], wk_ref[:, part]).astype(BF16)
         k_ref[:, part] = k
         put(k_ref.at[:, part], k_hbm.at[:, part])
-        k = k.astype(F32)
-        f_ref[:, part] = (k / (1.0 + jnp.exp(-k))).astype(BF16)
-        put(f_ref.at[:, part], f_hbm.at[:, part])
-    for j, part in enumerate(tiles):
-        ins[1 + n + j].wait()
-        turned = wv_ref[:, part].T
-        wvt_ref[part, :] = turned
-        put(wvt_ref.at[part], wvt_hbm.at[part])
-        vt_ref[part, :] = dot_nt(turned, x_ref[...]).astype(BF16)
+        f = silu(k)
+        ins[2 + 2 * j].wait()
+        vt_ref[part, :] = dot_nn(x_ref[...], wv_ref[:, part]).astype(BF16).T
         put(vt_ref.at[part], vt_hbm.at[part])
-        for h in range(part.start, part.stop, DL):
-            head = slice(h, h + DL)
-            s_ref[head, :] = dot_nn(vt_ref[head, :], f_ref[:, head]).astype(BF16)
+        for h in range(0, step, DL):
+            head = slice(part.start + h, part.start + h + DL)
+            s_ref[head, :] = dot_nn(vt_ref[head, :], f[:, h : h + DL]).astype(BF16)
     for copy in outs:
         copy.wait()
 
 
-def add_within(f_ref, vt_ref, n_ref):
-    rows = f_ref.shape[0]
+def within_kernel(k_ref, vt_ref, n_ref):
+    rows = k_ref.shape[0]
     half = rows // 2
     upper = lax.broadcasted_iota(jnp.int32, (half, half), 0) <= lax.broadcasted_iota(
         jnp.int32, (half, half), 1
@@ -95,8 +98,8 @@
 
     def head(h, carry):
         cols = tile(h, DL)
-        f0 = f_ref[:half, cols]
-        f1 = f_ref[half:, cols]
+        f0 = silu(k_ref[:half, cols])
+        f1 = silu(k_ref[half:, cols])
         v0 = vt_ref[cols, :half]
         v1 = vt_ref[cols, half:]
         a00 = jnp.where(upper, dot_nt(f0, f0), 0.0).astype(BF16)
@@ -109,15 +112,29 @@
     lax.fori_loop(0, HL, head, 0, unroll=2)
 
 
-def linear_kernel(stages, pos_ref, f_ref, n_ref, *refs):
-    heard = refs[:stages]
-    o_ref = refs[stages]
-    bits = [((pos_ref[0] >> k) & 1).astype(F32) for k in range(stages)]
+def set_bits(pos_ref, count):
+    return [((pos_ref[0] >> (k + 1)) & 1).astype(F32) for k in range(count)]
+
+
+def carry_kernel(stages, pos_ref, s_ref, *refs):
+    bits = set_bits(pos_ref, stages)
+    first = 1.0 - (pos_ref[0] & 1).astype(F32)
+    total = s_ref[...].astype(F32) * first
+    for ref, bit in zip(refs, bits):
+        total = total + ref[...].astype(F32) * bit
+    refs[stages][...] = total.astype(BF16)
+
+
+def linear_kernel(stages, pos_ref, k_ref, n_ref, *refs):
+    heard, message_ref, o_ref = refs[:stages], refs[stages], refs[stages + 1]
+    bits = set_bits(pos_ref, stages)
 
     def head(h, carry):
         cols = tile(h, DL)
-        before = sum(ref[cols, :].astype(F32) * bit for ref, bit in zip(heard, bits)).astype(BF16)
-        n = n_ref[cols, :] + dot_nt(before, f_ref[:, cols])
+        before = message_ref[cols, :].astype(F32)
+        for ref, bit in zip(heard, bits):
+            before = before + ref[cols, :].astype(F32) * bit
+        n = n_ref[cols, :] + dot_nt(before.astype(BF16), silu(k_ref[:, cols]))
         mean = jnp.sum(n * n, axis=0, keepdims=True) * (1.0 / DL)
         o_ref[cols, :] = n * lax.rsqrt(mean + 1e-06)
         return carry
@@ -229,18 +246,15 @@
     lax.fori_loop(0, list_ref.shape[0], query, 0)
 
 
-def local_kernel(
-    size, list_ref, count_ref, pos_ref, k_ref, vt_ref, f_ref, m_ref, l_ref, acc_ref, n_ref, found_ref
-):
+def own_attention_kernel(size, list_ref, count_ref, pos_ref, k_ref, vt_ref, m_ref, l_ref, acc_ref, found_ref):
     queries = list_ref.shape[0]
     blocks = [pos_ref[0] * queries + kb for kb in range(queries)]
     attend_listed(
         True, size, blocks, list_ref, count_ref, found_ref, k_ref, k_ref, vt_ref, m_ref, l_ref, acc_ref
     )
-    add_within(f_ref, vt_ref, n_ref)
-
-
-def attend_halo(size, pieces, list_ref, count_ref, pos_ref, piece_refs, wk_ref, wvt_ref, q_ref, state, scratch):
+
+
+def attend_halo(size, pieces, list_ref, count_ref, pos_ref, piece_refs, wk_ref, wv_ref, q_ref, state, scratch):
     found_ref, x_ref, k_ref, vt_ref = scratch
     queries = list_ref.shape[0]
     pos = pos_ref[0]
@@ -253,7 +267,7 @@
         row += rows
         run = pos + step if near else pos - step
         blocks += [run * queries + first + i for i in range(rows // size)]
-    project(x_ref[...], wk_ref, wvt_ref, k_ref, vt_ref)
+    project(x_ref[...], wk_ref, wv_ref, k_ref, vt_ref)
     attend_listed(
         False, size, blocks, list_ref, count_ref, found_ref, q_ref, k_ref, vt_ref, *state
     )
@@ -261,15 +275,15 @@
 
 def halo_kernel(size, pieces, list_ref, count_ref, pos_ref, *refs):
     n = len(pieces)
-    wk_ref, wvt_ref, q_ref = refs[n : n + 3]
+    wk_ref, wv_ref, q_ref = refs[n : n + 3]
     attend_halo(
-        size, pieces, list_ref, count_ref, pos_ref, refs[:n], wk_ref, wvt_ref, q_ref, refs[n + 6 : n + 9], refs[n + 9 :]
+        size, pieces, list_ref, count_ref, pos_ref, refs[:n], wk_ref, wv_ref, q_ref, refs[n + 6 : n + 9], refs[n + 9 :]
     )
 
 
 def final_kernel(size, pieces, list_ref, count_ref, pos_ref, *refs):
     n = len(pieces)
-    wk_ref, wvt_ref, q_ref, lin_ref, wo_ref = refs[n : n + 5]
+    wk_ref, wv_ref, q_ref, lin_ref, wo_ref = refs[n : n + 5]
     out_ref, m_ref, l_ref, acc_ref, comb_ref = refs[n + 8 : n + 13]
     attend_halo(
         size,
@@ -279,7 +293,7 @@
         pos_ref,
         refs[:n],
         wk_ref,
-        wvt_ref,
+        wv_ref,
         q_ref,
         (m_ref, l_ref, acc_ref),
         refs[n + 13 :],
@@ -298,7 +312,7 @@
     out_ref[...] = dot_nn(comb_ref[...], wo_ref[...]).astype(BF16)
 
 
-COSTLY = ()
+COSTLY = ("within",)
 
 
 def call(
@@ -366,7 +380,7 @@
         )
 
     def join_halo(name, softmax, pieces, arrays):
-        ins = tables + tuple(arrays) + (qk_weight, value_t, keyed) + tuple(softmax)
+        ins = tables + tuple(arrays) + (qk_weight, value_weight, keyed) + tuple(softmax)
         first = len(ins) - 3
         return call(
             functools.partial(halo_kernel, size, pieces),
@@ -379,26 +393,24 @@
         )
 
     cut = half * size
-    own = pltpu.with_memory_space_constraint(own, pltpu.HBM)
+    in_hbm = functools.partial(pltpu.with_memory_space_constraint, memory_space=pltpu.HBM)
     (first_rows,) = call(
         cut_kernel,
         "cut",
-        (own,),
+        (in_hbm(own),),
         [((cut, width), BF16)],
         scratch=(pltpu.SemaphoreType.DMA(()),),
         space=pltpu.HBM,
     )
     near_a = swap(first_rows, 1)
     steps = width // 256
-    keyed, features, values_t, value_t, last_rows, state = call(
+    keyed, values_t, last_rows, state = call(
         own_kernel,
         "own",
-        (own,) + tuple(pltpu.with_memory_space_constraint(w, pltpu.HBM) for w in (qk_weight, value_weight)),
+        (in_hbm(after(own, first_rows)), in_hbm(qk_weight), in_hbm(value_weight)),
         [
             ((rows, width), BF16),
-            ((rows, width), BF16),
             ((width, rows), BF16),
-            ((width, width), BF16),
             ((rows - cut, width), BF16),
             ((width, DL), BF16),
         ],
@@ -407,50 +419,60 @@
             pltpu.VMEM((width, width), BF16),
             pltpu.VMEM((width, width), BF16),
             pltpu.VMEM((rows, width), BF16),
-            pltpu.VMEM((rows, width), BF16),
             pltpu.VMEM((width, rows), BF16),
-            pltpu.VMEM((width, width), BF16),
             pltpu.SemaphoreType.DMA((1 + 2 * steps,)),
-            pltpu.SemaphoreType.DMA((1 + 4 * steps,)),
+            pltpu.SemaphoreType.DMA((1 + 2 * steps,)),
         ),
         limit=56 * MIB,
         space=pltpu.HBM,
-        out_space=[pltpu.HBM] * 5 + [pltpu.VMEM],
-    )
-    heard = [swap(state, 1)]
-    near_b = swap(last_rows, 1)
+        out_space=[pltpu.HBM] * 3 + [pltpu.VMEM],
+    )
     far_b = across(last_rows)
+    heard = [swap(state, 2)]
     shapes = [((blocks, H // 2, 2 * size), F32)] * 2 + [((blocks, width, size), F32)]
-    *softmax, within = call(
-        functools.partial(local_kernel, size),
-        "local",
-        tables + tuple(pltpu.with_memory_space_constraint(a, pltpu.HBM) for a in (keyed, values_t, features)),
-        shapes + [((width, rows), F32)],
+    softmax = call(
+        functools.partial(own_attention_kernel, size),
+        "own_attention",
+        tables + (in_hbm(keyed), in_hbm(values_t)),
+        shapes,
         smem=3,
         scratch=(pltpu.SMEM((blocks + 1,), jnp.int32),),
     )
-    far_a = onward(after(near_a, within))
-    total = state + after(heard[0], within)
-    heard.append(swap(total, 2))
-    softmax = join_halo("halo_a", softmax, [(True, 0)], [after(near_a, within, total)])
+    total = state
     stride = 4
     while stride < count:
         total = total + after(heard[-1], softmax[0])
         heard.append(swap(total, stride))
         stride *= 2
-    softmax = join_halo(
-        "halo_b", softmax, [(False, 0), (True, half)], [after(far_a, total), near_b]
-    )
+    far_a = onward(after(near_a, total))
+    near_b = swap(after(last_rows, near_a), 1)
+    (within,) = call(
+        within_kernel,
+        "within",
+        (after(in_hbm(keyed), softmax[0], near_a), in_hbm(values_t)),
+        [((width, rows), F32)],
+    )
+    softmax = join_halo("halo_a", softmax, [(True, 0)], [after(near_a, within)])
+    (message,) = call(
+        functools.partial(carry_kernel, len(heard)),
+        "carry",
+        (position, after(state, softmax[0])) + tuple(heard),
+        [((width, DL), BF16)],
+        smem=1,
+    )
+    message = swap(message, 1)
+    softmax = join_halo("halo_b", softmax, [(False, half)], [after(far_b, heard[-1], softmax[0])])
+    softmax = join_halo("halo_c", softmax, [(False, 0)], [after(far_a, softmax[0])])
     (linear,) = call(
         functools.partial(linear_kernel, len(heard)),
         "linear",
-        (position, after(features, softmax[0]), within) + tuple(heard),
+        (position, after(keyed, softmax[0]), within) + tuple(heard) + (message,),
         [((width, rows), F32)],
         smem=1,
     )
-    pieces = [(False, half)]
-    arrays = (after(far_b, linear),)
-    ins = tables + arrays + (qk_weight, value_t, keyed, linear, out_weight) + tuple(softmax)
+    pieces = [(True, half)]
+    arrays = (after(near_b, linear),)
+    ins = tables + arrays + (qk_weight, value_weight, keyed, linear, out_weight) + tuple(softmax)
     first = len(ins) - 3
     update, *_ = call(
         functools.partial(final_kernel, size, pieces),

time: 62.5 us -> 57.8 us (0.925)
  the two profiles are of different devices: /device:TPU:0 before, /device:TPU:14 now
where the time goes in v3:
time: 57.8 us; the launch traced here: 56.8 us
  Pallas kernels  36.4 us (63%)
  starting transfers between devices  11.8 us (20%)
  waiting for transfers between devices  8.17 us (14%)
    pallas_call x10, Pallas kernels, call(): pl.pallas_call(kernel, name=name, in_specs=[SMEM] * smem + [pl.BlockSpec(...  36.4 us
    ppermute x1, starting transfers between devices, across(): lax.ppermute(value, 'seq', [(i, i + 1) for i in odd] + [(i + 1, i) for i...  5.56 us
    ppermute x5, waiting for transfers between devices, swap(): return lax.ppermute(value, 'seq', [(i, i ^ bit) for i in range(count)])  5.36 us
    ppermute x5, starting transfers between devices, swap(): return lax.ppermute(value, 'seq', [(i, i ^ bit) for i in range(count)])  3.18 us
    ppermute x1, starting transfers between devices, onward(): return lax.ppermute(value, 'seq', pairs)  3.11 us
    ppermute x1, waiting for transfers between devices, onward(): return lax.ppermute(value, 'seq', pairs)  2.81 us
  transfers between devices with their start and end apart: 7, of which 2 were waited for; matrix products, arithmetic and copies ran while one was open for 0% of the time, Pallas kernels for 51%

profile of v3, /device:TPU:14, one launch (start us, length us, event | category | flops | bytes accessed | tf_op | source)
XLA Modules:
  0.0 56.8 jit_solution(8288940702211626661)
XLA Ops:
  0.0 1.0 %cut.1 = bf16[256,1024]{1,0:T(8,128)(2,1)S(1)} custom-call(bf16[512,1024]{1,0:T(8,128)(2,1)} %bitcast.15), custom_call_target="tpu_custom_call" | custom-call | flops 1 | bytes 1000 | tf_op jit(solution)/shard_map/cut/pallas_call | solution.py:330
  1.1 0.0 copy-start.5
  1.1 0.0 copy-start.6
  1.1 0.6 %collective-permute-start = (bf16[256,1024]{1,0:T(8,128)(2,1)S(1)}, bf16[256,1024]{1,0:T(8,128)(2,1)S(1)}, u32[]{:S(2)}, u32[]{:S(2)}) collective-permute-start(bf16[256,1024]{1,0:T(8,128)(2,1)S(1)} %cut.1), channel_id=1, source_target_pairs={{0,2},{2,0},{4,6},{6,4},{8,10},{10,8},{12,14},{14,12},{1,3},{3,1},... | collective-permute-start | bytes 1572872 | tf_op jit(solution)/shard_map/ppermute | solution.py:364
  1.7 9.4 %own.1 = (bf16[512,1024]{1,0:T(8,128)(2,1)}, bf16[1024,512]{1,0:T(8,128)(2,1)}, bf16[256,1024]{1,0:T(8,128)(2,1)}, bf16[1024,128]{1,0:T(8,128)(2,1)}) custom-call(bf16[512,1024]{1,0:T(8,128)(2,1)} %bitcast.16, bf16[1024,1024]{1,0:T(8,128)(2,1)} %refs_1_.7, bf16[1024,1024]{1,0:T(8,128)(2,1)} %refs_2_.7), custom_call_target="tpu_custom_call" | custom-call | flops 1 | bytes 1000 | tf_op jit(solution)/shard_map/own/pallas_call | solution.py:330
  11.1 0.5 collective-permute-start.2
  11.6 5.6 %collective-permute-start.4 = (bf16[256,1024]{1,0:T(8,128)(2,1)}, bf16[256,1024]{1,0:T(8,128)(2,1)S(1)}, u32[]{:S(2)}, u32[]{:S(2)}) collective-permute-start(bf16[256,1024]{1,0:T(8,128)(2,1)} %get-tuple-element.35), channel_id=1, source_target_pairs={{2,4},{6,8},{10,12},{4,2},{8,6},{12,10},{3,5},{7,9},{11,13},{5,3},... | collective-permute-start | bytes 1572872 | tf_op jit(solution)/shard_map/ppermute | solution.py:372
  17.2 4.9 %own_attention.1 = (f32[4,8,256]{2,1,0:T(8,128)S(1)}, f32[4,8,256]{2,1,0:T(8,128)S(1)}, f32[4,1024,128]{2,1,0:T(8,128)S(1)}) custom-call(s32[4,4]{1,0:T(4,128)S(1)} %bitcast.5, s32[4]{0:T(128)S(1)} %bitcast.10, s32[1]{0:T(128)} %bitcast.2.pos_ref, bf16[512,1024]{1,0:T(8,128)(2,1)} %get-tuple-element.55.k_ref.refs_3_, bf16[1024,512]{1,0:T(8,128)(2,1)} %get-tuple-element.38.vt_ref), custom_call_target="tpu_custom_call" | custom-call | flops 1 | bytes 1000 | tf_op jit(solution)/shard_map/own_attention/pallas_call | solution.py:330
  22.1 0.0 collective-permute-done.2.refs_0_
  22.2 0.1 add.3
  22.2 0.0 copy-start
  22.2 0.0 copy-start.1
  22.3 0.0 copy-start.2
  22.3 1.1 %collective-permute-start.5 = (bf16[1024,128]{1,0:T(8,128)(2,1)S(1)}, bf16[1024,128]{1,0:T(8,128)(2,1)S(1)}, u32[]{:S(2)}, u32[]{:S(2)}) collective-permute-start(bf16[1024,128]{1,0:T(8,128)(2,1)S(1)} %add.3), channel_id=1, source_target_pairs={{0,8},{2,10},{4,12},{6,14},{8,0},{10,2},{12,4},{14,6},{1,9},{3,11}... | collective-permute-start | bytes 786440 | tf_op jit(solution)/shard_map/ppermute | solution.py:364
  23.4 0.0 collective-permute-done.refs_0_
  23.4 0.9 %collective-permute-start.1 = (bf16[256,1024]{1,0:T(8,128)(2,1)S(1)}, bf16[256,1024]{1,0:T(8,128)(2,1)S(1)}, u32[]{:S(2)}, u32[]{:S(2)}) collective-permute-start(bf16[256,1024]{1,0:T(8,128)(2,1)S(1)} %copy-done.7), channel_id=1, source_target_pairs={{0,2},{2,0},{4,6},{6,4},{8,10},{10,8},{12,14},{14,12},{1,3},{3,1},... | collective-permute-start | bytes 1572872 | tf_op jit(solution)/shard_map/ppermute | solution.py:364
  24.3 3.1 %collective-permute-start.3 = (bf16[256,1024]{1,0:T(8,128)(2,1)S(1)}, bf16[256,1024]{1,0:T(8,128)(2,1)S(1)}, u32[]{:S(2)}, u32[]{:S(2)}) collective-permute-start(bf16[256,1024]{1,0:T(8,128)(2,1)S(1)} %collective-permute-done.refs_0_), channel_id=1, source_target_pairs={{0,4},{4,8},{8,12},{6,2},{10,6},{14,10},{1,5},{5,9},{9,13},{7,3},{... | collective-permute-start | bytes 1572872 | tf_op jit(solution)/shard_map/ppermute | solution.py:368
  27.4 4.4 %within.1.n_ref = f32[1024,512]{1,0:T(8,128)S(1)} custom-call(bf16[512,1024]{1,0:T(8,128)(2,1)} %get-tuple-element.55.k_ref.refs_3_, bf16[1024,512]{1,0:T(8,128)(2,1)} %get-tuple-element.38.vt_ref), custom_call_target="tpu_custom_call" | custom-call | flops 99999997952 | bytes 1000 | tf_op jit(solution)/shard_map/within/pallas_call | solution.py:330
  31.8 2.1 %halo_a.1 = (f32[4,8,256]{2,1,0:T(8,128)S(1)}, f32[4,8,256]{2,1,0:T(8,128)S(1)}, f32[4,1024,128]{2,1,0:T(8,128)S(1)}) custom-call(s32[4,4]{1,0:T(4,128)S(1)} %bitcast.6, s32[4]{0:T(128)S(1)} %bitcast.11, s32[1]{0:T(128)} %bitcast.2.pos_ref, ...), custom_call_target="tpu_custom_call", output_to_operand_aliasing={{0}: (7, {}), {1}: (8, {}), {2}: (9, {})} | custom-call | flops 1 | bytes 1000 | tf_op jit(solution)/shard_map/halo_a/pallas_call | solution.py:330
  33.9 5.3 %collective-permute-done.5.refs_1_ = bf16[1024,128]{1,0:T(8,128)(2,1)S(1)} collective-permute-done((bf16[1024,128]{1,0:T(8,128)(2,1)S(1)}, bf16[1024,128]{1,0:T(8,128)(2,1)S(1)}, u32[]{:S(2)}, u32[]{:S(2)}) %collective-permute-start.5) | collective-permute-done | bytes 262176 | tf_op jit(solution)/shard_map/ppermute | solution.py:364
  39.2 0.2 carry.1
  39.4 0.1 collective-permute-start.6
  39.5 0.0 collective-permute-done.4.refs_0_
  39.5 3.4 %halo_b.1 = (f32[4,8,256]{2,1,0:T(8,128)S(1)}, f32[4,8,256]{2,1,0:T(8,128)S(1)}, f32[4,1024,128]{2,1,0:T(8,128)S(1)}) custom-call(s32[4,4]{1,0:T(4,128)S(1)} %bitcast.7, s32[4]{0:T(128)S(1)} %bitcast.12, s32[1]{0:T(128)} %bitcast.2.pos_ref, ...), custom_call_target="tpu_custom_call", output_to_operand_aliasing={{0}: (7, {}), {1}: (8, {}), {2}: (9, {})} | custom-call | flops 1 | bytes 1000 | tf_op jit(solution)/shard_map/halo_b/pallas_call | solution.py:330
  43.0 2.8 %collective-permute-done.3.refs_0_ = bf16[256,1024]{1,0:T(8,128)(2,1)S(1)} collective-permute-done((bf16[256,1024]{1,0:T(8,128)(2,1)S(1)}, bf16[256,1024]{1,0:T(8,128)(2,1)S(1)}, u32[]{:S(2)}, u32[]{:S(2)}) %collective-permute-start.3) | collective-permute-done | bytes 524320 | tf_op jit(solution)/shard_map/ppermute | solution.py:368
  45.8 2.8 %halo_c.1 = (f32[4,8,256]{2,1,0:T(8,128)S(1)}, f32[4,8,256]{2,1,0:T(8,128)S(1)}, f32[4,1024,128]{2,1,0:T(8,128)S(1)}) custom-call(s32[4,4]{1,0:T(4,128)S(1)} %bitcast.8, s32[4]{0:T(128)S(1)} %bitcast.13, s32[1]{0:T(128)} %bitcast.2.pos_ref, ...), custom_call_target="tpu_custom_call", output_to_operand_aliasing={{0}: (7, {}), {1}: (8, {}), {2}: (9, {})} | custom-call | flops 1 | bytes 1000 | tf_op jit(solution)/shard_map/halo_c/pallas_call | solution.py:330
  48.5 0.0 copy-start.3
  48.5 0.0 collective-permute-done.6.refs_2_
  48.5 1.5 %linear.1.refs_4_ = f32[1024,512]{1,0:T(8,128)S(1)} custom-call(s32[1]{0:T(128)} %bitcast.2.pos_ref, bf16[512,1024]{1,0:T(8,128)(2,1)S(1)} %copy-done.2, f32[1024,512]{1,0:T(8,128)S(1)} %within.1.n_ref, bf16[1024,128]{1,0:T(8,128)(2,1)S(1)} %collective-permute-done.2.refs_0_, bf16[1024,128]{1,0:T(8,128)(2,1)S(1)} %collective-permute-done.5.refs_1_, ...), custom_call_target="tpu_custom_call" | custom-call | flops 1 | bytes 1000 | tf_op jit(solution)/shard_map/linear/pallas_call | solution.py:330
  50.1 0.0 collective-permute-done.1.refs_0_
  50.1 0.0 copy-done.3
  50.1 6.7 %final.1 = (bf16[512,1024]{1,0:T(8,128)(2,1)}, f32[4,8,256]{2,1,0:T(8,128)S(1)}, f32[4,8,256]{2,1,0:T(8,128)S(1)}, f32[4,1024,128]{2,1,0:T(8,128)S(1)}) custom-call(s32[4,4]{1,0:T(4,128)S(1)} %bitcast.9, s32[4]{0:T(128)S(1)} %bitcast.14, s32[1]{0:T(128)} %bitcast.2.pos_ref, ...), custom_call_target="tpu_custom_call", output_to_operand_aliasing={{1}: (9, {}), {2}: (10, {}), {3}: (11, {})} | custom-call | flops 1 | bytes 1000 | tf_op jit(solution)/shard_map/final/pallas_call | solution.py:330
  (9 shorter events, 0.0 us)
Async XLA Ops:
  1.1 16.1 %copy-start.5 = (s32[1,4,4]{2,1,0:T(4,128)S(1)}, s32[1,4,4]{2,1,0:T(4,128)}, u32[]{:S(2)}) copy-start(s32[1,4,4]{2,1,0:T(4,128)} %param.10) | copy-start | bytes 196
  1.1 16.1 %copy-start.6 = (s32[1,4]{1,0:T(1,128)S(1)}, s32[1,4]{1,0:T(1,128)}, u32[]{:S(2)}) copy-start(s32[1,4]{1,0:T(1,128)} %param.11) | copy-start | bytes 52
  1.1 22.3 %collective-permute-start = (bf16[256,1024]{1,0:T(8,128)(2,1)S(1)}, bf16[256,1024]{1,0:T(8,128)(2,1)S(1)}, u32[]{:S(2)}, u32[]{:S(2)}) collective-permute-start(bf16[256,1024]{1,0:T(8,128)(2,1)S(1)} %cut.1), channel_id=1, source_target_pairs={{0,2},{2,0},{4,6},{6,4},{8,10},{10,8},{12,14},{14,12},{1,3},{3,1},... | collective-permute-start | bytes 1572872 | tf_op jit(solution)/shard_map/ppermute | solution.py:364
  11.1 11.1 %copy-start.4 = (bf16[1024,128]{1,0:T(8,128)(2,1)S(1)}, bf16[1024,128]{1,0:T(8,128)(2,1)}, u32[]{:S(2)}) copy-start(bf16[1024,128]{1,0:T(8,128)(2,1)} %get-tuple-element.56.s_ref) | copy-start | bytes 786436
  11.1 12.3 %copy-start.7 = (bf16[256,1024]{1,0:T(8,128)(2,1)S(1)}, bf16[256,1024]{1,0:T(8,128)(2,1)}, u32[]{:S(2)}) copy-start(bf16[256,1024]{1,0:T(8,128)(2,1)} %get-tuple-element.35) | copy-start | bytes 1572868
  11.1 11.1 %collective-permute-start.2 = (bf16[1024,128]{1,0:T(8,128)(2,1)}, bf16[1024,128]{1,0:T(8,128)(2,1)S(1)}, u32[]{:S(2)}, u32[]{:S(2)}) collective-permute-start(bf16[1024,128]{1,0:T(8,128)(2,1)} %get-tuple-element.56.s_ref), channel_id=1, source_target_pairs={{0,4},{2,6},{4,0},{6,2},{8,12},{10,14},{12,8},{14,10},{1,5},{3,7},... | collective-permute-start | bytes 786440 | tf_op jit(solution)/shard_map/ppermute | solution.py:364
  11.6 27.9 %collective-permute-start.4 = (bf16[256,1024]{1,0:T(8,128)(2,1)}, bf16[256,1024]{1,0:T(8,128)(2,1)S(1)}, u32[]{:S(2)}, u32[]{:S(2)}) collective-permute-start(bf16[256,1024]{1,0:T(8,128)(2,1)} %get-tuple-element.35), channel_id=1, source_target_pairs={{2,4},{6,8},{10,12},{4,2},{8,6},{12,10},{3,5},{7,9},{11,13},{5,3},... | collective-permute-start | bytes 1572872 | tf_op jit(solution)/shard_map/ppermute | solution.py:372
  22.2 9.5 %copy-start = (bf16[1024,1024]{1,0:T(8,128)(2,1)S(1)}, bf16[1024,1024]{1,0:T(8,128)(2,1)}, u32[]{:S(2)}) copy-start(bf16[1024,1024]{1,0:T(8,128)(2,1)} %refs_1_.7) | copy-start | bytes 6291460
  22.2 9.5 %copy-start.1 = (bf16[1024,1024]{1,0:T(8,128)(2,1)S(1)}, bf16[1024,1024]{1,0:T(8,128)(2,1)}, u32[]{:S(2)}) copy-start(bf16[1024,1024]{1,0:T(8,128)(2,1)} %refs_2_.7) | copy-start | bytes 6291460
  22.3 9.5 %copy-start.2 = (bf16[512,1024]{1,0:T(8,128)(2,1)S(1)}, bf16[512,1024]{1,0:T(8,128)(2,1)}, u32[]{:S(2)}) copy-start(bf16[512,1024]{1,0:T(8,128)(2,1)} %get-tuple-element.55.k_ref.refs_3_) | copy-start | bytes 3145732
  22.3 17.0 %collective-permute-start.5 = (bf16[1024,128]{1,0:T(8,128)(2,1)S(1)}, bf16[1024,128]{1,0:T(8,128)(2,1)S(1)}, u32[]{:S(2)}, u32[]{:S(2)}) collective-permute-start(bf16[1024,128]{1,0:T(8,128)(2,1)S(1)} %add.3), channel_id=1, source_target_pairs={{0,8},{2,10},{4,12},{6,14},{8,0},{10,2},{12,4},{14,6},{1,9},{3,11}... | collective-permute-start | bytes 786440 | tf_op jit(solution)/shard_map/ppermute | solution.py:364
  23.4 26.7 %collective-permute-start.1 = (bf16[256,1024]{1,0:T(8,128)(2,1)S(1)}, bf16[256,1024]{1,0:T(8,128)(2,1)S(1)}, u32[]{:S(2)}, u32[]{:S(2)}) collective-permute-start(bf16[256,1024]{1,0:T(8,128)(2,1)S(1)} %copy-done.7), channel_id=1, source_target_pairs={{0,2},{2,0},{4,6},{6,4},{8,10},{10,8},{12,14},{14,12},{1,3},{3,1},... | collective-permute-start | bytes 1572872 | tf_op jit(solution)/shard_map/ppermute | solution.py:364
  24.3 21.5 %collective-permute-start.3 = (bf16[256,1024]{1,0:T(8,128)(2,1)S(1)}, bf16[256,1024]{1,0:T(8,128)(2,1)S(1)}, u32[]{:S(2)}, u32[]{:S(2)}) collective-permute-start(bf16[256,1024]{1,0:T(8,128)(2,1)S(1)} %collective-permute-done.refs_0_), channel_id=1, source_target_pairs={{0,4},{4,8},{8,12},{6,2},{10,6},{14,10},{1,5},{5,9},{9,13},{7,3},{... | collective-permute-start | bytes 1572872 | tf_op jit(solution)/shard_map/ppermute | solution.py:368
  39.4 9.1 %collective-permute-start.6 = (bf16[1024,128]{1,0:T(8,128)(2,1)S(1)}, bf16[1024,128]{1,0:T(8,128)(2,1)S(1)}, u32[]{:S(2)}, u32[]{:S(2)}) collective-permute-start(bf16[1024,128]{1,0:T(8,128)(2,1)S(1)} %carry.1), channel_id=1, source_target_pairs={{0,2},{2,0},{4,6},{6,4},{8,10},{10,8},{12,14},{14,12},{1,3},{3,1},... | collective-permute-start | bytes 786440 | tf_op jit(solution)/shard_map/ppermute | solution.py:364
  48.5 1.6 %copy-start.3 = (bf16[1024,1024]{1,0:T(8,128)(2,1)S(1)}, bf16[1024,1024]{1,0:T(8,128)(2,1)}, u32[]{:S(2)}) copy-start(bf16[1024,1024]{1,0:T(8,128)(2,1)} %refs_5_.1) | copy-start | bytes 6291460

commit v4 on v3

--- a/solution.py
+++ b/solution.py
@@ -52,39 +52,32 @@
 def own_kernel(
     x_hbm, wk_hbm, wv_hbm, k_hbm, vt_hbm, b_hbm, s_ref, x_ref, wk_ref, wv_ref, k_ref, vt_ref, in_sems, out_sems
 ):
-    width = x_ref.shape[1]
+    ins = [
+        pltpu.make_async_copy(src, dst, in_sems.at[i])
+        for i, (src, dst) in enumerate(((x_hbm, x_ref), (wk_hbm, wk_ref), (wv_hbm, wv_ref)))
+    ]
+    outs = [
+        pltpu.make_async_copy(src, dst, out_sems.at[i])
+        for i, (src, dst) in enumerate(
+            ((x_ref.at[x_ref.shape[0] - b_hbm.shape[0] :], b_hbm), (k_ref, k_hbm), (vt_ref, vt_hbm))
+        )
+    ]
+    for copy in ins:
+        copy.start()
+    ins[0].wait()
+    outs[0].start()
+    ins[1].wait()
+    k_ref[...] = dot_nn(x_ref[...], wk_ref[...]).astype(BF16)
+    outs[1].start()
+    ins[2].wait()
     step = 256
-    tiles = [slice(i, i + step) for i in range(0, width, step)]
-    n = len(tiles)
-    ins = [pltpu.make_async_copy(x_hbm, x_ref, in_sems.at[0])]
-    for j, part in enumerate(tiles):
-        for i, (src, dst) in enumerate(((wk_hbm, wk_ref), (wv_hbm, wv_ref))):
-            ins.append(pltpu.make_async_copy(src.at[:, part], dst.at[:, part], in_sems.at[1 + 2 * j + i]))
-    for copy in ins[:3]:
-        copy.start()
-    outs = []
-
-    def put(src, dst):
-        copy = pltpu.make_async_copy(src, dst, out_sems.at[len(outs)])
-        copy.start()
-        outs.append(copy)
-
-    ins[0].wait()
-    put(x_ref.at[x_ref.shape[0] - b_hbm.shape[0] :], b_hbm)
-    for j, part in enumerate(tiles):
-        for copy in ins[3 + 2 * j : 5 + 2 * j]:
-            copy.start()
-        ins[1 + 2 * j].wait()
-        k = dot_nn(x_ref[...], wk_ref[:, part]).astype(BF16)
-        k_ref[:, part] = k
-        put(k_ref.at[:, part], k_hbm.at[:, part])
-        f = silu(k)
-        ins[2 + 2 * j].wait()
-        vt_ref[part, :] = dot_nn(x_ref[...], wv_ref[:, part]).astype(BF16).T
-        put(vt_ref.at[part], vt_hbm.at[part])
-        for h in range(0, step, DL):
-            head = slice(part.start + h, part.start + h + DL)
-            s_ref[head, :] = dot_nn(vt_ref[head, :], f[:, h : h + DL]).astype(BF16)
+    for i in range(0, wv_ref.shape[1], step):
+        part = slice(i, i + step)
+        vt_ref[part, :] = dot_nt(wv_ref[:, part].T, x_ref[...]).astype(BF16)
+    for h in range(HL):
+        part = slice(h * DL, (h + 1) * DL)
+        s_ref[part, :] = dot_nn(vt_ref[part, :], silu(k_ref[:, part])).astype(BF16)
+    outs[2].start()
     for copy in outs:
         copy.wait()
 
@@ -363,6 +356,9 @@
     def swap(value, bit):
         return lax.ppermute(value, "seq", [(i, i ^ bit) for i in range(count)])
 
+    def up(value, bit):
+        return lax.ppermute(value, "seq", [(i, i | bit) for i in range(count) if not i & bit])
+
     def onward(value):
         pairs = [(i, i + 2) for i in range(0, count - 2, 2)] + [(i, i - 2) for i in range(3, count, 2)]
         return lax.ppermute(value, "seq", pairs)
@@ -403,7 +399,6 @@
         space=pltpu.HBM,
     )
     near_a = swap(first_rows, 1)
-    steps = width // 256
     keyed, values_t, last_rows, state = call(
         own_kernel,
         "own",
@@ -420,15 +415,18 @@
             pltpu.VMEM((width, width), BF16),
             pltpu.VMEM((rows, width), BF16),
             pltpu.VMEM((width, rows), BF16),
-            pltpu.SemaphoreType.DMA((1 + 2 * steps,)),
-            pltpu.SemaphoreType.DMA((1 + 2 * steps,)),
+            pltpu.SemaphoreType.DMA((3,)),
+            pltpu.SemaphoreType.DMA((3,)),
         ),
         limit=56 * MIB,
         space=pltpu.HBM,
         out_space=[pltpu.HBM] * 3 + [pltpu.VMEM],
     )
     far_b = across(last_rows)
-    heard = [swap(state, 2)]
+    def halves(value, bit):
+        return (swap if 2 * bit < count else up)(value, bit)
+
+    heard = [halves(state, 2)]
     shapes = [((blocks, H // 2, 2 * size), F32)] * 2 + [((blocks, width, size), F32)]
     softmax = call(
         functools.partial(own_attention_kernel, size),
@@ -442,14 +440,14 @@
     stride = 4
     while stride < count:
         total = total + after(heard[-1], softmax[0])
-        heard.append(swap(total, stride))
+        heard.append(halves(total, stride))
         stride *= 2
     far_a = onward(after(near_a, total))
     near_b = swap(after(last_rows, near_a), 1)
     (within,) = call(
         within_kernel,
         "within",
-        (after(in_hbm(keyed), softmax[0], near_a), in_hbm(values_t)),
+        (after(keyed, softmax[0], near_a), values_t),
         [((width, rows), F32)],
     )
     softmax = join_halo("halo_a", softmax, [(True, 0)], [after(near_a, within)])

time: 57.8 us -> 57.8 us (level)
  the two profiles are of different devices: /device:TPU:14 before, /device:TPU:17 now
where the time goes in v4:
time: 57.8 us; the launch traced here: 57.4 us
  Pallas kernels  32.9 us (57%)
  starting transfers between devices  13 us (22%)
  waiting for transfers between devices  10.1 us (17%)
  other arithmetic  1.02 us (2%)
    pallas_call x10, Pallas kernels, call(): pl.pallas_call(kernel, name=name, in_specs=[SMEM] * smem + [pl.BlockSpec(...  32.9 us
    ppermute x1, waiting for transfers between devices, onward(): return lax.ppermute(value, 'seq', pairs)  10.1 us
    ppermute x4, starting transfers between devices, swap(): return lax.ppermute(value, 'seq', [(i, i ^ bit) for i in range(count)])  6.89 us
    ppermute x1, starting transfers between devices, onward(): return lax.ppermute(value, 'seq', pairs)  2.66 us
    ppermute x1, starting transfers between devices, across(): lax.ppermute(value, 'seq', [(i, i + 1) for i in odd] + [(i + 1, i) for i...  1.91 us
    ppermute x1, starting transfers between devices, up(): lax.ppermute(value, 'seq', [(i, i | bit) for i in range(count) if not i &...  1.56 us
  transfers between devices with their start and end apart: 7, of which 1 were waited for; matrix products, arithmetic and copies ran while one was open for 2% of the time, Pallas kernels for 44%

profile of v4, /device:TPU:17, one launch (start us, length us, event | category | flops | bytes accessed | tf_op | source)
XLA Modules:
  0.0 57.4 jit_solution(2213219151342883950)
XLA Ops:
  0.0 1.9 %cut.1 = bf16[256,1024]{1,0:T(8,128)(2,1)} custom-call(bf16[512,1024]{1,0:T(8,128)(2,1)} %bitcast.15), custom_call_target="tpu_custom_call" | custom-call | flops 1 | bytes 1000 | tf_op jit(solution)/shard_map/cut/pallas_call | solution.py:323
  1.9 0.0 copy-start.6
  1.9 0.0 copy-start.7
  1.9 1.3 %collective-permute-start = (bf16[256,1024]{1,0:T(8,128)(2,1)}, bf16[256,1024]{1,0:T(8,128)(2,1)S(1)}, u32[]{:S(2)}, u32[]{:S(2)}) collective-permute-start(bf16[256,1024]{1,0:T(8,128)(2,1)} %cut.1), channel_id=1, source_target_pairs={{0,2},{2,0},{4,6},{6,4},{8,10},{10,8},{12,14},{14,12},{1,3},{3,1},... | collective-permute-start | bytes 1572872 | tf_op jit(solution)/shard_map/ppermute | solution.py:357
  3.2 6.3 %own.1 = (bf16[512,1024]{1,0:T(8,128)(2,1)}, bf16[1024,512]{1,0:T(8,128)(2,1)}, bf16[256,1024]{1,0:T(8,128)(2,1)}, bf16[1024,128]{1,0:T(8,128)(2,1)}) custom-call(bf16[512,1024]{1,0:T(8,128)(2,1)} %bitcast.16, bf16[1024,1024]{1,0:T(8,128)(2,1)} %refs_1_.7, bf16[1024,1024]{1,0:T(8,128)(2,1)} %refs_2_.7), custom_call_target="tpu_custom_call" | custom-call | flops 1 | bytes 1000 | tf_op jit(solution)/shard_map/own/pallas_call | solution.py:323
  9.5 0.0 copy-start.2
  9.5 1.3 %collective-permute-start.2 = (bf16[1024,128]{1,0:T(8,128)(2,1)}, bf16[1024,128]{1,0:T(8,128)(2,1)S(1)}, u32[]{:S(2)}, u32[]{:S(2)}) collective-permute-start(bf16[1024,128]{1,0:T(8,128)(2,1)} %get-tuple-element.56.s_ref), channel_id=1, source_target_pairs={{0,4},{2,6},{4,0},{6,2},{8,12},{10,14},{12,8},{14,10},{1,5},{3,7},... | collective-permute-start | bytes 786440 | tf_op jit(solution)/shard_map/ppermute | solution.py:357
  10.9 1.9 %collective-permute-start.4 = (bf16[256,1024]{1,0:T(8,128)(2,1)}, bf16[256,1024]{1,0:T(8,128)(2,1)S(1)}, u32[]{:S(2)}, u32[]{:S(2)}) collective-permute-start(bf16[256,1024]{1,0:T(8,128)(2,1)} %get-tuple-element.35), channel_id=1, source_target_pairs={{2,4},{6,8},{10,12},{4,2},{8,6},{12,10},{3,5},{7,9},{11,13},{5,3},... | collective-permute-start | bytes 1572872 | tf_op jit(solution)/shard_map/ppermute | solution.py:368
  12.8 5.7 %own_attention.1 = (f32[4,8,256]{2,1,0:T(8,128)S(1)}, f32[4,8,256]{2,1,0:T(8,128)S(1)}, f32[4,1024,128]{2,1,0:T(8,128)S(1)}) custom-call(s32[4,4]{1,0:T(4,128)S(1)} %bitcast.5, s32[4]{0:T(128)S(1)} %bitcast.10, s32[1]{0:T(128)} %bitcast.2.pos_ref, bf16[512,1024]{1,0:T(8,128)(2,1)} %get-tuple-element.55.k_ref.refs_3_, bf16[1024,512]{1,0:T(8,128)(2,1)} %get-tuple-element.38.vt_ref), custom_call_target="tpu_custom_call" | custom-call | flops 1 | bytes 1000 | tf_op jit(solution)/shard_map/own_attention/pallas_call | solution.py:323
  18.5 0.0 collective-permute-done.2.refs_0_
  18.5 1.0 %add.3 = bf16[1024,128]{1,0:T(8,128)(2,1)S(1)} add(bf16[1024,128]{1,0:T(8,128)(2,1)} %get-tuple-element.56.s_ref, bf16[1024,128]{1,0:T(8,128)(2,1)S(1)} %collective-permute-done.2.refs_0_) | non-fusion elementwise | flops 131072 | bytes 786432 | tf_op jit(solution)/shard_map/add | solution.py:442
  19.5 0.0 copy-start
  19.5 0.0 copy-start.1
  19.6 1.6 %collective-permute-start.5 = (bf16[1024,128]{1,0:T(8,128)(2,1)S(1)}, bf16[1024,128]{1,0:T(8,128)(2,1)S(1)}, u32[]{:S(2)}, u32[]{:S(2)}) collective-permute-start(bf16[1024,128]{1,0:T(8,128)(2,1)S(1)} %add.3), channel_id=1, source_target_pairs={{0,8},{2,10},{4,12},{6,14},{1,9},{3,11},{5,13},{7,15},{16,24},{18,... | collective-permute-start | bytes 786440 | tf_op jit(solution)/shard_map/ppermute | solution.py:360
  21.1 0.0 collective-permute-done.refs_0_
  21.1 0.5 collective-permute-start.1
  21.7 2.7 %collective-permute-start.3 = (bf16[256,1024]{1,0:T(8,128)(2,1)S(1)}, bf16[256,1024]{1,0:T(8,128)(2,1)S(1)}, u32[]{:S(2)}, u32[]{:S(2)}) collective-permute-start(bf16[256,1024]{1,0:T(8,128)(2,1)S(1)} %collective-permute-done.refs_0_), channel_id=1, source_target_pairs={{0,4},{4,8},{8,12},{6,2},{10,6},{14,10},{1,5},{5,9},{9,13},{7,3},{... | collective-permute-start | bytes 1572872 | tf_op jit(solution)/shard_map/ppermute | solution.py:364
  24.4 2.8 %within.1.n_ref = f32[1024,512]{1,0:T(8,128)S(1)} custom-call(bf16[512,1024]{1,0:T(8,128)(2,1)S(1)} %copy-done.2, bf16[1024,512]{1,0:T(8,128)(2,1)S(1)} %copy-done.4), custom_call_target="tpu_custom_call" | custom-call | flops 99999997952 | bytes 1000 | tf_op jit(solution)/shard_map/within/pallas_call | solution.py:323
  27.2 2.8 %halo_a.1 = (f32[4,8,256]{2,1,0:T(8,128)S(1)}, f32[4,8,256]{2,1,0:T(8,128)S(1)}, f32[4,1024,128]{2,1,0:T(8,128)S(1)}) custom-call(s32[4,4]{1,0:T(4,128)S(1)} %bitcast.6, s32[4]{0:T(128)S(1)} %bitcast.11, s32[1]{0:T(128)} %bitcast.2.pos_ref, ...), custom_call_target="tpu_custom_call", output_to_operand_aliasing={{0}: (7, {}), {1}: (8, {}), {2}: (9, {})} | custom-call | flops 1 | bytes 1000 | tf_op jit(solution)/shard_map/halo_a/pallas_call | solution.py:323
  30.0 0.0 collective-permute-done.5.refs_1_
  30.0 0.2 carry.1
  30.2 3.7 %collective-permute-start.6 = (bf16[1024,128]{1,0:T(8,128)(2,1)S(1)}, bf16[1024,128]{1,0:T(8,128)(2,1)S(1)}, u32[]{:S(2)}, u32[]{:S(2)}) collective-permute-start(bf16[1024,128]{1,0:T(8,128)(2,1)S(1)} %carry.1), channel_id=1, source_target_pairs={{0,2},{2,0},{4,6},{6,4},{8,10},{10,8},{12,14},{14,12},{1,3},{3,1},... | collective-permute-start | bytes 786440 | tf_op jit(solution)/shard_map/ppermute | solution.py:357
  33.9 0.0 collective-permute-done.4.refs_0_
  33.9 3.4 %halo_b.1 = (f32[4,8,256]{2,1,0:T(8,128)S(1)}, f32[4,8,256]{2,1,0:T(8,128)S(1)}, f32[4,1024,128]{2,1,0:T(8,128)S(1)}) custom-call(s32[4,4]{1,0:T(4,128)S(1)} %bitcast.7, s32[4]{0:T(128)S(1)} %bitcast.12, s32[1]{0:T(128)} %bitcast.2.pos_ref, ...), custom_call_target="tpu_custom_call", output_to_operand_aliasing={{0}: (7, {}), {1}: (8, {}), {2}: (9, {})} | custom-call | flops 1 | bytes 1000 | tf_op jit(solution)/shard_map/halo_b/pallas_call | solution.py:323
  37.3 10.1 %collective-permute-done.3.refs_0_ = bf16[256,1024]{1,0:T(8,128)(2,1)S(1)} collective-permute-done((bf16[256,1024]{1,0:T(8,128)(2,1)S(1)}, bf16[256,1024]{1,0:T(8,128)(2,1)S(1)}, u32[]{:S(2)}, u32[]{:S(2)}) %collective-permute-start.3) | collective-permute-done | bytes 524320 | tf_op jit(solution)/shard_map/ppermute | solution.py:364
  47.4 2.8 %halo_c.1 = (f32[4,8,256]{2,1,0:T(8,128)S(1)}, f32[4,8,256]{2,1,0:T(8,128)S(1)}, f32[4,1024,128]{2,1,0:T(8,128)S(1)}) custom-call(s32[4,4]{1,0:T(4,128)S(1)} %bitcast.8, s32[4]{0:T(128)S(1)} %bitcast.13, s32[1]{0:T(128)} %bitcast.2.pos_ref, ...), custom_call_target="tpu_custom_call", output_to_operand_aliasing={{0}: (7, {}), {1}: (8, {}), {2}: (9, {})} | custom-call | flops 1 | bytes 1000 | tf_op jit(solution)/shard_map/halo_c/pallas_call | solution.py:323
  50.2 0.0 copy-start.3
  50.2 0.0 collective-permute-done.6.refs_2_
  50.2 1.5 %linear.1.refs_4_ = f32[1024,512]{1,0:T(8,128)S(1)} custom-call(s32[1]{0:T(128)} %bitcast.2.pos_ref, bf16[512,1024]{1,0:T(8,128)(2,1)S(1)} %copy-done.2, f32[1024,512]{1,0:T(8,128)S(1)} %within.1.n_ref, bf16[1024,128]{1,0:T(8,128)(2,1)S(1)} %collective-permute-done.2.refs_0_, bf16[1024,128]{1,0:T(8,128)(2,1)S(1)} %collective-permute-done.5.refs_1_, ...), custom_call_target="tpu_custom_call" | custom-call | flops 1 | bytes 1000 | tf_op jit(solution)/shard_map/linear/pallas_call | solution.py:323
  51.8 0.0 collective-permute-done.1.refs_0_
  51.8 0.0 copy-done.3
  51.8 5.6 %final.1 = (bf16[512,1024]{1,0:T(8,128)(2,1)}, f32[4,8,256]{2,1,0:T(8,128)S(1)}, f32[4,8,256]{2,1,0:T(8,128)S(1)}, f32[4,1024,128]{2,1,0:T(8,128)S(1)}) custom-call(s32[4,4]{1,0:T(4,128)S(1)} %bitcast.9, s32[4]{0:T(128)S(1)} %bitcast.14, s32[1]{0:T(128)} %bitcast.2.pos_ref, ...), custom_call_target="tpu_custom_call", output_to_operand_aliasing={{1}: (9, {}), {2}: (10, {}), {3}: (11, {})} | custom-call | flops 1 | bytes 1000 | tf_op jit(solution)/shard_map/final/pallas_call | solution.py:323
  (11 shorter events, 0.0 us)
Async XLA Ops:
  1.9 10.9 %copy-start.6 = (s32[1,4,4]{2,1,0:T(4,128)S(1)}, s32[1,4,4]{2,1,0:T(4,128)}, u32[]{:S(2)}) copy-start(s32[1,4,4]{2,1,0:T(4,128)} %param.10) | copy-start | bytes 196
  1.9 10.9 %copy-start.7 = (s32[1,4]{1,0:T(1,128)S(1)}, s32[1,4]{1,0:T(1,128)}, u32[]{:S(2)}) copy-start(s32[1,4]{1,0:T(1,128)} %param.11) | copy-start | bytes 52
  1.9 19.2 %collective-permute-start = (bf16[256,1024]{1,0:T(8,128)(2,1)}, bf16[256,1024]{1,0:T(8,128)(2,1)S(1)}, u32[]{:S(2)}, u32[]{:S(2)}) collective-permute-start(bf16[256,1024]{1,0:T(8,128)(2,1)} %cut.1), channel_id=1, source_target_pairs={{0,2},{2,0},{4,6},{6,4},{8,10},{10,8},{12,14},{14,12},{1,3},{3,1},... | collective-permute-start | bytes 1572872 | tf_op jit(solution)/shard_map/ppermute | solution.py:357
  9.5 14.9 %copy-start.2 = (bf16[512,1024]{1,0:T(8,128)(2,1)S(1)}, bf16[512,1024]{1,0:T(8,128)(2,1)}, u32[]{:S(2)}) copy-start(bf16[512,1024]{1,0:T(8,128)(2,1)} %get-tuple-element.55.k_ref.refs_3_) | copy-start | bytes 3145732
  9.5 14.9 %copy-start.4 = (bf16[1024,512]{1,0:T(8,128)(2,1)S(1)}, bf16[1024,512]{1,0:T(8,128)(2,1)}, u32[]{:S(2)}) copy-start(bf16[1024,512]{1,0:T(8,128)(2,1)} %get-tuple-element.38.vt_ref) | copy-start | bytes 3145732
  9.5 9.0 %collective-permute-start.2 = (bf16[1024,128]{1,0:T(8,128)(2,1)}, bf16[1024,128]{1,0:T(8,128)(2,1)S(1)}, u32[]{:S(2)}, u32[]{:S(2)}) collective-permute-start(bf16[1024,128]{1,0:T(8,128)(2,1)} %get-tuple-element.56.s_ref), channel_id=1, source_target_pairs={{0,4},{2,6},{4,0},{6,2},{8,12},{10,14},{12,8},{14,10},{1,5},{3,7},... | collective-permute-start | bytes 786440 | tf_op jit(solution)/shard_map/ppermute | solution.py:357
  10.9 23.0 %collective-permute-start.4 = (bf16[256,1024]{1,0:T(8,128)(2,1)}, bf16[256,1024]{1,0:T(8,128)(2,1)S(1)}, u32[]{:S(2)}, u32[]{:S(2)}) collective-permute-start(bf16[256,1024]{1,0:T(8,128)(2,1)} %get-tuple-element.35), channel_id=1, source_target_pairs={{2,4},{6,8},{10,12},{4,2},{8,6},{12,10},{3,5},{7,9},{11,13},{5,3},... | collective-permute-start | bytes 1572872 | tf_op jit(solution)/shard_map/ppermute | solution.py:368
  12.8 8.4 %copy-start.8 = (bf16[256,1024]{1,0:T(8,128)(2,1)S(1)}, bf16[256,1024]{1,0:T(8,128)(2,1)}, u32[]{:S(2)}) copy-start(bf16[256,1024]{1,0:T(8,128)(2,1)} %get-tuple-element.35) | copy-start | bytes 1572868
  19.5 7.7 %copy-start = (bf16[1024,1024]{1,0:T(8,128)(2,1)S(1)}, bf16[1024,1024]{1,0:T(8,128)(2,1)}, u32[]{:S(2)}) copy-start(bf16[1024,1024]{1,0:T(8,128)(2,1)} %refs_1_.7) | copy-start | bytes 6291460
  19.5 7.7 %copy-start.1 = (bf16[1024,1024]{1,0:T(8,128)(2,1)S(1)}, bf16[1024,1024]{1,0:T(8,128)(2,1)}, u32[]{:S(2)}) copy-start(bf16[1024,1024]{1,0:T(8,128)(2,1)} %refs_2_.7) | copy-start | bytes 6291460
  19.6 10.4 %collective-permute-start.5 = (bf16[1024,128]{1,0:T(8,128)(2,1)S(1)}, bf16[1024,128]{1,0:T(8,128)(2,1)S(1)}, u32[]{:S(2)}, u32[]{:S(2)}) collective-permute-start(bf16[1024,128]{1,0:T(8,128)(2,1)S(1)} %add.3), channel_id=1, source_target_pairs={{0,8},{2,10},{4,12},{6,14},{1,9},{3,11},{5,13},{7,15},{16,24},{18,... | collective-permute-start | bytes 786440 | tf_op jit(solution)/shard_map/ppermute | solution.py:360
  21.1 30.6 %collective-permute-start.1 = (bf16[256,1024]{1,0:T(8,128)(2,1)S(1)}, bf16[256,1024]{1,0:T(8,128)(2,1)S(1)}, u32[]{:S(2)}, u32[]{:S(2)}) collective-permute-start(bf16[256,1024]{1,0:T(8,128)(2,1)S(1)} %copy-done.8), channel_id=1, source_target_pairs={{0,2},{2,0},{4,6},{6,4},{8,10},{10,8},{12,14},{14,12},{1,3},{3,1},... | collective-permute-start | bytes 1572872 | tf_op jit(solution)/shard_map/ppermute | solution.py:357
  21.7 25.8 %collective-permute-start.3 = (bf16[256,1024]{1,0:T(8,128)(2,1)S(1)}, bf16[256,1024]{1,0:T(8,128)(2,1)S(1)}, u32[]{:S(2)}, u32[]{:S(2)}) collective-permute-start(bf16[256,1024]{1,0:T(8,128)(2,1)S(1)} %collective-permute-done.refs_0_), channel_id=1, source_target_pairs={{0,4},{4,8},{8,12},{6,2},{10,6},{14,10},{1,5},{5,9},{9,13},{7,3},{... | collective-permute-start | bytes 1572872 | tf_op jit(solution)/shard_map/ppermute | solution.py:364
  27.2 2.8 %copy-start.5 = (bf16[1024,128]{1,0:T(8,128)(2,1)S(1)}, bf16[1024,128]{1,0:T(8,128)(2,1)}, u32[]{:S(2)}) copy-start(bf16[1024,128]{1,0:T(8,128)(2,1)} %get-tuple-element.56.s_ref) | copy-start | bytes 786436
  30.2 20.0 %collective-permute-start.6 = (bf16[1024,128]{1,0:T(8,128)(2,1)S(1)}, bf16[1024,128]{1,0:T(8,128)(2,1)S(1)}, u32[]{:S(2)}, u32[]{:S(2)}) collective-permute-start(bf16[1024,128]{1,0:T(8,128)(2,1)S(1)} %carry.1), channel_id=1, source_target_pairs={{0,2},{2,0},{4,6},{6,4},{8,10},{10,8},{12,14},{14,12},{1,3},{3,1},... | collective-permute-start | bytes 786440 | tf_op jit(solution)/shard_map/ppermute | solution.py:357
  50.2 1.6 %copy-start.3 = (bf16[1024,1024]{1,0:T(8,128)(2,1)S(1)}, bf16[1024,1024]{1,0:T(8,128)(2,1)}, u32[]{:S(2)}) copy-start(bf16[1024,1024]{1,0:T(8,128)(2,1)} %refs_5_.1) | copy-start | bytes 6291460

commit v5 on v4

--- a/solution.py
+++ b/solution.py
@@ -301,11 +301,11 @@
             comb_ref[rows, cols] = both.T.astype(BF16)
         return carry
 
-    lax.fori_loop(0, list_ref.shape[0], finish, 0)
+    lax.fori_loop(0, list_ref.shape[0], finish, 0, unroll=True)
     out_ref[...] = dot_nn(comb_ref[...], wo_ref[...]).astype(BF16)
 
 
-COSTLY = ("within",)
+COSTLY = ("halo_a",)
 
 
 def call(
@@ -424,7 +424,7 @@
     )
     far_b = across(last_rows)
     def halves(value, bit):
-        return (swap if 2 * bit < count else up)(value, bit)
+        return swap(value, bit)
 
     heard = [halves(state, 2)]
     shapes = [((blocks, H // 2, 2 * size), F32)] * 2 + [((blocks, width, size), F32)]

time: 57.8 us -> 54.7 us (0.946)
  the two profiles are of different devices: /device:TPU:17 before, /device:TPU:4 now
where the time goes in v5:
time: 54.7 us; the launch traced here: 55.5 us
  Pallas kernels  31.8 us (58%)
  starting transfers between devices  13.7 us (25%)
  waiting for transfers between devices  8.77 us (16%)
  other arithmetic  1.02 us (2%)
    pallas_call x10, Pallas kernels, call(): pl.pallas_call(kernel, name=name, in_specs=[SMEM] * smem + [pl.BlockSpec(...  31.8 us
    ppermute x5, starting transfers between devices, swap(): return lax.ppermute(value, 'seq', [(i, i ^ bit) for i in range(count)])  8.76 us
    ppermute x5, waiting for transfers between devices, swap(): return lax.ppermute(value, 'seq', [(i, i ^ bit) for i in range(count)])  5.21 us
    ppermute x1, waiting for transfers between devices, onward(): return lax.ppermute(value, 'seq', pairs)  3.56 us
    ppermute x1, starting transfers between devices, across(): lax.ppermute(value, 'seq', [(i, i + 1) for i in odd] + [(i + 1, i) for i...  3.45 us
    ppermute x1, starting transfers between devices, onward(): return lax.ppermute(value, 'seq', pairs)  1.47 us
  transfers between devices with their start and end apart: 7, of which 2 were waited for; matrix products, arithmetic and copies ran while one was open for 2% of the time, Pallas kernels for 46%

profile of v5, /device:TPU:4, one launch (start us, length us, event | category | flops | bytes accessed | tf_op | source)
XLA Modules:
  0.0 55.5 jit_solution(11251194862843098062)
XLA Ops:
  0.0 1.0 %cut.1 = bf16[256,1024]{1,0:T(8,128)(2,1)S(1)} custom-call(bf16[512,1024]{1,0:T(8,128)(2,1)} %bitcast.15), custom_call_target="tpu_custom_call" | custom-call | flops 1 | bytes 1000 | tf_op jit(solution)/shard_map/cut/pallas_call | solution.py:323
  1.1 0.0 copy-start.6
  1.1 0.0 copy-start.7
  1.1 0.1 collective-permute-start
  1.2 6.3 %own.1 = (bf16[512,1024]{1,0:T(8,128)(2,1)}, bf16[1024,512]{1,0:T(8,128)(2,1)}, bf16[256,1024]{1,0:T(8,128)(2,1)}, bf16[1024,128]{1,0:T(8,128)(2,1)}) custom-call(bf16[512,1024]{1,0:T(8,128)(2,1)} %bitcast.16, bf16[1024,1024]{1,0:T(8,128)(2,1)} %refs_1_.7, bf16[1024,1024]{1,0:T(8,128)(2,1)} %refs_2_.7), custom_call_target="tpu_custom_call" | custom-call | flops 1 | bytes 1000 | tf_op jit(solution)/shard_map/own/pallas_call | solution.py:323
  7.4 0.0 copy-start
  7.5 2.1 %collective-permute-start.2 = (bf16[1024,128]{1,0:T(8,128)(2,1)}, bf16[1024,128]{1,0:T(8,128)(2,1)S(1)}, u32[]{:S(2)}, u32[]{:S(2)}) collective-permute-start(bf16[1024,128]{1,0:T(8,128)(2,1)} %get-tuple-element.56.s_ref), channel_id=1, source_target_pairs={{0,4},{2,6},{4,0},{6,2},{8,12},{10,14},{12,8},{14,10},{1,5},{3,7},... | collective-permute-start | bytes 786440 | tf_op jit(solution)/shard_map/ppermute | solution.py:357
  9.6 3.5 %collective-permute-start.4 = (bf16[256,1024]{1,0:T(8,128)(2,1)}, bf16[256,1024]{1,0:T(8,128)(2,1)S(1)}, u32[]{:S(2)}, u32[]{:S(2)}) collective-permute-start(bf16[256,1024]{1,0:T(8,128)(2,1)} %get-tuple-element.35), channel_id=1, source_target_pairs={{2,4},{6,8},{10,12},{4,2},{8,6},{12,10},{3,5},{7,9},{11,13},{5,3},... | collective-permute-start | bytes 1572872 | tf_op jit(solution)/shard_map/ppermute | solution.py:368
  13.1 5.6 %own_attention.1 = (f32[4,8,256]{2,1,0:T(8,128)S(1)}, f32[4,8,256]{2,1,0:T(8,128)S(1)}, f32[4,1024,128]{2,1,0:T(8,128)S(1)}) custom-call(s32[4,4]{1,0:T(4,128)S(1)} %bitcast.5, s32[4]{0:T(128)S(1)} %bitcast.10, s32[1]{0:T(128)} %bitcast.2.pos_ref, bf16[512,1024]{1,0:T(8,128)(2,1)} %get-tuple-element.55.k_ref.refs_3_, bf16[1024,512]{1,0:T(8,128)(2,1)} %get-tuple-element.38.vt_ref), custom_call_target="tpu_custom_call" | custom-call | flops 1 | bytes 1000 | tf_op jit(solution)/shard_map/own_attention/pallas_call | solution.py:323
  18.7 0.0 collective-permute-done.2.refs_0_
  18.7 1.0 %add.3 = bf16[1024,128]{1,0:T(8,128)(2,1)S(1)} add(bf16[1024,128]{1,0:T(8,128)(2,1)} %get-tuple-element.56.s_ref, bf16[1024,128]{1,0:T(8,128)(2,1)S(1)} %collective-permute-done.2.refs_0_) | non-fusion elementwise | flops 131072 | bytes 786432 | tf_op jit(solution)/shard_map/add | solution.py:442
  19.8 0.0 copy-start.1
  19.8 0.0 copy-start.2
  19.8 2.0 %collective-permute-start.5 = (bf16[1024,128]{1,0:T(8,128)(2,1)S(1)}, bf16[1024,128]{1,0:T(8,128)(2,1)S(1)}, u32[]{:S(2)}, u32[]{:S(2)}) collective-permute-start(bf16[1024,128]{1,0:T(8,128)(2,1)S(1)} %add.3), channel_id=1, source_target_pairs={{0,8},{2,10},{4,12},{6,14},{8,0},{10,2},{12,4},{14,6},{1,9},{3,11}... | collective-permute-start | bytes 786440 | tf_op jit(solution)/shard_map/ppermute | solution.py:357
  21.8 0.0 collective-permute-done.refs_0_
  21.8 0.9 %collective-permute-start.1 = (bf16[256,1024]{1,0:T(8,128)(2,1)S(1)}, bf16[256,1024]{1,0:T(8,128)(2,1)S(1)}, u32[]{:S(2)}, u32[]{:S(2)}) collective-permute-start(bf16[256,1024]{1,0:T(8,128)(2,1)S(1)} %copy-done.8), channel_id=1, source_target_pairs={{0,2},{2,0},{4,6},{6,4},{8,10},{10,8},{12,14},{14,12},{1,3},{3,1},... | collective-permute-start | bytes 1572872 | tf_op jit(solution)/shard_map/ppermute | solution.py:357
  22.7 2.8 %within.1.n_ref = f32[1024,512]{1,0:T(8,128)S(1)} custom-call(bf16[512,1024]{1,0:T(8,128)(2,1)S(1)} %copy-done, bf16[1024,512]{1,0:T(8,128)(2,1)S(1)} %copy-done.3), custom_call_target="tpu_custom_call" | custom-call | flops 1 | bytes 1000 | tf_op jit(solution)/shard_map/within/pallas_call | solution.py:323
  25.5 1.5 %collective-permute-start.3 = (bf16[256,1024]{1,0:T(8,128)(2,1)}, bf16[256,1024]{1,0:T(8,128)(2,1)S(1)}, u32[]{:S(2)}, u32[]{:S(2)}) collective-permute-start(bf16[256,1024]{1,0:T(8,128)(2,1)} %collective-permute-done.refs_0_), channel_id=1, source_target_pairs={{0,4},{4,8},{8,12},{6,2},{10,6},{14,10},{1,5},{5,9},{9,13},{7,3},{... | collective-permute-start | bytes 1572872 | tf_op jit(solution)/shard_map/ppermute | solution.py:364
  27.0 2.6 %halo_a.1 = (f32[4,8,256]{2,1,0:T(8,128)S(1)}, f32[4,8,256]{2,1,0:T(8,128)S(1)}, f32[4,1024,128]{2,1,0:T(8,128)S(1)}) custom-call(s32[4,4]{1,0:T(4,128)S(1)} %bitcast.6, s32[4]{0:T(128)S(1)} %bitcast.11, s32[1]{0:T(128)} %bitcast.2.pos_ref, ...), custom_call_target="tpu_custom_call", output_to_operand_aliasing={{0}: (7, {}), {1}: (8, {}), {2}: (9, {})} | custom-call | flops 99999997952 | bytes 1000 | tf_op jit(solution)/shard_map/halo_a/pallas_call | solution.py:323
  29.6 5.2 %collective-permute-done.5.refs_1_ = bf16[1024,128]{1,0:T(8,128)(2,1)S(1)} collective-permute-done((bf16[1024,128]{1,0:T(8,128)(2,1)S(1)}, bf16[1024,128]{1,0:T(8,128)(2,1)S(1)}, u32[]{:S(2)}, u32[]{:S(2)}) %collective-permute-start.5) | collective-permute-done | bytes 262176 | tf_op jit(solution)/shard_map/ppermute | solution.py:357
  34.8 0.2 carry.1
  35.0 3.7 %collective-permute-start.6 = (bf16[1024,128]{1,0:T(8,128)(2,1)S(1)}, bf16[1024,128]{1,0:T(8,128)(2,1)S(1)}, u32[]{:S(2)}, u32[]{:S(2)}) collective-permute-start(bf16[1024,128]{1,0:T(8,128)(2,1)S(1)} %carry.1), channel_id=1, source_target_pairs={{0,2},{2,0},{4,6},{6,4},{8,10},{10,8},{12,14},{14,12},{1,3},{3,1},... | collective-permute-start | bytes 786440 | tf_op jit(solution)/shard_map/ppermute | solution.py:357
  38.7 0.0 collective-permute-done.4.refs_0_
  38.7 2.8 %halo_b.1 = (f32[4,8,256]{2,1,0:T(8,128)S(1)}, f32[4,8,256]{2,1,0:T(8,128)S(1)}, f32[4,1024,128]{2,1,0:T(8,128)S(1)}) custom-call(s32[4,4]{1,0:T(4,128)S(1)} %bitcast.7, s32[4]{0:T(128)S(1)} %bitcast.12, s32[1]{0:T(128)} %bitcast.2.pos_ref, ...), custom_call_target="tpu_custom_call", output_to_operand_aliasing={{0}: (7, {}), {1}: (8, {}), {2}: (9, {})} | custom-call | flops 1 | bytes 1000 | tf_op jit(solution)/shard_map/halo_b/pallas_call | solution.py:323
  41.5 3.6 %collective-permute-done.3.refs_0_ = bf16[256,1024]{1,0:T(8,128)(2,1)S(1)} collective-permute-done((bf16[256,1024]{1,0:T(8,128)(2,1)}, bf16[256,1024]{1,0:T(8,128)(2,1)S(1)}, u32[]{:S(2)}, u32[]{:S(2)}) %collective-permute-start.3) | collective-permute-done | bytes 524320 | tf_op jit(solution)/shard_map/ppermute | solution.py:364
  45.0 3.8 %halo_c.1 = (f32[4,8,256]{2,1,0:T(8,128)S(1)}, f32[4,8,256]{2,1,0:T(8,128)S(1)}, f32[4,1024,128]{2,1,0:T(8,128)S(1)}) custom-call(s32[4,4]{1,0:T(4,128)S(1)} %bitcast.8, s32[4]{0:T(128)S(1)} %bitcast.13, s32[1]{0:T(128)} %bitcast.2.pos_ref, ...), custom_call_target="tpu_custom_call", output_to_operand_aliasing={{0}: (7, {}), {1}: (8, {}), {2}: (9, {})} | custom-call | flops 1 | bytes 1000 | tf_op jit(solution)/shard_map/halo_c/pallas_call | solution.py:323
  48.8 0.0 copy-start.4
  48.8 0.0 collective-permute-done.6.refs_2_
  48.8 1.5 %linear.1.refs_4_ = f32[1024,512]{1,0:T(8,128)S(1)} custom-call(s32[1]{0:T(128)} %bitcast.2.pos_ref, bf16[512,1024]{1,0:T(8,128)(2,1)S(1)} %copy-done, f32[1024,512]{1,0:T(8,128)S(1)} %within.1.n_ref, bf16[1024,128]{1,0:T(8,128)(2,1)S(1)} %collective-permute-done.2.refs_0_, bf16[1024,128]{1,0:T(8,128)(2,1)S(1)} %collective-permute-done.5.refs_1_, ...), custom_call_target="tpu_custom_call" | custom-call | flops 1 | bytes 1000 | tf_op jit(solution)/shard_map/linear/pallas_call | solution.py:323
  50.4 0.0 collective-permute-done.1.refs_0_
  50.4 0.0 copy-done.4
  50.4 5.2 %final.1 = (bf16[512,1024]{1,0:T(8,128)(2,1)}, f32[4,8,256]{2,1,0:T(8,128)S(1)}, f32[4,8,256]{2,1,0:T(8,128)S(1)}, f32[4,1024,128]{2,1,0:T(8,128)S(1)}) custom-call(s32[4,4]{1,0:T(4,128)S(1)} %bitcast.9, s32[4]{0:T(128)S(1)} %bitcast.14, s32[1]{0:T(128)} %bitcast.2.pos_ref, ...), custom_call_target="tpu_custom_call", output_to_operand_aliasing={{1}: (9, {}), {2}: (10, {}), {3}: (11, {})} | custom-call | flops 1 | bytes 1000 | tf_op jit(solution)/shard_map/final/pallas_call | solution.py:323
  (11 shorter events, 0.0 us)
Async XLA Ops:
  1.1 12.0 %copy-start.6 = (s32[1,4,4]{2,1,0:T(4,128)S(1)}, s32[1,4,4]{2,1,0:T(4,128)}, u32[]{:S(2)}) copy-start(s32[1,4,4]{2,1,0:T(4,128)} %param.10) | copy-start | bytes 196
  1.1 12.0 %copy-start.7 = (s32[1,4]{1,0:T(1,128)S(1)}, s32[1,4]{1,0:T(1,128)}, u32[]{:S(2)}) copy-start(s32[1,4]{1,0:T(1,128)} %param.11) | copy-start | bytes 52
  1.1 20.7 %collective-permute-start = (bf16[256,1024]{1,0:T(8,128)(2,1)S(1)}, bf16[256,1024]{1,0:T(8,128)(2,1)}, u32[]{:S(2)}, u32[]{:S(2)}) collective-permute-start(bf16[256,1024]{1,0:T(8,128)(2,1)S(1)} %cut.1), channel_id=1, source_target_pairs={{0,2},{2,0},{4,6},{6,4},{8,10},{10,8},{12,14},{14,12},{1,3},{3,1},... | collective-permute-start | bytes 1572872 | tf_op jit(solution)/shard_map/ppermute | solution.py:357
  7.4 15.2 %copy-start = (bf16[512,1024]{1,0:T(8,128)(2,1)S(1)}, bf16[512,1024]{1,0:T(8,128)(2,1)}, u32[]{:S(2)}) copy-start(bf16[512,1024]{1,0:T(8,128)(2,1)} %get-tuple-element.55.k_ref.refs_3_) | copy-start | bytes 3145732
  7.5 15.2 %copy-start.3 = (bf16[1024,512]{1,0:T(8,128)(2,1)S(1)}, bf16[1024,512]{1,0:T(8,128)(2,1)}, u32[]{:S(2)}) copy-start(bf16[1024,512]{1,0:T(8,128)(2,1)} %get-tuple-element.38.vt_ref) | copy-start | bytes 3145732
  7.5 11.3 %collective-permute-start.2 = (bf16[1024,128]{1,0:T(8,128)(2,1)}, bf16[1024,128]{1,0:T(8,128)(2,1)S(1)}, u32[]{:S(2)}, u32[]{:S(2)}) collective-permute-start(bf16[1024,128]{1,0:T(8,128)(2,1)} %get-tuple-element.56.s_ref), channel_id=1, source_target_pairs={{0,4},{2,6},{4,0},{6,2},{8,12},{10,14},{12,8},{14,10},{1,5},{3,7},... | collective-permute-start | bytes 786440 | tf_op jit(solution)/shard_map/ppermute | solution.py:357
  9.6 29.1 %collective-permute-start.4 = (bf16[256,1024]{1,0:T(8,128)(2,1)}, bf16[256,1024]{1,0:T(8,128)(2,1)S(1)}, u32[]{:S(2)}, u32[]{:S(2)}) collective-permute-start(bf16[256,1024]{1,0:T(8,128)(2,1)} %get-tuple-element.35), channel_id=1, source_target_pairs={{2,4},{6,8},{10,12},{4,2},{8,6},{12,10},{3,5},{7,9},{11,13},{5,3},... | collective-permute-start | bytes 1572872 | tf_op jit(solution)/shard_map/ppermute | solution.py:368
  13.0 8.7 %copy-start.8 = (bf16[256,1024]{1,0:T(8,128)(2,1)S(1)}, bf16[256,1024]{1,0:T(8,128)(2,1)}, u32[]{:S(2)}) copy-start(bf16[256,1024]{1,0:T(8,128)(2,1)} %get-tuple-element.35) | copy-start | bytes 1572868
  19.8 7.2 %copy-start.1 = (bf16[1024,1024]{1,0:T(8,128)(2,1)S(1)}, bf16[1024,1024]{1,0:T(8,128)(2,1)}, u32[]{:S(2)}) copy-start(bf16[1024,1024]{1,0:T(8,128)(2,1)} %refs_1_.7) | copy-start | bytes 6291460
  19.8 7.2 %copy-start.2 = (bf16[1024,1024]{1,0:T(8,128)(2,1)S(1)}, bf16[1024,1024]{1,0:T(8,128)(2,1)}, u32[]{:S(2)}) copy-start(bf16[1024,1024]{1,0:T(8,128)(2,1)} %refs_2_.7) | copy-start | bytes 6291460
  19.8 15.0 %collective-permute-start.5 = (bf16[1024,128]{1,0:T(8,128)(2,1)S(1)}, bf16[1024,128]{1,0:T(8,128)(2,1)S(1)}, u32[]{:S(2)}, u32[]{:S(2)}) collective-permute-start(bf16[1024,128]{1,0:T(8,128)(2,1)S(1)} %add.3), channel_id=1, source_target_pairs={{0,8},{2,10},{4,12},{6,14},{8,0},{10,2},{12,4},{14,6},{1,9},{3,11}... | collective-permute-start | bytes 786440 | tf_op jit(solution)/shard_map/ppermute | solution.py:357
  21.8 28.6 %collective-permute-start.1 = (bf16[256,1024]{1,0:T(8,128)(2,1)S(1)}, bf16[256,1024]{1,0:T(8,128)(2,1)S(1)}, u32[]{:S(2)}, u32[]{:S(2)}) collective-permute-start(bf16[256,1024]{1,0:T(8,128)(2,1)S(1)} %copy-done.8), channel_id=1, source_target_pairs={{0,2},{2,0},{4,6},{6,4},{8,10},{10,8},{12,14},{14,12},{1,3},{3,1},... | collective-permute-start | bytes 1572872 | tf_op jit(solution)/shard_map/ppermute | solution.py:357
  25.5 19.5 %collective-permute-start.3 = (bf16[256,1024]{1,0:T(8,128)(2,1)}, bf16[256,1024]{1,0:T(8,128)(2,1)S(1)}, u32[]{:S(2)}, u32[]{:S(2)}) collective-permute-start(bf16[256,1024]{1,0:T(8,128)(2,1)} %collective-permute-done.refs_0_), channel_id=1, source_target_pairs={{0,4},{4,8},{8,12},{6,2},{10,6},{14,10},{1,5},{5,9},{9,13},{7,3},{... | collective-permute-start | bytes 1572872 | tf_op jit(solution)/shard_map/ppermute | solution.py:364
  27.0 7.8 %copy-start.5 = (bf16[1024,128]{1,0:T(8,128)(2,1)S(1)}, bf16[1024,128]{1,0:T(8,128)(2,1)}, u32[]{:S(2)}) copy-start(bf16[1024,128]{1,0:T(8,128)(2,1)} %get-tuple-element.56.s_ref) | copy-start | bytes 786436
  35.0 13.8 %collective-permute-start.6 = (bf16[1024,128]{1,0:T(8,128)(2,1)S(1)}, bf16[1024,128]{1,0:T(8,128)(2,1)S(1)}, u32[]{:S(2)}, u32[]{:S(2)}) collective-permute-start(bf16[1024,128]{1,0:T(8,128)(2,1)S(1)} %carry.1), channel_id=1, source_target_pairs={{0,2},{2,0},{4,6},{6,4},{8,10},{10,8},{12,14},{14,12},{1,3},{3,1},... | collective-permute-start | bytes 786440 | tf_op jit(solution)/shard_map/ppermute | solution.py:357
  48.8 1.6 %copy-start.4 = (bf16[1024,1024]{1,0:T(8,128)(2,1)S(1)}, bf16[1024,1024]{1,0:T(8,128)(2,1)}, u32[]{:S(2)}) copy-start(bf16[1024,1024]{1,0:T(8,128)(2,1)} %refs_5_.1) | copy-start | bytes 6291460

commit v6 on v5

--- a/solution.py
+++ b/solution.py
@@ -460,7 +460,7 @@
     )
     message = swap(message, 1)
     softmax = join_halo("halo_b", softmax, [(False, half)], [after(far_b, heard[-1], softmax[0])])
-    softmax = join_halo("halo_c", softmax, [(False, 0)], [after(far_a, softmax[0])])
+    softmax = join_halo("halo_c", softmax, [(True, half)], [after(near_b, softmax[0])])
     (linear,) = call(
         functools.partial(linear_kernel, len(heard)),
         "linear",
@@ -468,8 +468,8 @@
         [((width, rows), F32)],
         smem=1,
     )
-    pieces = [(True, half)]
-    arrays = (after(near_b, linear),)
+    pieces = [(False, 0)]
+    arrays = (after(far_a, linear),)
     ins = tables + arrays + (qk_weight, value_weight, keyed, linear, out_weight) + tuple(softmax)
     first = len(ins) - 3
     update, *_ = call(

time: 54.7 us -> 54.7 us (level)
  the two profiles are of different devices: /device:TPU:4 before, /device:TPU:0 now
where the time goes in v6:
time: 54.7 us; the launch traced here: 53.9 us
  Pallas kernels  29.4 us (54%)
  starting transfers between devices  13.5 us (25%)
  waiting for transfers between devices  9.61 us (18%)
  other arithmetic  1.08 us (2%)
    pallas_call x10, Pallas kernels, call(): pl.pallas_call(kernel, name=name, in_specs=[SMEM] * smem + [pl.BlockSpec(...  29.4 us
    ppermute x5, waiting for transfers between devices, swap(): return lax.ppermute(value, 'seq', [(i, i ^ bit) for i in range(count)])  9.6 us
    ppermute x5, starting transfers between devices, swap(): return lax.ppermute(value, 'seq', [(i, i ^ bit) for i in range(count)])  7.43 us
    ppermute x1, starting transfers between devices, onward(): return lax.ppermute(value, 'seq', pairs)  5.39 us
  transfers between devices with their start and end apart: 7, of which 4 were waited for; matrix products, arithmetic and copies ran while one was open for 2% of the time, Pallas kernels for 44%

profile of v6, /device:TPU:0, one launch (start us, length us, event | category | flops | bytes accessed | tf_op | source)
XLA Modules:
  0.0 53.9 jit_solution(6276855511663301054)
XLA Ops:
  0.0 1.0 %cut.1 = bf16[256,1024]{1,0:T(8,128)(2,1)S(1)} custom-call(bf16[512,1024]{1,0:T(8,128)(2,1)} %bitcast.15), custom_call_target="tpu_custom_call" | custom-call | flops 1 | bytes 1000 | tf_op jit(solution)/shard_map/cut/pallas_call | solution.py:323
  1.1 0.0 copy-start.6
  1.1 0.0 copy-start.7
  1.1 3.0 %collective-permute-start = (bf16[256,1024]{1,0:T(8,128)(2,1)S(1)}, bf16[256,1024]{1,0:T(8,128)(2,1)}, u32[]{:S(2)}, u32[]{:S(2)}) collective-permute-start(bf16[256,1024]{1,0:T(8,128)(2,1)S(1)} %cut.1), channel_id=1, source_target_pairs={{0,2},{2,0},{4,6},{6,4},{8,10},{10,8},{12,14},{14,12},{1,3},{3,1},... | collective-permute-start | bytes 1572872 | tf_op jit(solution)/shard_map/ppermute | solution.py:357
  4.1 6.3 %own.1 = (bf16[512,1024]{1,0:T(8,128)(2,1)}, bf16[1024,512]{1,0:T(8,128)(2,1)}, bf16[256,1024]{1,0:T(8,128)(2,1)}, bf16[1024,128]{1,0:T(8,128)(2,1)}) custom-call(bf16[512,1024]{1,0:T(8,128)(2,1)} %bitcast.16, bf16[1024,1024]{1,0:T(8,128)(2,1)} %refs_1_.7, bf16[1024,1024]{1,0:T(8,128)(2,1)} %refs_2_.7), custom_call_target="tpu_custom_call" | custom-call | flops 1 | bytes 1000 | tf_op jit(solution)/shard_map/own/pallas_call | solution.py:323
  10.4 0.0 copy-start
  10.4 0.0 copy-start.3
  10.4 1.6 %collective-permute-start.1 = (bf16[1024,128]{1,0:T(8,128)(2,1)}, bf16[1024,128]{1,0:T(8,128)(2,1)S(1)}, u32[]{:S(2)}, u32[]{:S(2)}) collective-permute-start(bf16[1024,128]{1,0:T(8,128)(2,1)} %get-tuple-element.56.s_ref), channel_id=1, source_target_pairs={{0,4},{2,6},{4,0},{6,2},{8,12},{10,14},{12,8},{14,10},{1,5},{3,7},... | collective-permute-start | bytes 786440 | tf_op jit(solution)/shard_map/ppermute | solution.py:357
  12.0 0.7 %collective-permute-start.4 = (bf16[256,1024]{1,0:T(8,128)(2,1)}, bf16[256,1024]{1,0:T(8,128)(2,1)S(1)}, u32[]{:S(2)}, u32[]{:S(2)}) collective-permute-start(bf16[256,1024]{1,0:T(8,128)(2,1)} %get-tuple-element.41), channel_id=1, source_target_pairs={{2,4},{6,8},{10,12},{4,2},{8,6},{12,10},{3,5},{7,9},{11,13},{5,3},... | collective-permute-start | bytes 1572872 | tf_op jit(solution)/shard_map/ppermute | solution.py:368
  12.8 5.6 %own_attention.1 = (f32[4,8,256]{2,1,0:T(8,128)S(1)}, f32[4,8,256]{2,1,0:T(8,128)S(1)}, f32[4,1024,128]{2,1,0:T(8,128)S(1)}) custom-call(s32[4,4]{1,0:T(4,128)S(1)} %bitcast.5, s32[4]{0:T(128)S(1)} %bitcast.10, s32[1]{0:T(128)} %bitcast.2.pos_ref, bf16[512,1024]{1,0:T(8,128)(2,1)} %get-tuple-element.55.k_ref.refs_3_, bf16[1024,512]{1,0:T(8,128)(2,1)} %get-tuple-element.36.vt_ref), custom_call_target="tpu_custom_call" | custom-call | flops 1 | bytes 1000 | tf_op jit(solution)/shard_map/own_attention/pallas_call | solution.py:323
  18.4 1.6 %collective-permute-done.1.refs_0_ = bf16[1024,128]{1,0:T(8,128)(2,1)S(1)} collective-permute-done((bf16[1024,128]{1,0:T(8,128)(2,1)}, bf16[1024,128]{1,0:T(8,128)(2,1)S(1)}, u32[]{:S(2)}, u32[]{:S(2)}) %collective-permute-start.1) | collective-permute-done | bytes 262176 | tf_op jit(solution)/shard_map/ppermute | solution.py:357
  19.9 1.1 %add.3 = bf16[1024,128]{1,0:T(8,128)(2,1)S(1)} add(bf16[1024,128]{1,0:T(8,128)(2,1)} %get-tuple-element.56.s_ref, bf16[1024,128]{1,0:T(8,128)(2,1)S(1)} %collective-permute-done.1.refs_0_) | non-fusion elementwise | flops 131072 | bytes 786432 | tf_op jit(solution)/shard_map/add | solution.py:442
  21.0 0.0 copy-start.1
  21.0 0.0 copy-start.2
  21.0 2.6 %collective-permute-start.5 = (bf16[1024,128]{1,0:T(8,128)(2,1)S(1)}, bf16[1024,128]{1,0:T(8,128)(2,1)S(1)}, u32[]{:S(2)}, u32[]{:S(2)}) collective-permute-start(bf16[1024,128]{1,0:T(8,128)(2,1)S(1)} %add.3), channel_id=1, source_target_pairs={{0,8},{2,10},{4,12},{6,14},{8,0},{10,2},{12,4},{14,6},{1,9},{3,11}... | collective-permute-start | bytes 786440 | tf_op jit(solution)/shard_map/ppermute | solution.py:357
  23.7 0.0 collective-permute-done.refs_0_
  23.7 5.4 %collective-permute-start.2 = (bf16[256,1024]{1,0:T(8,128)(2,1)}, bf16[256,1024]{1,0:T(8,128)(2,1)S(1)}, u32[]{:S(2)}, u32[]{:S(2)}) collective-permute-start(bf16[256,1024]{1,0:T(8,128)(2,1)} %collective-permute-done.refs_0_), channel_id=1, source_target_pairs={{0,4},{4,8},{8,12},{6,2},{10,6},{14,10},{1,5},{5,9},{9,13},{7,3},{... | collective-permute-start | bytes 1572872 | tf_op jit(solution)/shard_map/ppermute | solution.py:364
  29.1 2.8 %within.1.n_ref = f32[1024,512]{1,0:T(8,128)S(1)} custom-call(bf16[512,1024]{1,0:T(8,128)(2,1)S(1)} %copy-done, bf16[1024,512]{1,0:T(8,128)(2,1)S(1)} %copy-done.3), custom_call_target="tpu_custom_call" | custom-call | flops 1 | bytes 1000 | tf_op jit(solution)/shard_map/within/pallas_call | solution.py:323
  31.9 0.1 collective-permute-start.3
  32.0 3.3 %halo_a.1 = (f32[4,8,256]{2,1,0:T(8,128)S(1)}, f32[4,8,256]{2,1,0:T(8,128)S(1)}, f32[4,1024,128]{2,1,0:T(8,128)S(1)}) custom-call(s32[4,4]{1,0:T(4,128)S(1)} %bitcast.6, s32[4]{0:T(128)S(1)} %bitcast.11, s32[1]{0:T(128)} %bitcast.2.pos_ref, ...), custom_call_target="tpu_custom_call", output_to_operand_aliasing={{0}: (7, {}), {1}: (8, {}), {2}: (9, {})} | custom-call | flops 99999997952 | bytes 1000 | tf_op jit(solution)/shard_map/halo_a/pallas_call | solution.py:323
  35.3 4.1 %collective-permute-done.5.refs_1_ = bf16[1024,128]{1,0:T(8,128)(2,1)S(1)} collective-permute-done((bf16[1024,128]{1,0:T(8,128)(2,1)S(1)}, bf16[1024,128]{1,0:T(8,128)(2,1)S(1)}, u32[]{:S(2)}, u32[]{:S(2)}) %collective-permute-start.5) | collective-permute-done | bytes 262176 | tf_op jit(solution)/shard_map/ppermute | solution.py:357
  39.4 0.2 carry.1
  39.6 0.1 collective-permute-start.6
  39.6 0.0 collective-permute-done.4.refs_0_
  39.6 2.1 %halo_b.1 = (f32[4,8,256]{2,1,0:T(8,128)S(1)}, f32[4,8,256]{2,1,0:T(8,128)S(1)}, f32[4,1024,128]{2,1,0:T(8,128)S(1)}) custom-call(s32[4,4]{1,0:T(4,128)S(1)} %bitcast.7, s32[4]{0:T(128)S(1)} %bitcast.12, s32[1]{0:T(128)} %bitcast.2.pos_ref, ...), custom_call_target="tpu_custom_call", output_to_operand_aliasing={{0}: (7, {}), {1}: (8, {}), {2}: (9, {})} | custom-call | flops 1 | bytes 1000 | tf_op jit(solution)/shard_map/halo_b/pallas_call | solution.py:323
  41.7 2.6 %collective-permute-done.3.refs_0_ = bf16[256,1024]{1,0:T(8,128)(2,1)S(1)} collective-permute-done((bf16[256,1024]{1,0:T(8,128)(2,1)S(1)}, bf16[256,1024]{1,0:T(8,128)(2,1)S(1)}, u32[]{:S(2)}, u32[]{:S(2)}) %collective-permute-start.3) | collective-permute-done | bytes 524320 | tf_op jit(solution)/shard_map/ppermute | solution.py:357
  44.4 2.1 %halo_c.1 = (f32[4,8,256]{2,1,0:T(8,128)S(1)}, f32[4,8,256]{2,1,0:T(8,128)S(1)}, f32[4,1024,128]{2,1,0:T(8,128)S(1)}) custom-call(s32[4,4]{1,0:T(4,128)S(1)} %bitcast.8, s32[4]{0:T(128)S(1)} %bitcast.13, s32[1]{0:T(128)} %bitcast.2.pos_ref, ...), custom_call_target="tpu_custom_call", output_to_operand_aliasing={{0}: (7, {}), {1}: (8, {}), {2}: (9, {})} | custom-call | flops 1 | bytes 1000 | tf_op jit(solution)/shard_map/halo_c/pallas_call | solution.py:323
  46.5 0.0 copy-start.4
  46.5 1.4 %collective-permute-done.6.refs_2_ = bf16[1024,128]{1,0:T(8,128)(2,1)S(1)} collective-permute-done((bf16[1024,128]{1,0:T(8,128)(2,1)S(1)}, bf16[1024,128]{1,0:T(8,128)(2,1)S(1)}, u32[]{:S(2)}, u32[]{:S(2)}) %collective-permute-start.6) | collective-permute-done | bytes 262176 | tf_op jit(solution)/shard_map/ppermute | solution.py:357
  47.8 1.5 %linear.1.refs_4_ = f32[1024,512]{1,0:T(8,128)S(1)} custom-call(s32[1]{0:T(128)} %bitcast.2.pos_ref, bf16[512,1024]{1,0:T(8,128)(2,1)S(1)} %copy-done, f32[1024,512]{1,0:T(8,128)S(1)} %within.1.n_ref, bf16[1024,128]{1,0:T(8,128)(2,1)S(1)} %collective-permute-done.1.refs_0_, bf16[1024,128]{1,0:T(8,128)(2,1)S(1)} %collective-permute-done.5.refs_1_, ...), custom_call_target="tpu_custom_call" | custom-call | flops 1 | bytes 1000 | tf_op jit(solution)/shard_map/linear/pallas_call | solution.py:323
  49.4 0.0 collective-permute-done.2.refs_0_
  49.4 4.5 %final.1 = (bf16[512,1024]{1,0:T(8,128)(2,1)}, f32[4,8,256]{2,1,0:T(8,128)S(1)}, f32[4,8,256]{2,1,0:T(8,128)S(1)}, f32[4,1024,128]{2,1,0:T(8,128)S(1)}) custom-call(s32[4,4]{1,0:T(4,128)S(1)} %bitcast.9, s32[4]{0:T(128)S(1)} %bitcast.14, s32[1]{0:T(128)} %bitcast.2.pos_ref, ...), custom_call_target="tpu_custom_call", output_to_operand_aliasing={{1}: (9, {}), {2}: (10, {}), {3}: (11, {})} | custom-call | flops 1 | bytes 1000 | tf_op jit(solution)/shard_map/final/pallas_call | solution.py:323
  (11 shorter events, 0.0 us)
Async XLA Ops:
  1.1 11.7 %copy-start.6 = (s32[1,4,4]{2,1,0:T(4,128)S(1)}, s32[1,4,4]{2,1,0:T(4,128)}, u32[]{:S(2)}) copy-start(s32[1,4,4]{2,1,0:T(4,128)} %param.10) | copy-start | bytes 196
  1.1 11.7 %copy-start.7 = (s32[1,4]{1,0:T(1,128)S(1)}, s32[1,4]{1,0:T(1,128)}, u32[]{:S(2)}) copy-start(s32[1,4]{1,0:T(1,128)} %param.11) | copy-start | bytes 52
  1.1 22.6 %collective-permute-start = (bf16[256,1024]{1,0:T(8,128)(2,1)S(1)}, bf16[256,1024]{1,0:T(8,128)(2,1)}, u32[]{:S(2)}, u32[]{:S(2)}) collective-permute-start(bf16[256,1024]{1,0:T(8,128)(2,1)S(1)} %cut.1), channel_id=1, source_target_pairs={{0,2},{2,0},{4,6},{6,4},{8,10},{10,8},{12,14},{14,12},{1,3},{3,1},... | collective-permute-start | bytes 1572872 | tf_op jit(solution)/shard_map/ppermute | solution.py:357
  10.4 18.7 %copy-start = (bf16[512,1024]{1,0:T(8,128)(2,1)S(1)}, bf16[512,1024]{1,0:T(8,128)(2,1)}, u32[]{:S(2)}) copy-start(bf16[512,1024]{1,0:T(8,128)(2,1)} %get-tuple-element.55.k_ref.refs_3_) | copy-start | bytes 3145732
  10.4 18.7 %copy-start.3 = (bf16[1024,512]{1,0:T(8,128)(2,1)S(1)}, bf16[1024,512]{1,0:T(8,128)(2,1)}, u32[]{:S(2)}) copy-start(bf16[1024,512]{1,0:T(8,128)(2,1)} %get-tuple-element.36.vt_ref) | copy-start | bytes 3145732
  10.4 9.5 %collective-permute-start.1 = (bf16[1024,128]{1,0:T(8,128)(2,1)}, bf16[1024,128]{1,0:T(8,128)(2,1)S(1)}, u32[]{:S(2)}, u32[]{:S(2)}) collective-permute-start(bf16[1024,128]{1,0:T(8,128)(2,1)} %get-tuple-element.56.s_ref), channel_id=1, source_target_pairs={{0,4},{2,6},{4,0},{6,2},{8,12},{10,14},{12,8},{14,10},{1,5},{3,7},... | collective-permute-start | bytes 786440 | tf_op jit(solution)/shard_map/ppermute | solution.py:357
  12.0 27.6 %collective-permute-start.4 = (bf16[256,1024]{1,0:T(8,128)(2,1)}, bf16[256,1024]{1,0:T(8,128)(2,1)S(1)}, u32[]{:S(2)}, u32[]{:S(2)}) collective-permute-start(bf16[256,1024]{1,0:T(8,128)(2,1)} %get-tuple-element.41), channel_id=1, source_target_pairs={{2,4},{6,8},{10,12},{4,2},{8,6},{12,10},{3,5},{7,9},{11,13},{5,3},... | collective-permute-start | bytes 1572872 | tf_op jit(solution)/shard_map/ppermute | solution.py:368
  19.9 12.0 %copy-start.8 = (bf16[256,1024]{1,0:T(8,128)(2,1)S(1)}, bf16[256,1024]{1,0:T(8,128)(2,1)}, u32[]{:S(2)}) copy-start(bf16[256,1024]{1,0:T(8,128)(2,1)} %get-tuple-element.41) | copy-start | bytes 1572868
  21.0 11.0 %copy-start.1 = (bf16[1024,1024]{1,0:T(8,128)(2,1)S(1)}, bf16[1024,1024]{1,0:T(8,128)(2,1)}, u32[]{:S(2)}) copy-start(bf16[1024,1024]{1,0:T(8,128)(2,1)} %refs_1_.7) | copy-start | bytes 6291460
  21.0 11.0 %copy-start.2 = (bf16[1024,1024]{1,0:T(8,128)(2,1)S(1)}, bf16[1024,1024]{1,0:T(8,128)(2,1)}, u32[]{:S(2)}) copy-start(bf16[1024,1024]{1,0:T(8,128)(2,1)} %refs_2_.7) | copy-start | bytes 6291460
  21.0 18.3 %collective-permute-start.5 = (bf16[1024,128]{1,0:T(8,128)(2,1)S(1)}, bf16[1024,128]{1,0:T(8,128)(2,1)S(1)}, u32[]{:S(2)}, u32[]{:S(2)}) collective-permute-start(bf16[1024,128]{1,0:T(8,128)(2,1)S(1)} %add.3), channel_id=1, source_target_pairs={{0,8},{2,10},{4,12},{6,14},{8,0},{10,2},{12,4},{14,6},{1,9},{3,11}... | collective-permute-start | bytes 786440 | tf_op jit(solution)/shard_map/ppermute | solution.py:357
  23.7 25.7 %collective-permute-start.2 = (bf16[256,1024]{1,0:T(8,128)(2,1)}, bf16[256,1024]{1,0:T(8,128)(2,1)S(1)}, u32[]{:S(2)}, u32[]{:S(2)}) collective-permute-start(bf16[256,1024]{1,0:T(8,128)(2,1)} %collective-permute-done.refs_0_), channel_id=1, source_target_pairs={{0,4},{4,8},{8,12},{6,2},{10,6},{14,10},{1,5},{5,9},{9,13},{7,3},{... | collective-permute-start | bytes 1572872 | tf_op jit(solution)/shard_map/ppermute | solution.py:364
  31.9 12.5 %collective-permute-start.3 = (bf16[256,1024]{1,0:T(8,128)(2,1)S(1)}, bf16[256,1024]{1,0:T(8,128)(2,1)S(1)}, u32[]{:S(2)}, u32[]{:S(2)}) collective-permute-start(bf16[256,1024]{1,0:T(8,128)(2,1)S(1)} %copy-done.8), channel_id=1, source_target_pairs={{0,2},{2,0},{4,6},{6,4},{8,10},{10,8},{12,14},{14,12},{1,3},{3,1},... | collective-permute-start | bytes 1572872 | tf_op jit(solution)/shard_map/ppermute | solution.py:357
  32.0 7.4 %copy-start.5 = (bf16[1024,128]{1,0:T(8,128)(2,1)S(1)}, bf16[1024,128]{1,0:T(8,128)(2,1)}, u32[]{:S(2)}) copy-start(bf16[1024,128]{1,0:T(8,128)(2,1)} %get-tuple-element.56.s_ref) | copy-start | bytes 786436
  39.6 8.3 %collective-permute-start.6 = (bf16[1024,128]{1,0:T(8,128)(2,1)S(1)}, bf16[1024,128]{1,0:T(8,128)(2,1)S(1)}, u32[]{:S(2)}, u32[]{:S(2)}) collective-permute-start(bf16[1024,128]{1,0:T(8,128)(2,1)S(1)} %carry.1), channel_id=1, source_target_pairs={{0,2},{2,0},{4,6},{6,4},{8,10},{10,8},{12,14},{14,12},{1,3},{3,1},... | collective-permute-start | bytes 786440 | tf_op jit(solution)/shard_map/ppermute | solution.py:357
  46.5 2.9 %copy-start.4 = (bf16[1024,1024]{1,0:T(8,128)(2,1)S(1)}, bf16[1024,1024]{1,0:T(8,128)(2,1)}, u32[]{:S(2)}) copy-start(bf16[1024,1024]{1,0:T(8,128)(2,1)} %refs_5_.1) | copy-start | bytes 6291460

commit v7 on v6

--- a/solution.py
+++ b/solution.py
@@ -102,7 +102,7 @@
         n_ref[cols, half:] = dot_nn(v0, a01) + dot_nn(v1, a11)
         return carry
 
-    lax.fori_loop(0, HL, head, 0, unroll=2)
+    lax.fori_loop(0, HL, head, 0, unroll=8)
 
 
 def set_bits(pos_ref, count):
@@ -132,7 +132,7 @@
         o_ref[cols, :] = n * lax.rsqrt(mean + 1e-06)
         return carry
 
-    lax.fori_loop(0, HL, head, 0, unroll=2)
+    lax.fori_loop(0, HL, head, 0, unroll=8)
 
 
 def listed(list_ref, count_ref, qb, block):
@@ -239,7 +239,10 @@
     lax.fori_loop(0, list_ref.shape[0], query, 0)
 
 
-def own_attention_kernel(size, list_ref, count_ref, pos_ref, k_ref, vt_ref, m_ref, l_ref, acc_ref, found_ref):
+def own_attention_kernel(
+    size, list_ref, count_ref, pos_ref, k_ref, vt_ref, s_ref, m_ref, l_ref, acc_ref, kept_ref, found_ref
+):
+    kept_ref[...] = s_ref[...]
     queries = list_ref.shape[0]
     blocks = [pos_ref[0] * queries + kb for kb in range(queries)]
     attend_listed(
@@ -428,15 +431,15 @@
 
     heard = [halves(state, 2)]
     shapes = [((blocks, H // 2, 2 * size), F32)] * 2 + [((blocks, width, size), F32)]
-    softmax = call(
+    *softmax, kept = call(
         functools.partial(own_attention_kernel, size),
         "own_attention",
-        tables + (in_hbm(keyed), in_hbm(values_t)),
-        shapes,
+        tables + (in_hbm(keyed), in_hbm(values_t), in_hbm(state)),
+        shapes + [((width, DL), BF16)],
         smem=3,
         scratch=(pltpu.SMEM((blocks + 1,), jnp.int32),),
     )
-    total = state
+    total = kept
     stride = 4
     while stride < count:
         total = total + after(heard[-1], softmax[0])

time: 54.7 us -> 53.2 us (0.973)
  waiting for transfers between devices: 9.61 us -> 7.02 us
  Pallas kernels: 29.4 us -> 30.5 us
  other arithmetic: 1.08 us -> 0.07 us
  starting transfers between devices: 13.5 us -> 14.3 us
    ppermute x5, waiting for transfers between devices: 9.6 us -> 7.02 us  [swap(): return lax.ppermute(value, 'seq', [(i, i ^ bit) for i in range(count)])]
    pallas_call x10, Pallas kernels: 29.4 us -> 30.5 us  [call(): pl.pallas_call(kernel, name=name, in_specs=[SMEM] * smem + [pl.BlockSpec(...]
    add x1, other arithmetic: 1.08 us -> 0.07 us  [on_device(): total = total + after(heard[-1], softmax[0])]
    ppermute x1, starting transfers between devices: 5.39 us -> 6.22 us  [onward(): return lax.ppermute(value, 'seq', pairs)]
  transfers between devices with their start and end apart: 7 -> 7, of which waited for: 4 -> 4; matrix products, arithmetic and copies ran while one was open for 2% -> 0% of each run, Pallas kernels for 44% -> 48%
where the time goes in v7:
time: 53.2 us; the launch traced here: 52.2 us
  Pallas kernels  30.5 us (57%)
  starting transfers between devices  14.3 us (27%)
  waiting for transfers between devices  7.02 us (13%)
    pallas_call x10, Pallas kernels, call(): pl.pallas_call(kernel, name=name, in_specs=[SMEM] * smem + [pl.BlockSpec(...  30.5 us
    ppermute x5, starting transfers between devices, swap(): return lax.ppermute(value, 'seq', [(i, i ^ bit) for i in range(count)])  7.43 us
    ppermute x5, waiting for transfers between devices, swap(): return lax.ppermute(value, 'seq', [(i, i ^ bit) for i in range(count)])  7.02 us
    ppermute x1, starting transfers between devices, onward(): return lax.ppermute(value, 'seq', pairs)  6.22 us
  transfers between devices with their start and end apart: 7, of which 4 were waited for; matrix products, arithmetic and copies ran while one was open for 0% of the time, Pallas kernels for 48%

profile of v7, /device:TPU:0, one launch (start us, length us, event | category | flops | bytes accessed | tf_op | source)
XLA Modules:
  0.0 52.2 jit_solution(18374058611191547752)
XLA Ops:
  0.0 1.0 %cut.1 = bf16[256,1024]{1,0:T(8,128)(2,1)S(1)} custom-call(bf16[512,1024]{1,0:T(8,128)(2,1)} %bitcast.15), custom_call_target="tpu_custom_call" | custom-call | flops 1 | bytes 1000 | tf_op jit(solution)/shard_map/cut/pallas_call | solution.py:326
  1.1 0.0 copy-start.6
  1.1 0.0 copy-start.7
  1.1 3.0 %collective-permute-start = (bf16[256,1024]{1,0:T(8,128)(2,1)S(1)}, bf16[256,1024]{1,0:T(8,128)(2,1)}, u32[]{:S(2)}, u32[]{:S(2)}) collective-permute-start(bf16[256,1024]{1,0:T(8,128)(2,1)S(1)} %cut.1), channel_id=1, source_target_pairs={{0,2},{2,0},{4,6},{6,4},{8,10},{10,8},{12,14},{14,12},{1,3},{3,1},... | collective-permute-start | bytes 1572872 | tf_op jit(solution)/shard_map/ppermute | solution.py:360
  4.1 6.3 %own.1 = (bf16[512,1024]{1,0:T(8,128)(2,1)}, bf16[1024,512]{1,0:T(8,128)(2,1)}, bf16[256,1024]{1,0:T(8,128)(2,1)}, bf16[1024,128]{1,0:T(8,128)(2,1)}) custom-call(bf16[512,1024]{1,0:T(8,128)(2,1)} %bitcast.16, bf16[1024,1024]{1,0:T(8,128)(2,1)} %refs_1_.7, bf16[1024,1024]{1,0:T(8,128)(2,1)} %refs_2_.7), custom_call_target="tpu_custom_call" | custom-call | flops 1 | bytes 1000 | tf_op jit(solution)/shard_map/own/pallas_call | solution.py:326
  10.4 0.0 copy-start
  10.4 1.6 %collective-permute-start.1 = (bf16[1024,128]{1,0:T(8,128)(2,1)}, bf16[1024,128]{1,0:T(8,128)(2,1)S(1)}, u32[]{:S(2)}, u32[]{:S(2)}) collective-permute-start(bf16[1024,128]{1,0:T(8,128)(2,1)} %get-tuple-element.58.s_ref), channel_id=1, source_target_pairs={{0,4},{2,6},{4,0},{6,2},{8,12},{10,14},{12,8},{14,10},{1,5},{3,7},... | collective-permute-start | bytes 786440 | tf_op jit(solution)/shard_map/ppermute | solution.py:360
  12.0 0.7 %collective-permute-start.4 = (bf16[256,1024]{1,0:T(8,128)(2,1)}, bf16[256,1024]{1,0:T(8,128)(2,1)S(1)}, u32[]{:S(2)}, u32[]{:S(2)}) collective-permute-start(bf16[256,1024]{1,0:T(8,128)(2,1)} %get-tuple-element.43), channel_id=1, source_target_pairs={{2,4},{6,8},{10,12},{4,2},{8,6},{12,10},{3,5},{7,9},{11,13},{5,3},... | collective-permute-start | bytes 1572872 | tf_op jit(solution)/shard_map/ppermute | solution.py:371
  12.8 6.3 %own_attention.1 = (f32[4,8,256]{2,1,0:T(8,128)S(1)}, f32[4,8,256]{2,1,0:T(8,128)S(1)}, f32[4,1024,128]{2,1,0:T(8,128)S(1)}, bf16[1024,128]{1,0:T(8,128)(2,1)S(1)}) custom-call(s32[4,4]{1,0:T(4,128)S(1)} %bitcast.5, s32[4]{0:T(128)S(1)} %bitcast.10, s32[1]{0:T(128)} %bitcast.2.pos_ref, bf16[512,1024]{1,0:T(8,128)(2,1)} %get-tuple-element.57.k_ref.refs_3_, ...), custom_call_target="tpu_custom_call" | custom-call | flops 1 | bytes 1000 | tf_op jit(solution)/shard_map/own_attention/pallas_call | solution.py:326
  19.1 0.8 %collective-permute-done.1.refs_0_ = bf16[1024,128]{1,0:T(8,128)(2,1)S(1)} collective-permute-done((bf16[1024,128]{1,0:T(8,128)(2,1)}, bf16[1024,128]{1,0:T(8,128)(2,1)S(1)}, u32[]{:S(2)}, u32[]{:S(2)}) %collective-permute-start.1) | collective-permute-done | bytes 262176 | tf_op jit(solution)/shard_map/ppermute | solution.py:360
  19.9 0.1 add.3
  20.0 0.0 copy-start.1
  20.0 0.0 copy-start.2
  20.0 2.6 %collective-permute-start.5 = (bf16[1024,128]{1,0:T(8,128)(2,1)S(1)}, bf16[1024,128]{1,0:T(8,128)(2,1)S(1)}, u32[]{:S(2)}, u32[]{:S(2)}) collective-permute-start(bf16[1024,128]{1,0:T(8,128)(2,1)S(1)} %add.3), channel_id=1, source_target_pairs={{0,8},{2,10},{4,12},{6,14},{8,0},{10,2},{12,4},{14,6},{1,9},{3,11}... | collective-permute-start | bytes 786440 | tf_op jit(solution)/shard_map/ppermute | solution.py:360
  22.7 0.0 collective-permute-done.refs_0_
  22.7 6.2 %collective-permute-start.2 = (bf16[256,1024]{1,0:T(8,128)(2,1)}, bf16[256,1024]{1,0:T(8,128)(2,1)S(1)}, u32[]{:S(2)}, u32[]{:S(2)}) collective-permute-start(bf16[256,1024]{1,0:T(8,128)(2,1)} %collective-permute-done.refs_0_), channel_id=1, source_target_pairs={{0,4},{4,8},{8,12},{6,2},{10,6},{14,10},{1,5},{5,9},{9,13},{7,3},{... | collective-permute-start | bytes 1572872 | tf_op jit(solution)/shard_map/ppermute | solution.py:367
  28.9 0.0 copy-done
  28.9 2.0 %within.1.n_ref = f32[1024,512]{1,0:T(8,128)S(1)} custom-call(bf16[512,1024]{1,0:T(8,128)(2,1)S(1)} %copy-done, bf16[1024,512]{1,0:T(8,128)(2,1)S(1)} %copy-done.3), custom_call_target="tpu_custom_call" | custom-call | flops 1 | bytes 1000 | tf_op jit(solution)/shard_map/within/pallas_call | solution.py:326
  31.0 0.1 collective-permute-start.3
  31.1 4.1 %halo_a.1 = (f32[4,8,256]{2,1,0:T(8,128)S(1)}, f32[4,8,256]{2,1,0:T(8,128)S(1)}, f32[4,1024,128]{2,1,0:T(8,128)S(1)}) custom-call(s32[4,4]{1,0:T(4,128)S(1)} %bitcast.6, s32[4]{0:T(128)S(1)} %bitcast.11, s32[1]{0:T(128)} %bitcast.2.pos_ref, ...), custom_call_target="tpu_custom_call", output_to_operand_aliasing={{0}: (7, {}), {1}: (8, {}), {2}: (9, {})} | custom-call | flops 99999997952 | bytes 1000 | tf_op jit(solution)/shard_map/halo_a/pallas_call | solution.py:326
  35.2 4.2 %collective-permute-done.5.refs_1_ = bf16[1024,128]{1,0:T(8,128)(2,1)S(1)} collective-permute-done((bf16[1024,128]{1,0:T(8,128)(2,1)S(1)}, bf16[1024,128]{1,0:T(8,128)(2,1)S(1)}, u32[]{:S(2)}, u32[]{:S(2)}) %collective-permute-start.5) | collective-permute-done | bytes 262176 | tf_op jit(solution)/shard_map/ppermute | solution.py:360
  39.4 0.2 carry.1
  39.6 0.1 collective-permute-start.6
  39.6 0.0 collective-permute-done.4.refs_0_
  39.6 2.1 %halo_b.1 = (f32[4,8,256]{2,1,0:T(8,128)S(1)}, f32[4,8,256]{2,1,0:T(8,128)S(1)}, f32[4,1024,128]{2,1,0:T(8,128)S(1)}) custom-call(s32[4,4]{1,0:T(4,128)S(1)} %bitcast.7, s32[4]{0:T(128)S(1)} %bitcast.12, s32[1]{0:T(128)} %bitcast.2.pos_ref, ...), custom_call_target="tpu_custom_call", output_to_operand_aliasing={{0}: (7, {}), {1}: (8, {}), {2}: (9, {})} | custom-call | flops 1 | bytes 1000 | tf_op jit(solution)/shard_map/halo_b/pallas_call | solution.py:326
  41.7 0.6 %collective-permute-done.3.refs_0_ = bf16[256,1024]{1,0:T(8,128)(2,1)S(1)} collective-permute-done((bf16[256,1024]{1,0:T(8,128)(2,1)S(1)}, bf16[256,1024]{1,0:T(8,128)(2,1)S(1)}, u32[]{:S(2)}, u32[]{:S(2)}) %collective-permute-start.3) | collective-permute-done | bytes 524320 | tf_op jit(solution)/shard_map/ppermute | solution.py:360
  42.4 2.8 %halo_c.1 = (f32[4,8,256]{2,1,0:T(8,128)S(1)}, f32[4,8,256]{2,1,0:T(8,128)S(1)}, f32[4,1024,128]{2,1,0:T(8,128)S(1)}) custom-call(s32[4,4]{1,0:T(4,128)S(1)} %bitcast.8, s32[4]{0:T(128)S(1)} %bitcast.13, s32[1]{0:T(128)} %bitcast.2.pos_ref, ...), custom_call_target="tpu_custom_call", output_to_operand_aliasing={{0}: (7, {}), {1}: (8, {}), {2}: (9, {})} | custom-call | flops 1 | bytes 1000 | tf_op jit(solution)/shard_map/halo_c/pallas_call | solution.py:326
  45.1 0.0 copy-start.4
  45.1 1.4 %collective-permute-done.6.refs_2_ = bf16[1024,128]{1,0:T(8,128)(2,1)S(1)} collective-permute-done((bf16[1024,128]{1,0:T(8,128)(2,1)S(1)}, bf16[1024,128]{1,0:T(8,128)(2,1)S(1)}, u32[]{:S(2)}, u32[]{:S(2)}) %collective-permute-start.6) | collective-permute-done | bytes 262176 | tf_op jit(solution)/shard_map/ppermute | solution.py:360
  46.5 1.3 %linear.1.refs_4_ = f32[1024,512]{1,0:T(8,128)S(1)} custom-call(s32[1]{0:T(128)} %bitcast.2.pos_ref, bf16[512,1024]{1,0:T(8,128)(2,1)S(1)} %copy-done, f32[1024,512]{1,0:T(8,128)S(1)} %within.1.n_ref, bf16[1024,128]{1,0:T(8,128)(2,1)S(1)} %collective-permute-done.1.refs_0_, bf16[1024,128]{1,0:T(8,128)(2,1)S(1)} %collective-permute-done.5.refs_1_, ...), custom_call_target="tpu_custom_call" | custom-call | flops 1 | bytes 1000 | tf_op jit(solution)/shard_map/linear/pallas_call | solution.py:326
  47.8 0.0 collective-permute-done.2.refs_0_
  47.8 4.4 %final.1 = (bf16[512,1024]{1,0:T(8,128)(2,1)}, f32[4,8,256]{2,1,0:T(8,128)S(1)}, f32[4,8,256]{2,1,0:T(8,128)S(1)}, f32[4,1024,128]{2,1,0:T(8,128)S(1)}) custom-call(s32[4,4]{1,0:T(4,128)S(1)} %bitcast.9, s32[4]{0:T(128)S(1)} %bitcast.14, s32[1]{0:T(128)} %bitcast.2.pos_ref, ...), custom_call_target="tpu_custom_call", output_to_operand_aliasing={{1}: (9, {}), {2}: (10, {}), {3}: (11, {})} | custom-call | flops 1 | bytes 1000 | tf_op jit(solution)/shard_map/final/pallas_call | solution.py:326
  (11 shorter events, 0.0 us)
Async XLA Ops:
  1.1 11.7 %copy-start.6 = (s32[1,4,4]{2,1,0:T(4,128)S(1)}, s32[1,4,4]{2,1,0:T(4,128)}, u32[]{:S(2)}) copy-start(s32[1,4,4]{2,1,0:T(4,128)} %param.10) | copy-start | bytes 196
  1.1 11.7 %copy-start.7 = (s32[1,4]{1,0:T(1,128)S(1)}, s32[1,4]{1,0:T(1,128)}, u32[]{:S(2)}) copy-start(s32[1,4]{1,0:T(1,128)} %param.11) | copy-start | bytes 52
  1.1 21.6 %collective-permute-start = (bf16[256,1024]{1,0:T(8,128)(2,1)S(1)}, bf16[256,1024]{1,0:T(8,128)(2,1)}, u32[]{:S(2)}, u32[]{:S(2)}) collective-permute-start(bf16[256,1024]{1,0:T(8,128)(2,1)S(1)} %cut.1), channel_id=1, source_target_pairs={{0,2},{2,0},{4,6},{6,4},{8,10},{10,8},{12,14},{14,12},{1,3},{3,1},... | collective-permute-start | bytes 1572872 | tf_op jit(solution)/shard_map/ppermute | solution.py:360
  10.4 18.5 %copy-start = (bf16[512,1024]{1,0:T(8,128)(2,1)S(1)}, bf16[512,1024]{1,0:T(8,128)(2,1)}, u32[]{:S(2)}) copy-start(bf16[512,1024]{1,0:T(8,128)(2,1)} %get-tuple-element.57.k_ref.refs_3_) | copy-start | bytes 3145732
  10.4 18.5 %copy-start.3 = (bf16[1024,512]{1,0:T(8,128)(2,1)S(1)}, bf16[1024,512]{1,0:T(8,128)(2,1)}, u32[]{:S(2)}) copy-start(bf16[1024,512]{1,0:T(8,128)(2,1)} %get-tuple-element.36.vt_ref) | copy-start | bytes 3145732
  10.4 9.5 %collective-permute-start.1 = (bf16[1024,128]{1,0:T(8,128)(2,1)}, bf16[1024,128]{1,0:T(8,128)(2,1)S(1)}, u32[]{:S(2)}, u32[]{:S(2)}) collective-permute-start(bf16[1024,128]{1,0:T(8,128)(2,1)} %get-tuple-element.58.s_ref), channel_id=1, source_target_pairs={{0,4},{2,6},{4,0},{6,2},{8,12},{10,14},{12,8},{14,10},{1,5},{3,7},... | collective-permute-start | bytes 786440 | tf_op jit(solution)/shard_map/ppermute | solution.py:360
  12.0 27.6 %collective-permute-start.4 = (bf16[256,1024]{1,0:T(8,128)(2,1)}, bf16[256,1024]{1,0:T(8,128)(2,1)S(1)}, u32[]{:S(2)}, u32[]{:S(2)}) collective-permute-start(bf16[256,1024]{1,0:T(8,128)(2,1)} %get-tuple-element.43), channel_id=1, source_target_pairs={{2,4},{6,8},{10,12},{4,2},{8,6},{12,10},{3,5},{7,9},{11,13},{5,3},... | collective-permute-start | bytes 1572872 | tf_op jit(solution)/shard_map/ppermute | solution.py:371
  19.9 11.0 %copy-start.8 = (bf16[256,1024]{1,0:T(8,128)(2,1)S(1)}, bf16[256,1024]{1,0:T(8,128)(2,1)}, u32[]{:S(2)}) copy-start(bf16[256,1024]{1,0:T(8,128)(2,1)} %get-tuple-element.43) | copy-start | bytes 1572868
  20.0 11.0 %copy-start.1 = (bf16[1024,1024]{1,0:T(8,128)(2,1)S(1)}, bf16[1024,1024]{1,0:T(8,128)(2,1)}, u32[]{:S(2)}) copy-start(bf16[1024,1024]{1,0:T(8,128)(2,1)} %refs_1_.7) | copy-start | bytes 6291460
  20.0 11.0 %copy-start.2 = (bf16[1024,1024]{1,0:T(8,128)(2,1)S(1)}, bf16[1024,1024]{1,0:T(8,128)(2,1)}, u32[]{:S(2)}) copy-start(bf16[1024,1024]{1,0:T(8,128)(2,1)} %refs_2_.7) | copy-start | bytes 6291460
  20.0 19.3 %collective-permute-start.5 = (bf16[1024,128]{1,0:T(8,128)(2,1)S(1)}, bf16[1024,128]{1,0:T(8,128)(2,1)S(1)}, u32[]{:S(2)}, u32[]{:S(2)}) collective-permute-start(bf16[1024,128]{1,0:T(8,128)(2,1)S(1)} %add.3), channel_id=1, source_target_pairs={{0,8},{2,10},{4,12},{6,14},{8,0},{10,2},{12,4},{14,6},{1,9},{3,11}... | collective-permute-start | bytes 786440 | tf_op jit(solution)/shard_map/ppermute | solution.py:360
  22.7 25.1 %collective-permute-start.2 = (bf16[256,1024]{1,0:T(8,128)(2,1)}, bf16[256,1024]{1,0:T(8,128)(2,1)S(1)}, u32[]{:S(2)}, u32[]{:S(2)}) collective-permute-start(bf16[256,1024]{1,0:T(8,128)(2,1)} %collective-permute-done.refs_0_), channel_id=1, source_target_pairs={{0,4},{4,8},{8,12},{6,2},{10,6},{14,10},{1,5},{5,9},{9,13},{7,3},{... | collective-permute-start | bytes 1572872 | tf_op jit(solution)/shard_map/ppermute | solution.py:367
  31.0 11.4 %collective-permute-start.3 = (bf16[256,1024]{1,0:T(8,128)(2,1)S(1)}, bf16[256,1024]{1,0:T(8,128)(2,1)S(1)}, u32[]{:S(2)}, u32[]{:S(2)}) collective-permute-start(bf16[256,1024]{1,0:T(8,128)(2,1)S(1)} %copy-done.8), channel_id=1, source_target_pairs={{0,2},{2,0},{4,6},{6,4},{8,10},{10,8},{12,14},{14,12},{1,3},{3,1},... | collective-permute-start | bytes 1572872 | tf_op jit(solution)/shard_map/ppermute | solution.py:360
  31.1 8.3 %copy-start.5 = (bf16[1024,128]{1,0:T(8,128)(2,1)S(1)}, bf16[1024,128]{1,0:T(8,128)(2,1)}, u32[]{:S(2)}) copy-start(bf16[1024,128]{1,0:T(8,128)(2,1)} %get-tuple-element.58.s_ref) | copy-start | bytes 786436
  39.6 7.0 %collective-permute-start.6 = (bf16[1024,128]{1,0:T(8,128)(2,1)S(1)}, bf16[1024,128]{1,0:T(8,128)(2,1)S(1)}, u32[]{:S(2)}, u32[]{:S(2)}) collective-permute-start(bf16[1024,128]{1,0:T(8,128)(2,1)S(1)} %carry.1), channel_id=1, source_target_pairs={{0,2},{2,0},{4,6},{6,4},{8,10},{10,8},{12,14},{14,12},{1,3},{3,1},... | collective-permute-start | bytes 786440 | tf_op jit(solution)/shard_map/ppermute | solution.py:360
  45.1 2.7 %copy-start.4 = (bf16[1024,1024]{1,0:T(8,128)(2,1)S(1)}, bf16[1024,1024]{1,0:T(8,128)(2,1)}, u32[]{:S(2)}) copy-start(bf16[1024,1024]{1,0:T(8,128)(2,1)} %refs_5_.1) | copy-start | bytes 6291460

commit v8 on v7

--- a/solution.py
+++ b/solution.py
@@ -259,11 +259,13 @@
     blocks = []
     for (near, first), ref in zip(pieces, piece_refs):
         rows = ref.shape[0]
-        x_ref[row : row + rows, :] = ref[...]
+        if len(pieces) > 1:
+            x_ref[row : row + rows, :] = ref[...]
         row += rows
         run = pos + step if near else pos - step
         blocks += [run * queries + first + i for i in range(rows // size)]
-    project(x_ref[...], wk_ref, wv_ref, k_ref, vt_ref)
+    x = piece_refs[0][...] if len(pieces) == 1 else x_ref[...]
+    project(x, wk_ref, wv_ref, k_ref, vt_ref)
     attend_listed(
         False, size, blocks, list_ref, count_ref, found_ref, q_ref, k_ref, vt_ref, *state
     )

time: 53.2 us -> 53.4 us (level)
  waiting for transfers between devices: 7.02 us -> 8.85 us
  Pallas kernels: 30.5 us -> 28.8 us
    ppermute x5, waiting for transfers between devices: 7.02 us -> 8.85 us  [swap(): return lax.ppermute(value, 'seq', [(i, i ^ bit) for i in range(count)])]
    pallas_call x10, Pallas kernels: 30.5 us -> 28.8 us  [call(): pl.pallas_call(kernel, name=name, in_specs=[SMEM] * smem + [pl.BlockSpec(...]
  transfers between devices with their start and end apart: 7 -> 7, of which waited for: 4 -> 4; matrix products, arithmetic and copies ran while one was open for 0% -> 0% of each run, Pallas kernels for 48% -> 45%
where the time goes in v8:
time: 53.4 us; the launch traced here: 52.4 us
  Pallas kernels  28.8 us (54%)
  starting transfers between devices  14.3 us (27%)
  waiting for transfers between devices  8.85 us (17%)
    pallas_call x10, Pallas kernels, call(): pl.pallas_call(kernel, name=name, in_specs=[SMEM] * smem + [pl.BlockSpec(...  28.8 us
    ppermute x5, waiting for transfers between devices, swap(): return lax.ppermute(value, 'seq', [(i, i ^ bit) for i in range(count)])  8.85 us
    ppermute x5, starting transfers between devices, swap(): return lax.ppermute(value, 'seq', [(i, i ^ bit) for i in range(count)])  7.55 us
    ppermute x1, starting transfers between devices, onward(): return lax.ppermute(value, 'seq', pairs)  6.1 us
  transfers between devices with their start and end apart: 7, of which 4 were waited for; matrix products, arithmetic and copies ran while one was open for 0% of the time, Pallas kernels for 45%

profile of v8, /device:TPU:0, one launch (start us, length us, event | category | flops | bytes accessed | tf_op | source)
XLA Modules:
  0.0 52.4 jit_solution(18374058611191547752)
XLA Ops:
  0.0 1.0 %cut.1 = bf16[256,1024]{1,0:T(8,128)(2,1)S(1)} custom-call(bf16[512,1024]{1,0:T(8,128)(2,1)} %bitcast.15), custom_call_target="tpu_custom_call" | custom-call | flops 1 | bytes 1000 | tf_op jit(solution)/shard_map/cut/pallas_call | solution.py:328
  1.1 0.0 copy-start.6
  1.1 0.0 copy-start.7
  1.1 3.0 %collective-permute-start = (bf16[256,1024]{1,0:T(8,128)(2,1)S(1)}, bf16[256,1024]{1,0:T(8,128)(2,1)}, u32[]{:S(2)}, u32[]{:S(2)}) collective-permute-start(bf16[256,1024]{1,0:T(8,128)(2,1)S(1)} %cut.1), channel_id=1, source_target_pairs={{0,2},{2,0},{4,6},{6,4},{8,10},{10,8},{12,14},{14,12},{1,3},{3,1},... | collective-permute-start | bytes 1572872 | tf_op jit(solution)/shard_map/ppermute | solution.py:362
  4.1 6.3 %own.1 = (bf16[512,1024]{1,0:T(8,128)(2,1)}, bf16[1024,512]{1,0:T(8,128)(2,1)}, bf16[256,1024]{1,0:T(8,128)(2,1)}, bf16[1024,128]{1,0:T(8,128)(2,1)}) custom-call(bf16[512,1024]{1,0:T(8,128)(2,1)} %bitcast.16, bf16[1024,1024]{1,0:T(8,128)(2,1)} %refs_1_.7, bf16[1024,1024]{1,0:T(8,128)(2,1)} %refs_2_.7), custom_call_target="tpu_custom_call" | custom-call | flops 1 | bytes 1000 | tf_op jit(solution)/shard_map/own/pallas_call | solution.py:328
  10.4 0.0 copy-start
  10.4 1.6 %collective-permute-start.1 = (bf16[1024,128]{1,0:T(8,128)(2,1)}, bf16[1024,128]{1,0:T(8,128)(2,1)S(1)}, u32[]{:S(2)}, u32[]{:S(2)}) collective-permute-start(bf16[1024,128]{1,0:T(8,128)(2,1)} %get-tuple-element.58.s_ref), channel_id=1, source_target_pairs={{0,4},{2,6},{4,0},{6,2},{8,12},{10,14},{12,8},{14,10},{1,5},{3,7},... | collective-permute-start | bytes 786440 | tf_op jit(solution)/shard_map/ppermute | solution.py:362
  12.0 0.7 %collective-permute-start.4 = (bf16[256,1024]{1,0:T(8,128)(2,1)}, bf16[256,1024]{1,0:T(8,128)(2,1)S(1)}, u32[]{:S(2)}, u32[]{:S(2)}) collective-permute-start(bf16[256,1024]{1,0:T(8,128)(2,1)} %get-tuple-element.43), channel_id=1, source_target_pairs={{2,4},{6,8},{10,12},{4,2},{8,6},{12,10},{3,5},{7,9},{11,13},{5,3},... | collective-permute-start | bytes 1572872 | tf_op jit(solution)/shard_map/ppermute | solution.py:373
  12.7 0.0 copy-done.6
  12.8 6.0 %own_attention.1 = (f32[4,8,256]{2,1,0:T(8,128)S(1)}, f32[4,8,256]{2,1,0:T(8,128)S(1)}, f32[4,1024,128]{2,1,0:T(8,128)S(1)}, bf16[1024,128]{1,0:T(8,128)(2,1)S(1)}) custom-call(s32[4,4]{1,0:T(4,128)S(1)} %bitcast.5, s32[4]{0:T(128)S(1)} %bitcast.10, s32[1]{0:T(128)} %bitcast.2.pos_ref, bf16[512,1024]{1,0:T(8,128)(2,1)} %get-tuple-element.57.k_ref.refs_3_, ...), custom_call_target="tpu_custom_call" | custom-call | flops 1 | bytes 1000 | tf_op jit(solution)/shard_map/own_attention/pallas_call | solution.py:328
  18.8 1.2 %collective-permute-done.1.refs_0_ = bf16[1024,128]{1,0:T(8,128)(2,1)S(1)} collective-permute-done((bf16[1024,128]{1,0:T(8,128)(2,1)}, bf16[1024,128]{1,0:T(8,128)(2,1)S(1)}, u32[]{:S(2)}, u32[]{:S(2)}) %collective-permute-start.1) | collective-permute-done | bytes 262176 | tf_op jit(solution)/shard_map/ppermute | solution.py:362
  19.9 0.1 add.3
  20.0 0.0 copy-start.1
  20.0 0.0 copy-start.2
  20.0 2.7 %collective-permute-start.5 = (bf16[1024,128]{1,0:T(8,128)(2,1)S(1)}, bf16[1024,128]{1,0:T(8,128)(2,1)S(1)}, u32[]{:S(2)}, u32[]{:S(2)}) collective-permute-start(bf16[1024,128]{1,0:T(8,128)(2,1)S(1)} %add.3), channel_id=1, source_target_pairs={{0,8},{2,10},{4,12},{6,14},{8,0},{10,2},{12,4},{14,6},{1,9},{3,11}... | collective-permute-start | bytes 786440 | tf_op jit(solution)/shard_map/ppermute | solution.py:362
  22.8 0.0 collective-permute-done.refs_0_
  22.8 6.1 %collective-permute-start.2 = (bf16[256,1024]{1,0:T(8,128)(2,1)}, bf16[256,1024]{1,0:T(8,128)(2,1)S(1)}, u32[]{:S(2)}, u32[]{:S(2)}) collective-permute-start(bf16[256,1024]{1,0:T(8,128)(2,1)} %collective-permute-done.refs_0_), channel_id=1, source_target_pairs={{0,4},{4,8},{8,12},{6,2},{10,6},{14,10},{1,5},{5,9},{9,13},{7,3},{... | collective-permute-start | bytes 1572872 | tf_op jit(solution)/shard_map/ppermute | solution.py:369
  28.9 2.0 %within.1.n_ref = f32[1024,512]{1,0:T(8,128)S(1)} custom-call(bf16[512,1024]{1,0:T(8,128)(2,1)S(1)} %copy-done, bf16[1024,512]{1,0:T(8,128)(2,1)S(1)} %copy-done.3), custom_call_target="tpu_custom_call" | custom-call | flops 1 | bytes 1000 | tf_op jit(solution)/shard_map/within/pallas_call | solution.py:328
  31.0 0.1 collective-permute-start.3
  31.1 3.5 %halo_a.1 = (f32[4,8,256]{2,1,0:T(8,128)S(1)}, f32[4,8,256]{2,1,0:T(8,128)S(1)}, f32[4,1024,128]{2,1,0:T(8,128)S(1)}) custom-call(s32[4,4]{1,0:T(4,128)S(1)} %bitcast.6, s32[4]{0:T(128)S(1)} %bitcast.11, s32[1]{0:T(128)} %bitcast.2.pos_ref, ...), custom_call_target="tpu_custom_call", output_to_operand_aliasing={{0}: (7, {}), {1}: (8, {}), {2}: (9, {})} | custom-call | flops 99999997952 | bytes 1000 | tf_op jit(solution)/shard_map/halo_a/pallas_call | solution.py:328
  34.5 4.8 %collective-permute-done.5.refs_1_ = bf16[1024,128]{1,0:T(8,128)(2,1)S(1)} collective-permute-done((bf16[1024,128]{1,0:T(8,128)(2,1)S(1)}, bf16[1024,128]{1,0:T(8,128)(2,1)S(1)}, u32[]{:S(2)}, u32[]{:S(2)}) %collective-permute-start.5) | collective-permute-done | bytes 262176 | tf_op jit(solution)/shard_map/ppermute | solution.py:362
  39.4 0.2 carry.1
  39.6 0.1 collective-permute-start.6
  39.6 0.0 collective-permute-done.4.refs_0_
  39.6 2.1 %halo_b.1 = (f32[4,8,256]{2,1,0:T(8,128)S(1)}, f32[4,8,256]{2,1,0:T(8,128)S(1)}, f32[4,1024,128]{2,1,0:T(8,128)S(1)}) custom-call(s32[4,4]{1,0:T(4,128)S(1)} %bitcast.7, s32[4]{0:T(128)S(1)} %bitcast.12, s32[1]{0:T(128)} %bitcast.2.pos_ref, ...), custom_call_target="tpu_custom_call", output_to_operand_aliasing={{0}: (7, {}), {1}: (8, {}), {2}: (9, {})} | custom-call | flops 1 | bytes 1000 | tf_op jit(solution)/shard_map/halo_b/pallas_call | solution.py:328
  41.7 1.6 %collective-permute-done.3.refs_0_ = bf16[256,1024]{1,0:T(8,128)(2,1)S(1)} collective-permute-done((bf16[256,1024]{1,0:T(8,128)(2,1)S(1)}, bf16[256,1024]{1,0:T(8,128)(2,1)S(1)}, u32[]{:S(2)}, u32[]{:S(2)}) %collective-permute-start.3) | collective-permute-done | bytes 524320 | tf_op jit(solution)/shard_map/ppermute | solution.py:362
  43.3 2.1 %halo_c.1 = (f32[4,8,256]{2,1,0:T(8,128)S(1)}, f32[4,8,256]{2,1,0:T(8,128)S(1)}, f32[4,1024,128]{2,1,0:T(8,128)S(1)}) custom-call(s32[4,4]{1,0:T(4,128)S(1)} %bitcast.8, s32[4]{0:T(128)S(1)} %bitcast.13, s32[1]{0:T(128)} %bitcast.2.pos_ref, ...), custom_call_target="tpu_custom_call", output_to_operand_aliasing={{0}: (7, {}), {1}: (8, {}), {2}: (9, {})} | custom-call | flops 1 | bytes 1000 | tf_op jit(solution)/shard_map/halo_c/pallas_call | solution.py:328
  45.4 0.0 copy-start.4
  45.4 1.2 %collective-permute-done.6.refs_2_ = bf16[1024,128]{1,0:T(8,128)(2,1)S(1)} collective-permute-done((bf16[1024,128]{1,0:T(8,128)(2,1)S(1)}, bf16[1024,128]{1,0:T(8,128)(2,1)S(1)}, u32[]{:S(2)}, u32[]{:S(2)}) %collective-permute-start.6) | collective-permute-done | bytes 262176 | tf_op jit(solution)/shard_map/ppermute | solution.py:362
  46.7 1.3 %linear.1.refs_4_ = f32[1024,512]{1,0:T(8,128)S(1)} custom-call(s32[1]{0:T(128)} %bitcast.2.pos_ref, bf16[512,1024]{1,0:T(8,128)(2,1)S(1)} %copy-done, f32[1024,512]{1,0:T(8,128)S(1)} %within.1.n_ref, bf16[1024,128]{1,0:T(8,128)(2,1)S(1)} %collective-permute-done.1.refs_0_, bf16[1024,128]{1,0:T(8,128)(2,1)S(1)} %collective-permute-done.5.refs_1_, ...), custom_call_target="tpu_custom_call" | custom-call | flops 1 | bytes 1000 | tf_op jit(solution)/shard_map/linear/pallas_call | solution.py:328
  47.9 0.0 collective-permute-done.2.refs_0_
  48.0 4.4 %final.1 = (bf16[512,1024]{1,0:T(8,128)(2,1)}, f32[4,8,256]{2,1,0:T(8,128)S(1)}, f32[4,8,256]{2,1,0:T(8,128)S(1)}, f32[4,1024,128]{2,1,0:T(8,128)S(1)}) custom-call(s32[4,4]{1,0:T(4,128)S(1)} %bitcast.9, s32[4]{0:T(128)S(1)} %bitcast.14, s32[1]{0:T(128)} %bitcast.2.pos_ref, ...), custom_call_target="tpu_custom_call", output_to_operand_aliasing={{1}: (9, {}), {2}: (10, {}), {3}: (11, {})} | custom-call | flops 1 | bytes 1000 | tf_op jit(solution)/shard_map/final/pallas_call | solution.py:328
  (11 shorter events, 0.0 us)
Async XLA Ops:
  1.1 11.7 %copy-start.6 = (s32[1,4,4]{2,1,0:T(4,128)S(1)}, s32[1,4,4]{2,1,0:T(4,128)}, u32[]{:S(2)}) copy-start(s32[1,4,4]{2,1,0:T(4,128)} %param.10) | copy-start | bytes 196
  1.1 11.7 %copy-start.7 = (s32[1,4]{1,0:T(1,128)S(1)}, s32[1,4]{1,0:T(1,128)}, u32[]{:S(2)}) copy-start(s32[1,4]{1,0:T(1,128)} %param.11) | copy-start | bytes 52
  1.1 21.7 %collective-permute-start = (bf16[256,1024]{1,0:T(8,128)(2,1)S(1)}, bf16[256,1024]{1,0:T(8,128)(2,1)}, u32[]{:S(2)}, u32[]{:S(2)}) collective-permute-start(bf16[256,1024]{1,0:T(8,128)(2,1)S(1)} %cut.1), channel_id=1, source_target_pairs={{0,2},{2,0},{4,6},{6,4},{8,10},{10,8},{12,14},{14,12},{1,3},{3,1},... | collective-permute-start | bytes 1572872 | tf_op jit(solution)/shard_map/ppermute | solution.py:362
  10.4 18.5 %copy-start = (bf16[512,1024]{1,0:T(8,128)(2,1)S(1)}, bf16[512,1024]{1,0:T(8,128)(2,1)}, u32[]{:S(2)}) copy-start(bf16[512,1024]{1,0:T(8,128)(2,1)} %get-tuple-element.57.k_ref.refs_3_) | copy-start | bytes 3145732
  10.4 18.5 %copy-start.3 = (bf16[1024,512]{1,0:T(8,128)(2,1)S(1)}, bf16[1024,512]{1,0:T(8,128)(2,1)}, u32[]{:S(2)}) copy-start(bf16[1024,512]{1,0:T(8,128)(2,1)} %get-tuple-element.36.vt_ref) | copy-start | bytes 3145732
  10.4 9.5 %collective-permute-start.1 = (bf16[1024,128]{1,0:T(8,128)(2,1)}, bf16[1024,128]{1,0:T(8,128)(2,1)S(1)}, u32[]{:S(2)}, u32[]{:S(2)}) collective-permute-start(bf16[1024,128]{1,0:T(8,128)(2,1)} %get-tuple-element.58.s_ref), channel_id=1, source_target_pairs={{0,4},{2,6},{4,0},{6,2},{8,12},{10,14},{12,8},{14,10},{1,5},{3,7},... | collective-permute-start | bytes 786440 | tf_op jit(solution)/shard_map/ppermute | solution.py:362
  12.0 27.6 %collective-permute-start.4 = (bf16[256,1024]{1,0:T(8,128)(2,1)}, bf16[256,1024]{1,0:T(8,128)(2,1)S(1)}, u32[]{:S(2)}, u32[]{:S(2)}) collective-permute-start(bf16[256,1024]{1,0:T(8,128)(2,1)} %get-tuple-element.43), channel_id=1, source_target_pairs={{2,4},{6,8},{10,12},{4,2},{8,6},{12,10},{3,5},{7,9},{11,13},{5,3},... | collective-permute-start | bytes 1572872 | tf_op jit(solution)/shard_map/ppermute | solution.py:373
  19.9 11.0 %copy-start.8 = (bf16[256,1024]{1,0:T(8,128)(2,1)S(1)}, bf16[256,1024]{1,0:T(8,128)(2,1)}, u32[]{:S(2)}) copy-start(bf16[256,1024]{1,0:T(8,128)(2,1)} %get-tuple-element.43) | copy-start | bytes 1572868
  20.0 11.0 %copy-start.1 = (bf16[1024,1024]{1,0:T(8,128)(2,1)S(1)}, bf16[1024,1024]{1,0:T(8,128)(2,1)}, u32[]{:S(2)}) copy-start(bf16[1024,1024]{1,0:T(8,128)(2,1)} %refs_1_.7) | copy-start | bytes 6291460
  20.0 11.0 %copy-start.2 = (bf16[1024,1024]{1,0:T(8,128)(2,1)S(1)}, bf16[1024,1024]{1,0:T(8,128)(2,1)}, u32[]{:S(2)}) copy-start(bf16[1024,1024]{1,0:T(8,128)(2,1)} %refs_2_.7) | copy-start | bytes 6291460
  20.0 19.3 %collective-permute-start.5 = (bf16[1024,128]{1,0:T(8,128)(2,1)S(1)}, bf16[1024,128]{1,0:T(8,128)(2,1)S(1)}, u32[]{:S(2)}, u32[]{:S(2)}) collective-permute-start(bf16[1024,128]{1,0:T(8,128)(2,1)S(1)} %add.3), channel_id=1, source_target_pairs={{0,8},{2,10},{4,12},{6,14},{8,0},{10,2},{12,4},{14,6},{1,9},{3,11}... | collective-permute-start | bytes 786440 | tf_op jit(solution)/shard_map/ppermute | solution.py:362
  22.8 25.2 %collective-permute-start.2 = (bf16[256,1024]{1,0:T(8,128)(2,1)}, bf16[256,1024]{1,0:T(8,128)(2,1)S(1)}, u32[]{:S(2)}, u32[]{:S(2)}) collective-permute-start(bf16[256,1024]{1,0:T(8,128)(2,1)} %collective-permute-done.refs_0_), channel_id=1, source_target_pairs={{0,4},{4,8},{8,12},{6,2},{10,6},{14,10},{1,5},{5,9},{9,13},{7,3},{... | collective-permute-start | bytes 1572872 | tf_op jit(solution)/shard_map/ppermute | solution.py:369
  31.0 12.4 %collective-permute-start.3 = (bf16[256,1024]{1,0:T(8,128)(2,1)S(1)}, bf16[256,1024]{1,0:T(8,128)(2,1)S(1)}, u32[]{:S(2)}, u32[]{:S(2)}) collective-permute-start(bf16[256,1024]{1,0:T(8,128)(2,1)S(1)} %copy-done.8), channel_id=1, source_target_pairs={{0,2},{2,0},{4,6},{6,4},{8,10},{10,8},{12,14},{14,12},{1,3},{3,1},... | collective-permute-start | bytes 1572872 | tf_op jit(solution)/shard_map/ppermute | solution.py:362
  31.1 8.3 %copy-start.5 = (bf16[1024,128]{1,0:T(8,128)(2,1)S(1)}, bf16[1024,128]{1,0:T(8,128)(2,1)}, u32[]{:S(2)}) copy-start(bf16[1024,128]{1,0:T(8,128)(2,1)} %get-tuple-element.58.s_ref) | copy-start | bytes 786436
  39.6 7.1 %collective-permute-start.6 = (bf16[1024,128]{1,0:T(8,128)(2,1)S(1)}, bf16[1024,128]{1,0:T(8,128)(2,1)S(1)}, u32[]{:S(2)}, u32[]{:S(2)}) collective-permute-start(bf16[1024,128]{1,0:T(8,128)(2,1)S(1)} %carry.1), channel_id=1, source_target_pairs={{0,2},{2,0},{4,6},{6,4},{8,10},{10,8},{12,14},{14,12},{1,3},{3,1},... | collective-permute-start | bytes 786440 | tf_op jit(solution)/shard_map/ppermute | solution.py:362
  45.4 2.5 %copy-start.4 = (bf16[1024,1024]{1,0:T(8,128)(2,1)S(1)}, bf16[1024,1024]{1,0:T(8,128)(2,1)}, u32[]{:S(2)}) copy-start(bf16[1024,1024]{1,0:T(8,128)(2,1)} %refs_5_.1) | copy-start | bytes 6291460
